TPU v7x, 512 devices: a whole 4x4x16 slice. The times are simulated.
512 devices in a mesh: spk: 16 (over y_lo, x, core), pts: 32 (over y_hi, z).
Axes of the slice: x: 4, y: 4 (y_hi: 2, y_lo: 2; y = y_hi * 2 + y_lo), z: 16, core: 2. Of those that a mesh axis runs over, the one named last changes fastest.
Arguments:
- desired: float32 [2, 8, 8192], P(None, None, 'pts'), may hold values from -6 to 6
- spk_cells: int32 [4096], replicated, may hold values from 0 to 4095, each once
- pt_cells: float32 [3, 8192], P(None, 'pts'), may hold values from 0 to 1
- eval_cells: float32 [3, 65536], P(None, ('spk', 'pts')), may hold values from 0 to 1
- wavenumber: float32 [1], replicated, may hold values from 15 to 25
Outputs:
- drives: float32 [2, 8, 4096], P(None, None, 'spk')
- residual: float32 [2, 8, 8192], P(None, None, 'pts')
- field: float32 [2, 8, 65536], P(None, None, ('spk', 'pts'))
Inputs may be any that keep to these rules, and one draw needn't show every extreme that they name: `spk_cells`: each cell of the 64 x 64 wall holds exactly one loudspeaker.
All inputs are finite; a program needn't handle non-finite values.
Results may differ from a plain program's by a relative error of at most 0.0003.
Values sent between devices are 32-bit elements; how exact they have to be, the bound alone decides.
No kernel may reach another device: no remote copies, remote signals or barrier semaphores. Data moves between devices by JAX's collectives and lax.ppermute only.
A program may use at most 64 MiB of HBM per device.

v0:
```python
import functools
import math

import jax
import jax.numpy as jnp
from jax import lax
from jax.experimental import pallas as pl
from jax.experimental.pallas import tpu as pltpu
from jax.sharding import Mesh
from jax.sharding import PartitionSpec as P

WALL = 64
SPK = ("ylo", "x", "core")
PTS = ("yhi", "za", "zb", "zc")
FLD = ("za", "zb")
NEAR = ("yhi", "zc")

wall_pitch = 0.05
front_gap = 0.5
depth_span = 3.15
side_span = 3.2
tikhonov = 0.1

SIN = (4.442883014678955, -7.308245658874512, 3.606354236602783, -0.8461116552352905, 0.1098245158791542)
COS = (-1.4142135381698608, 6.978850841522217, -5.739460468292236, 1.883557915687561, -0.3106880187988281)
ROUNDER = 12582912.0

f32 = jnp.float32
bf16 = jnp.bfloat16


def spec(space=pltpu.VMEM):
    return pl.BlockSpec(memory_space=space)


def call(kernel, out_shapes, scratch, limit_mib, n_smem, n_in, name, flops, trans=0):
    return pl.pallas_call(
        kernel,
        out_shape=out_shapes,
        in_specs=[spec(pltpu.SMEM)] * n_smem + [spec()] * (n_in - n_smem),
        out_specs=jax.tree.map(lambda _: spec(), out_shapes),
        scratch_shapes=scratch,
        compiler_params=pltpu.CompilerParams(vmem_limit_bytes=limit_mib << 20),
        cost_estimate=pl.CostEstimate(flops=flops, bytes_accessed=1 << 20, transcendentals=trans),
        name=name,
    )


def poly(coeffs, u):
    out = coeffs[-1]
    for c in coeffs[-2::-1]:
        out = out * u + c
    return out


def green(scaled, strength):
    inverse = lax.rsqrt(scaled)
    turns = scaled * inverse
    magnitude = inverse * strength
    whole = (turns + ROUNDER) - ROUNDER
    frac = turns - whole
    u = frac * frac
    s = poly(SIN, u) * frac
    c = poly(COS, u)
    ms = magnitude * s
    return magnitude - ms * s, ms * c


def wall_rows(cells, kappa):
    centre = (WALL - 1) * 0.5
    row = jnp.right_shift(cells, 6).astype(f32)
    col = jnp.bitwise_and(cells, WALL - 1).astype(f32)
    return (row - centre) * (wall_pitch * kappa), (col - centre) * (wall_pitch * kappa)


def column(row):
    return jnp.broadcast_to(row, (128, 128)).T


def total(x):
    return jnp.broadcast_to(jnp.sum(x, keepdims=True), (1, 128))


def add_up(ref):
    out = ref[0]
    for i in range(1, ref.shape[0]):
        out = out + ref[i]
    return out


def split_bf16(x):
    high = x.astype(bf16)
    return high, (x - high.astype(f32)).astype(bf16)


def eval_green_kernel(wave_ref, cells_ref, eval_ref, high_ref, low_ref):
    kappa = wave_ref[0] * (0.5 / math.pi)
    strength = kappa * (1.0 / WALL)
    ex = column((front_gap + eval_ref[0:1, :] * depth_span) * kappa)
    ey = column((eval_ref[1:2, :] * side_span - 0.5 * side_span) * kappa)
    ez = column((eval_ref[2:3, :] * side_span - 0.5 * side_span) * kappa)
    ex2 = ex * ex

    def step(i, carry):
        wy, wz = wall_rows(cells_ref[pl.ds(i, 1), :], kappa)
        lanes = pl.ds(pl.multiple_of(i * 128, 128), 128)
        for part in range(2):
            rows = slice(part * 64, part * 64 + 64)
            dy = ey[rows] - wy
            dz = ez[rows] - wz
            real, imag = green(ex2[rows] + dy * dy + dz * dz, strength)
            rh, rl = split_bf16(real)
            ih, il = split_bf16(imag)
            high_ref[part * 64 : part * 64 + 64, lanes] = rh
            low_ref[part * 64 : part * 64 + 64, lanes] = rl
            high_ref[128 + part * 64 : 128 + part * 64 + 64, lanes] = ih
            low_ref[128 + part * 64 : 128 + part * 64 + 64, lanes] = il
        return carry

    lax.fori_loop(0, cells_ref.shape[0], step, 0)


def first_kernel(own_ref, wave_ref, cells_ref, got_ref, g_ref, send_ref, wall_ref, acc_ref):
    kappa = wave_ref[0] * (0.5 / math.pi)
    strength = kappa * (1.0 / WALL)
    for blk in range(2):
        wy, wz = wall_rows(cells_ref[pl.ds(own_ref[0] * 2 + blk, 1), :], kappa)
        wall_ref[0, blk * 128 : blk * 128 + 128, :] = column(wy)
        wall_ref[1, blk * 128 : blk * 128 + 128, :] = column(wz)
    size = 32

    def chunk(k, carry):
        rows = pl.ds(pl.multiple_of(k * size, size), size)
        wy = wall_ref[0, rows, :]
        wz = wall_ref[1, rows, :]

        def source(j, sums):
            real_sum, imag_sum = sums
            for half in range(2):
                lanes = slice(half * 128, half * 128 + 128)
                px = (front_gap + got_ref[j, 2:3, lanes] * depth_span) * kappa
                py = (got_ref[j, 3:4, lanes] * side_span - 0.5 * side_span) * kappa
                pz = (got_ref[j, 4:5, lanes] * side_span - 0.5 * side_span) * kappa
                vr = got_ref[j, 0:1, lanes]
                vi = got_ref[j, 1:2, lanes]
                dy = py - wy
                dz = pz - wz
                real, imag = green(px * px + dy * dy + dz * dz, strength)
                g_ref[j * 2 + half, 0, rows, :] = real
                g_ref[j * 2 + half, 1, rows, :] = imag
                real_sum = real_sum + (real * vr + imag * vi)
                imag_sum = imag_sum + (real * vi - imag * vr)
            return real_sum, imag_sum

        zero = jnp.zeros((size, 128), f32)
        real_sum, imag_sum = lax.fori_loop(0, got_ref.shape[0], source, (zero, zero))
        acc_ref[0, rows, :] = real_sum
        acc_ref[1, rows, :] = imag_sum
        return carry

    lax.fori_loop(0, 256 // size, chunk, 0)
    rows = rows_of(acc_ref)
    for i in range(send_ref.shape[0]):
        send_ref[i, 0:4, :] = rows


def rows_of(acc_ref):
    rows = []
    for part in range(2):
        for blk in range(2):
            block = acc_ref[part, blk * 128 : blk * 128 + 128, :]
            rows.append(jnp.sum(block.T, axis=0, keepdims=True))
    return jnp.concatenate(rows, axis=0)


def forward(g_ref, rows, col_ref, out_ref):
    for part in range(2):
        for blk in range(2):
            i = part * 2 + blk
            col_ref[part, blk * 128 : blk * 128 + 128, :] = column(rows[i : i + 1, :])
    size = 64

    def step(t, carry):
        real_sum = jnp.zeros((8, 128), f32)
        imag_sum = jnp.zeros((8, 128), f32)
        for k in range(256 // size):
            rows = slice(k * size, k * size + size)
            gr = g_ref[t, 0, rows, :]
            gi = g_ref[t, 1, rows, :]
            qr = col_ref[0, rows, :]
            qi = col_ref[1, rows, :]
            real_sum = real_sum + (gr * qr - gi * qi).reshape(size // 8, 8, 128).sum(axis=0)
            imag_sum = imag_sum + (gi * qr + gr * qi).reshape(size // 8, 8, 128).sum(axis=0)
        out_ref[pl.ds(t, 1), :] = jnp.sum(real_sum, axis=0, keepdims=True)
        out_ref[pl.ds(t + 16, 1), :] = jnp.sum(imag_sum, axis=0, keepdims=True)
        return carry

    lax.fori_loop(0, 16, step, 0)


def adjoint(g_ref, im_ref, acc_ref):
    size = 64

    def chunk(k, carry):
        rows = pl.ds(pl.multiple_of(k * size, size), size)
        real_sum = jnp.zeros((size, 128), f32)
        imag_sum = jnp.zeros((size, 128), f32)
        for t in range(16):
            vr = im_ref[t : t + 1, :]
            vi = im_ref[16 + t : 17 + t, :]
            gr = g_ref[t, 0, rows, :]
            gi = g_ref[t, 1, rows, :]
            real_sum = real_sum + (gr * vr + gi * vi)
            imag_sum = imag_sum + (gr * vi - gi * vr)
        acc_ref[0, rows, :] = real_sum
        acc_ref[1, rows, :] = imag_sum
        return carry

    lax.fori_loop(0, 256 // size, chunk, 0)
    return rows_of(acc_ref)


def image_kernel(g_ref, got_ref, send_ref, own_ref, col_ref, im_ref):
    g0 = add_up(got_ref)
    own_ref[...] = g0
    forward(g_ref, g0, col_ref, im_ref)
    message = jnp.concatenate([im_ref[...], g0, total(g0 * g0), jnp.zeros((3, 128), f32)], axis=0)
    for i in range(send_ref.shape[0]):
        send_ref[i] = message


def adjoint_kernel(g_ref, got_ref, send_ref, im_ref, acc_ref):
    whole = add_up(got_ref)
    im_ref[...] = whole
    rows = adjoint(g_ref, im_ref, acc_ref)
    im = whole[0:32, :]
    message = jnp.concatenate([rows, total(im * im), jnp.zeros((3, 128), f32)], axis=0)
    for i in range(send_ref.shape[0]):
        send_ref[i] = message


def second_image_kernel(g_ref, got_ref, g0_ref, im0_ref, send_ref, alpha_ref, col_ref, im_ref):
    whole = add_up(got_ref)
    g0 = g0_ref[...]
    gamma = im0_ref[36:37, :]
    alpha = gamma / (whole[4:5, :] + tikhonov * gamma)
    alpha_ref[...] = alpha
    g1 = g0 - alpha * (whole[0:4, :] + tikhonov * g0)
    forward(g_ref, g1, col_ref, im_ref)
    message = jnp.concatenate([im_ref[...], g1, total(g1 * g1), total(g1 * g0), jnp.zeros((2, 128), f32)], axis=0)
    for i in range(send_ref.shape[0]):
        send_ref[i] = message


def norm_kernel(got_ref, im0_ref, send_ref, im1_ref):
    whole = add_up(got_ref)
    gamma0 = im0_ref[36:37, :]
    gamma1 = whole[36:37, :]
    cross = whole[37:38, :]
    beta = gamma1 / gamma0
    im1 = whole[0:32, :] + beta * im0_ref[0:32, :]
    im1_ref[0:32, :] = im1
    im1_ref[32:33, :] = beta
    im1_ref[33:34, :] = gamma1
    im1_ref[34:35, :] = gamma1 + (2.0 * cross + beta * gamma0) * beta
    square = total(im1 * im1)
    for i in range(send_ref.shape[0]):
        send_ref[i] = square


def drive_kernel(got_ref, alpha_ref, im0_ref, im1_ref, first_ref, second_ref, send_ref):
    alpha0 = alpha_ref[...]
    beta = im1_ref[32:33, :]
    alpha1 = im1_ref[33:34, :] / (add_up(got_ref) + tikhonov * im1_ref[34:35, :])
    change = alpha0 * im0_ref[0:32, :] + alpha1 * im1_ref[0:32, :]
    from_first = alpha0 + alpha1 * beta
    for s in range(16):
        rows = from_first * first_ref[s, 32:36, :] + alpha1 * second_ref[s, 32:36, :]
        for i in range(send_ref.shape[0]):
            send_ref[i, 4 * s : 4 * s + 4, :] = rows
    for i in range(send_ref.shape[0]):
        send_ref[i, 64:66, :] = change[2 * i : 2 * i + 2, :]
        send_ref[i, 66:68, :] = change[16 + 2 * i : 18 + 2 * i, :]


def field_kernel(own_ref, got_ref, high_ref, low_ref, desired_ref, drives_ref, residual_ref, field_ref):
    own = own_ref[0]
    for part in range(2):
        for blk in range(2):
            lanes = slice(blk * 128, blk * 128 + 128)
            drives_ref[part, :, lanes] = got_ref[:, own * 4 + part * 2 + blk, :]
            residual_ref[part, :, lanes] = desired_ref[part, :, lanes] - got_ref[:, 64 + part * 2 + blk, :]
    out = jnp.zeros((32, 256), f32)
    fine = jnp.zeros((16, 256), f32)
    for s in range(16):
        lanes = slice(s * 256, s * 256 + 256)
        parts = [
            jnp.concatenate([got_ref[:, 4 * s + 2 * part + blk, :] for blk in range(2)], axis=1)
            for part in range(2)
        ]
        high, low = split_bf16(jnp.concatenate(parts, axis=0))
        both = jnp.concatenate([high, low], axis=0)
        dims = (((1,), (1,)), ((), ()))
        out = out + lax.dot_general(both, high_ref[:, lanes], dims, preferred_element_type=f32)
        fine = fine + lax.dot_general(high, low_ref[:, lanes], dims, preferred_element_type=f32)
    out = out[0:16, :] + out[16:32, :] + fine
    field_ref[0] = out[0:8, 0:128] - out[8:16, 128:256]
    field_ref[1] = out[0:8, 128:256] + out[8:16, 0:128]


def exchange(array, axes):
    return lax.all_to_all(array, axes, split_axis=0, concat_axis=0, tiled=True)


def shape(*dims, dtype=f32):
    return jax.ShapeDtypeStruct(dims, dtype)


def local(desired, spk_cells, pt_cells, eval_cells, wavenumber):
    cells = spk_cells.reshape(32, 128)
    own = lax.axis_index(SPK).astype(jnp.int32).reshape(1)
    vmem = pltpu.VMEM

    outgoing = jnp.concatenate(
        [desired.transpose(1, 0, 2), jnp.broadcast_to(pt_cells, (8, 3, 256))], axis=1
    )
    got0 = exchange(outgoing, FLD)
    high, low = call(
        eval_green_kernel,
        (shape(256, 4096, dtype=bf16), shape(256, 4096, dtype=bf16)),
        [], 12, 1, 3, "eval_green", 524288 * 40, 524288,
    )(wavenumber, cells, eval_cells)
    g, send1 = call(
        first_kernel,
        (shape(16, 2, 256, 128), shape(4, 4, 128)),
        [vmem((2, 256, 128), f32), vmem((2, 256, 128), f32)], 12, 2, 4, "first", 524288 * 48, 524288,
    )(own, wavenumber, cells, got0)
    got1 = exchange(send1, NEAR)
    send2, g0 = call(
        image_kernel,
        (shape(16, 40, 128), shape(4, 128)),
        [vmem((2, 256, 128), f32), vmem((32, 128), f32)], 12, 0, 2, "image", 524288 * 8,
    )(g, got1)
    got2 = exchange(send2, SPK)
    send3, im0 = call(
        adjoint_kernel,
        (shape(4, 8, 128), shape(40, 128)),
        [vmem((2, 256, 128), f32)], 12, 0, 2, "adjoint", 524288 * 8,
    )(g, got2)
    got3 = exchange(send3, NEAR)
    send4, alpha = call(
        second_image_kernel,
        (shape(16, 40, 128), shape(1, 128)),
        [vmem((2, 256, 128), f32), vmem((32, 128), f32)], 12, 0, 4, "second_image", 524288 * 8,
    )(g, got3, g0, im0)
    got4 = exchange(send4, SPK)
    send5, im1 = call(
        norm_kernel,
        (shape(4, 1, 128), shape(40, 128)),
        [], 8, 0, 2, "norm", 81920,
    )(got4, im0)
    got5 = exchange(send5, NEAR)
    send6 = call(
        drive_kernel,
        shape(8, 72, 128),
        [], 8, 0, 6, "drive", 81920,
    )(got5, alpha, im0, im1, got2, got4)
    got6 = exchange(send6, FLD)
    return call(
        field_kernel,
        (shape(2, 8, 256), shape(2, 8, 256), shape(2, 8, 128)),
        [], 12, 1, 5, "field", 524288 * 96,
    )(own, got6, high, low, desired)


def solution(mesh):
    split = Mesh(
        mesh.devices.reshape(2, 4, 2, 2, 4, 2, 2), ("ylo", "x", "core", "yhi", "za", "zb", "zc")
    )
    in_specs = (P(None, None, PTS), P(), P(None, PTS), P(None, SPK + PTS), P())
    out_specs = (P(None, None, SPK), P(None, None, PTS), P(None, None, SPK + PTS))
    return jax.shard_map(local, mesh=split, in_specs=in_specs, out_specs=out_specs, check_vma=False)
```

profile of v0, /device:TPU:8, one launch (start us, length us, event | category | flops | bytes accessed | tf_op | source)
XLA Modules:
  0.0 120.2 jit_solution(13403884287393736349)
XLA Ops:
  0.6 0.7 copy.10
  1.4 0.7 broadcast_in_dim.3
  2.1 0.6 pad_maximum_fusion
  2.7 15.1 %all-to-all-start = ((f32[8,5,256]{2,1,0:T(8,128)}), f32[8,5,256]{2,1,0:T(8,128)S(1)}, u32[]{:S(2)}, u32[]{:S(2)}) async-start(f32[8,5,256]{2,1,0:T(8,128)} %pad_maximum_fusion), calls=%async_computation | async-start | bytes 131072 | tf_op jit(solution)/shard_map/all_to_all | solution.py:312
  18.4 13.0 %all-to-all-done.got_ref = f32[8,5,256]{2,1,0:T(8,128)S(1)} async-done(((f32[8,5,256]{2,1,0:T(8,128)}), f32[8,5,256]{2,1,0:T(8,128)S(1)}, u32[]{:S(2)}, u32[]{:S(2)}) %all-to-all-start) | async-done | bytes 40992 | tf_op jit(solution)/shard_map/all_to_all | solution.py:312
  31.4 0.7 copy-done.3
  32.1 4.1 %first.1 = (f32[16,2,256,128]{3,2,1,0:T(8,128)S(1)}, f32[4,4,128]{2,1,0:T(4,128)S(1)}) custom-call(s32[1]{0:T(128)} %bitcast.own_ref, f32[1]{0:T(128)S(6)} %copy.11.wave_ref, s32[32,128]{1,0:T(8,128)S(1)} %bitcast.5, f32[8,5,256]{2,1,0:T(8,128)S(1)} %all-to-all-done.got_ref), custom_call_target="tpu_custom_call" | custom-call | flops 25165824 | bytes 1048576 | tf_op jit(solution)/shard_map/first/pallas_call | solution.py:333
  36.2 10.0 %all_to_all.35.got_ref = f32[4,4,128]{2,1,0:T(4,128)S(1)} all-to-all(f32[4,4,128]{2,1,0:T(4,128)S(1)} %get-tuple-element.16), channel_id=1, replica_groups=mesh['ylo'=2,'x'=4,'core'=2,'yhi'=2,'za'=4,'zb'=2,'zc'=2] {'yhi','zc'}, dimensions={0} | all-to-all | bytes 16384 | tf_op jit(solution)/shard_map/all_to_all | solution.py:312
  46.2 1.2 %image.1 = (f32[16,40,128]{2,1,0:T(8,128)S(1)}, f32[4,128]{1,0:T(4,128)S(1)}) custom-call(f32[16,2,256,128]{3,2,1,0:T(8,128)S(1)} %get-tuple-element.15.g_ref, f32[4,4,128]{2,1,0:T(4,128)S(1)} %all_to_all.35.got_ref), custom_call_target="tpu_custom_call" | custom-call | flops 4194304 | bytes 1048576 | tf_op jit(solution)/shard_map/image/pallas_call | solution.py:339
  47.4 12.7 %all_to_all.36.got_ref.first_ref = f32[16,40,128]{2,1,0:T(8,128)S(1)} all-to-all(f32[16,40,128]{2,1,0:T(8,128)S(1)} %get-tuple-element.17), channel_id=1, replica_groups=mesh['ylo'=2,'x'=4,'core'=2,'yhi'=2,'za'=4,'zb'=2,'zc'=2] {'ylo','x','co..., dimensions={0} | all-to-all | bytes 655360 | tf_op jit(solution)/shard_map/all_to_all | solution.py:312
  60.1 1.0 adjoint.1
  61.2 8.6 %all_to_all.37.got_ref = f32[4,8,128]{2,1,0:T(8,128)S(1)} all-to-all(f32[4,8,128]{2,1,0:T(8,128)S(1)} %get-tuple-element.18), channel_id=1, replica_groups=mesh['ylo'=2,'x'=4,'core'=2,'yhi'=2,'za'=4,'zb'=2,'zc'=2] {'yhi','zc'}, dimensions={0} | all-to-all | bytes 32768 | tf_op jit(solution)/shard_map/all_to_all | solution.py:312
  69.7 1.3 %second_image.1 = (f32[16,40,128]{2,1,0:T(8,128)S(1)}, f32[1,128]{1,0:T(1,128)S(1)}) custom-call(f32[16,2,256,128]{3,2,1,0:T(8,128)S(1)} %get-tuple-element.15.g_ref, f32[4,8,128]{2,1,0:T(8,128)S(1)} %all_to_all.37.got_ref, f32[4,128]{1,0:T(4,128)S(1)} %get-tuple-element.19.g0_ref, f32[40,128]{1,0:T(8,128)S(1)} %get-tuple-element.20.im0_ref), custom_call_target="tpu_custom_call" | custom-call | flops 4194304 | bytes 1048576 | tf_op jit(solution)/shard_map/second_image/pallas_call | solution.py:351
  71.0 0.0 copy-start.5
  71.0 11.2 %all_to_all.38.got_ref.second_ref = f32[16,40,128]{2,1,0:T(8,128)S(1)} all-to-all(f32[16,40,128]{2,1,0:T(8,128)S(1)} %get-tuple-element.21), channel_id=1, replica_groups=mesh['ylo'=2,'x'=4,'core'=2,'yhi'=2,'za'=4,'zb'=2,'zc'=2] {'ylo','x','co..., dimensions={0} | all-to-all | bytes 655360 | tf_op jit(solution)/shard_map/all_to_all | solution.py:312
  82.2 0.1 norm.1
  82.4 8.5 %all_to_all.39.got_ref = f32[4,1,128]{2,1,0:T(1,128)S(1)} all-to-all(f32[4,1,128]{2,1,0:T(1,128)S(1)} %get-tuple-element.22), channel_id=1, replica_groups=mesh['ylo'=2,'x'=4,'core'=2,'yhi'=2,'za'=4,'zb'=2,'zc'=2] {'yhi','zc'}, dimensions={0} | all-to-all | bytes 4096 | tf_op jit(solution)/shard_map/all_to_all | solution.py:312
  90.9 0.8 drive.1
  91.7 3.4 %all-to-all-start.6 = ((f32[8,72,128]{2,1,0:T(8,128)}), f32[8,72,128]{2,1,0:T(8,128)S(1)}, u32[]{:S(2)}, u32[]{:S(2)}) async-start(f32[8,72,128]{2,1,0:T(8,128)} %drive.1), calls=%async_computation.6 | async-start | bytes 589824 | tf_op jit(solution)/shard_map/all_to_all | solution.py:312
  95.1 3.4 %eval_green.1 = (bf16[256,4096]{1,0:T(8,128)(2,1)S(1)}, bf16[256,4096]{1,0:T(8,128)(2,1)S(1)}) custom-call(f32[1]{0:T(128)S(6)} %copy.11.wave_ref, s32[32,128]{1,0:T(8,128)S(1)} %bitcast.6, f32[3,128]{1,0:T(4,128)S(1)} %copy-done.5), custom_call_target="tpu_custom_call" | custom-call | flops 20971520 | bytes 1048576 | tf_op jit(solution)/shard_map/eval_green/pallas_call | solution.py:328
  98.5 1.3 %copy-done = bf16[256,4096]{1,0:T(8,128)(2,1)} copy-done((bf16[256,4096]{1,0:T(8,128)(2,1)}, bf16[256,4096]{1,0:T(8,128)(2,1)S(1)}, u32[]{:S(2)}) %copy-start) | copy-done | bytes 2097176
  99.9 16.9 %all-to-all-done.6.got_ref = f32[8,72,128]{2,1,0:T(8,128)S(1)} async-done(((f32[8,72,128]{2,1,0:T(8,128)}), f32[8,72,128]{2,1,0:T(8,128)S(1)}, u32[]{:S(2)}, u32[]{:S(2)}) %all-to-all-start.6) | async-done | bytes 294944 | tf_op jit(solution)/shard_map/all_to_all | solution.py:312
  116.8 1.6 %copy-done.1 = bf16[256,4096]{1,0:T(8,128)(2,1)S(1)} copy-done((bf16[256,4096]{1,0:T(8,128)(2,1)S(1)}, bf16[256,4096]{1,0:T(8,128)(2,1)}, u32[]{:S(2)}) %copy-start.1) | copy-done | bytes 2097176
  118.4 1.8 %field.1 = (f32[2,8,256]{2,1,0:T(8,128)}, f32[2,8,256]{2,1,0:T(8,128)}, f32[2,8,128]{2,1,0:T(8,128)}) custom-call(s32[1]{0:T(128)} %bitcast.own_ref, f32[8,72,128]{2,1,0:T(8,128)S(1)} %all-to-all-done.6.got_ref, bf16[256,4096]{1,0:T(8,128)(2,1)S(1)} %get-tuple-element.25.high_ref, bf16[256,4096]{1,0:T(8,128)(2,1)S(1)} %copy-done.1, f32[2,8,256]{2,1,0:T(8,128)S(1)} %copy-done.2), custom_call_target="tpu_custom_call" | custom-call | flops 50331648 | bytes 1048576 | tf_op jit(solution)/shard_map/field/pallas_call | solution.py:369
  (8 shorter events, 0.0 us)
Async XLA Ops:
  2.7 28.7 %all-to-all-start = ((f32[8,5,256]{2,1,0:T(8,128)}), f32[8,5,256]{2,1,0:T(8,128)S(1)}, u32[]{:S(2)}, u32[]{:S(2)}) async-start(f32[8,5,256]{2,1,0:T(8,128)} %pad_maximum_fusion), calls=%async_computation | async-start | bytes 131072 | tf_op jit(solution)/shard_map/all_to_all | solution.py:312
  31.4 0.7 copy-start.3
  71.0 24.1 %copy-start.4 = (s32[4096]{0:T(1024)S(1)}, s32[4096]{0:T(1024)}, u32[]{:S(2)}) copy-start(s32[4096]{0:T(1024)} %param.6) | copy-start | bytes 49156
  71.0 24.1 %copy-start.5 = (f32[3,128]{1,0:T(4,128)S(1)}, f32[3,128]{1,0:T(4,128)}, u32[]{:S(2)}) copy-start(f32[3,128]{1,0:T(4,128)} %eval_ref.1) | copy-start | bytes 4612
  71.0 45.8 %copy-start.2 = (f32[2,8,256]{2,1,0:T(8,128)S(1)}, f32[2,8,256]{2,1,0:T(8,128)}, u32[]{:S(2)}) copy-start(f32[2,8,256]{2,1,0:T(8,128)} %desired_ref.1) | copy-start | bytes 49156
  91.7 25.1 %all-to-all-start.6 = ((f32[8,72,128]{2,1,0:T(8,128)}), f32[8,72,128]{2,1,0:T(8,128)S(1)}, u32[]{:S(2)}, u32[]{:S(2)}) async-start(f32[8,72,128]{2,1,0:T(8,128)} %drive.1), calls=%async_computation.6 | async-start | bytes 589824 | tf_op jit(solution)/shard_map/all_to_all | solution.py:312
  98.5 1.3 %copy-start = (bf16[256,4096]{1,0:T(8,128)(2,1)}, bf16[256,4096]{1,0:T(8,128)(2,1)S(1)}, u32[]{:S(2)}) copy-start(bf16[256,4096]{1,0:T(8,128)(2,1)S(1)} %get-tuple-element.26.low_ref) | copy-start | bytes 6291460
  116.8 1.6 %copy-start.1 = (bf16[256,4096]{1,0:T(8,128)(2,1)S(1)}, bf16[256,4096]{1,0:T(8,128)(2,1)}, u32[]{:S(2)}) copy-start(bf16[256,4096]{1,0:T(8,128)(2,1)} %copy-done) | copy-start | bytes 6291460
where the time goes:
time: 121 us; the launch traced here: 120 us
  blocking collectives  51 us (42%)
  waiting for transfers between devices  29.9 us (25%)
  starting transfers between devices  18.5 us (15%)
  Pallas kernels  13.7 us (11%)
  local copies, waits for them, and re-layouts  5.08 us (4%)
  between operations  1.39 us (1%)
    all_to_all x5, blocking collectives, exchange(): return lax.all_to_all(array, axes, split_axis=0, concat_axis=0, tiled=True)  51 us
    all_to_all x2, waiting for transfers between devices, exchange(): return lax.all_to_all(array, axes, split_axis=0, concat_axis=0, tiled=True)  29.9 us
    all_to_all x2, starting transfers between devices, exchange(): return lax.all_to_all(array, axes, split_axis=0, concat_axis=0, tiled=True)  18.5 us
    unnamed x13, local copies, waits for them, and re-layouts  4.38 us
    pallas_call x1, Pallas kernels, local(): call(first_kernel, (shape(16, 2, 256, 128), shape(4, 4, 128)), [vmem((2,...  4.06 us
    pallas_call x1, Pallas kernels, local(): call(eval_green_kernel, (shape(256, 4096, dtype=bf16), shape(256, 4096, d...  3.4 us
  transfers between devices with their start and end apart: 2, of which 2 were waited for; matrix products, arithmetic and copies ran while one was open for 0% of the time, Pallas kernels for 3%

commit v1 on v0

v1 whole, which is shorter than its diff:
```python
import math

import jax
import jax.numpy as jnp
from jax import lax
from jax.experimental import pallas as pl
from jax.experimental.pallas import tpu as pltpu
from jax.sharding import Mesh
from jax.sharding import PartitionSpec as P

WALL = 64
SPK = ("ylo", "x", "core")
PTS = ("yhi", "za", "zb", "zc")
FLD = ("za", "zb")
BANKS = ("x", "core")
NEAR = ("ylo", "yhi", "zc")

wall_pitch = 0.05
front_gap = 0.5
depth_span = 3.15
side_span = 3.2
tikhonov = 0.1
centre = (WALL - 1) * 0.5

SIN = (4.442879676818848, -7.307816505432129, 3.5977742671966553, -0.7911993861198425)
COS = (-1.4142040014266968, 6.97763729095459, -5.715188026428223, 1.728213906288147)
ROUNDER = 12582912.0

f32 = jnp.float32
bf16 = jnp.bfloat16
vmem = pltpu.VMEM


def spec(space=pltpu.VMEM):
    return pl.BlockSpec(memory_space=space)


def shape(*dims, dtype=f32):
    return jax.ShapeDtypeStruct(dims, dtype)


WHOLE = 64
SPACES = {"s": pltpu.SMEM, "v": pltpu.VMEM, "a": pl.ANY}


def call(kernel, out_shapes, scratch, limit_mib, spaces, name, flops, trans=0):
    return pl.pallas_call(
        kernel,
        out_shape=out_shapes,
        in_specs=[spec(SPACES[c]) for c in spaces],
        out_specs=jax.tree.map(lambda _: spec(), out_shapes),
        scratch_shapes=scratch,
        compiler_params=pltpu.CompilerParams(vmem_limit_bytes=min(limit_mib << 20, 67043328)),
        cost_estimate=pl.CostEstimate(flops=flops, bytes_accessed=1 << 20, transcendentals=trans),
        name=name,
    )


def poly(coeffs, u):
    out = coeffs[-1]
    for c in coeffs[-2::-1]:
        out = out * u + c
    return out


def green(scaled, strength):
    inverse = lax.rsqrt(scaled)
    turns = scaled * inverse
    magnitude = inverse * strength
    whole = (turns + ROUNDER) - ROUNDER
    frac = turns - whole
    u = frac * frac
    s = poly(SIN, u) * frac
    c = poly(COS, u)
    ms = magnitude * s
    return magnitude - ms * s, ms * c


def column(row):
    return jnp.broadcast_to(row, (128, 128)).T


def total(x):
    return jnp.broadcast_to(jnp.sum(x, keepdims=True), (1, 128))


def fold(x):
    out = x[0]
    for i in range(1, x.shape[0]):
        out = out + x[i]
    return out


def split_bf16(x):
    high = x.astype(bf16)
    return high, (x - high.astype(f32)).astype(bf16)


def iota(dims, dim):
    return lax.broadcasted_iota(jnp.int32, dims, dim)


def prepare_kernel(desired_hbm, points_hbm, send_ref, desired_ref, points_ref, sems):
    copies = [
        pltpu.make_async_copy(desired_hbm, desired_ref, sems.at[0]),
        pltpu.make_async_copy(points_hbm, points_ref, sems.at[1]),
    ]
    for copy in copies:
        copy.start()
    lanes = pl.ds(pl.multiple_of(lax.axis_index("ylo") * 128, 128), 128)
    for copy in copies:
        copy.wait()
    points = points_ref[:, lanes]
    for f in range(8):
        send_ref[f, 0:1, :] = desired_ref[0, f : f + 1, lanes]
        send_ref[f, 1:2, :] = desired_ref[1, f : f + 1, lanes]
        send_ref[f, 2:5, :] = points


def eval_green_kernel(wave_ref, eval_ref, high_ref, low_ref, token_ref):
    kappa = wave_ref[0] * (0.5 / math.pi)
    strength = kappa * (1.0 / WALL)
    token_ref[...] = jnp.zeros_like(token_ref)
    ex = column((front_gap + eval_ref[0:1, :] * depth_span) * kappa)
    ey = column((eval_ref[1:2, :] * side_span - 0.5 * side_span) * kappa)
    ez = column((eval_ref[2:3, :] * side_span - 0.5 * side_span) * kappa)
    lane = iota((1, 128), 1)
    dz = ez - (jnp.bitwise_and(lane, WALL - 1).astype(f32) - centre) * (wall_pitch * kappa)
    base = ex * ex + dz * dz

    def step(i, carry):
        wall_row = i * 2 + jnp.right_shift(lane, 6)
        wy = (wall_row.astype(f32) - centre) * (wall_pitch * kappa)
        lanes = pl.ds(pl.multiple_of(i * 128, 128), 128)
        for start in range(0, 128, 64):
            rows = slice(start, start + 64)
            dy = ey[rows] - wy
            real, imag = green(base[rows] + dy * dy, strength)
            rh, rl = split_bf16(real)
            ih, il = split_bf16(imag)
            high_ref[start : start + 64, lanes] = rh
            low_ref[start : start + 64, lanes] = rl
            high_ref[128 + start : 192 + start, lanes] = ih
            low_ref[128 + start : 192 + start, lanes] = il
        return carry

    lax.fori_loop(0, 32, step, 0)


def first_kernel(wave_ref, got_ref, token_ref, g_ref, send_ref, dz2_ref, rest_ref, acc_ref):
    kappa = wave_ref[0] * (0.5 / math.pi)
    strength = kappa * (1.0 / WALL)
    wz = (iota((WALL, 128), 0).astype(f32) - centre) * (wall_pitch * kappa)
    wy = ((iota((8, 128), 0) + lax.axis_index(BANKS) * 8).astype(f32) - centre) * (wall_pitch * kappa)
    for j in range(8):
        px = (front_gap + got_ref[j, 2:3, :] * depth_span) * kappa
        py = (got_ref[j, 3:4, :] * side_span - 0.5 * side_span) * kappa
        pz = (got_ref[j, 4:5, :] * side_span - 0.5 * side_span) * kappa
        dz = pz - wz
        dz2_ref[j] = dz * dz
        dy = py - wy
        rest_ref[j] = px * px + dy * dy
    size = 32

    def wall_row(r, carry):
        for start in range(0, WALL, size):
            rows = pl.ds(pl.multiple_of(r * WALL + start, size), size)

            def block(j, sums):
                real_sum, imag_sum = sums
                vr = got_ref[j, 0:1, :]
                vi = got_ref[j, 1:2, :]
                real, imag = green(
                    dz2_ref[j, start : start + size, :] + rest_ref[j, pl.ds(r, 1), :], strength
                )
                g_ref[j, 0, rows, :] = real
                g_ref[j, 1, rows, :] = imag
                real_sum = real_sum + (real * vr + imag * vi)
                imag_sum = imag_sum + (real * vi - imag * vr)
                return real_sum, imag_sum

            zero = jnp.zeros((size, 128), f32)
            real_sum, imag_sum = lax.fori_loop(0, 8, block, (zero, zero), unroll=2)
            acc_ref[0, rows, :] = real_sum
            acc_ref[1, rows, :] = imag_sum
        return carry

    lax.fori_loop(0, 8, wall_row, 0)
    rows = rows_of(acc_ref)
    for i in range(8):
        send_ref[i] = rows


def rows_of(acc_ref):
    rows = []
    for part in range(2):
        for blk in range(4):
            block = acc_ref[part, blk * 128 : blk * 128 + 128, :]
            rows.append(jnp.sum(block.T, axis=0, keepdims=True))
    return jnp.concatenate(rows, axis=0)


def forward(g_ref, rows, col_ref, out_ref):
    for part in range(2):
        for blk in range(4):
            i = part * 4 + blk
            col_ref[part, blk * 128 : blk * 128 + 128, :] = column(rows[i : i + 1, :])
    size = 64

    def step(t, carry):
        real_sum = jnp.zeros((8, 128), f32)
        imag_sum = jnp.zeros((8, 128), f32)
        for k in range(512 // size):
            at = slice(k * size, k * size + size)
            gr = g_ref[t, 0, at, :]
            gi = g_ref[t, 1, at, :]
            qr = col_ref[0, at, :]
            qi = col_ref[1, at, :]
            real_sum = real_sum + (gr * qr - gi * qi).reshape(size // 8, 8, 128).sum(axis=0)
            imag_sum = imag_sum + (gi * qr + gr * qi).reshape(size // 8, 8, 128).sum(axis=0)
        out_ref[pl.ds(t, 1), :] = jnp.sum(real_sum, axis=0, keepdims=True)
        out_ref[pl.ds(t + 8, 1), :] = jnp.sum(imag_sum, axis=0, keepdims=True)
        return carry

    lax.fori_loop(0, 8, step, 0)


def adjoint(g_ref, im, acc_ref):
    size = 64

    def chunk(k, carry):
        rows = pl.ds(pl.multiple_of(k * size, size), size)
        real_sum = jnp.zeros((size, 128), f32)
        imag_sum = jnp.zeros((size, 128), f32)
        for t in range(8):
            vr = im[t : t + 1, :]
            vi = im[8 + t : 9 + t, :]
            gr = g_ref[t, 0, rows, :]
            gi = g_ref[t, 1, rows, :]
            real_sum = real_sum + (gr * vr + gi * vi)
            imag_sum = imag_sum + (gr * vi - gi * vr)
        acc_ref[0, rows, :] = real_sum
        acc_ref[1, rows, :] = imag_sum
        return carry

    lax.fori_loop(0, 512 // size, chunk, 0)
    return rows_of(acc_ref)


def image_kernel(g_ref, got_ref, send_ref, own_ref, col_ref, im_ref):
    g0 = fold(got_ref)
    own_ref[...] = g0
    forward(g_ref, g0, col_ref, im_ref)
    im = im_ref[...]
    for i in range(8):
        send_ref[i, 0:16, :] = im
        send_ref[i, 16:24, :] = g0


def adjoint_kernel(g_ref, got_ref, send_ref, acc_ref):
    im = fold(got_ref[:, 0:16, :])
    rows = adjoint(g_ref, im, acc_ref)
    norm = jnp.broadcast_to(total(im * im), (8, 128))
    for i in range(8):
        send_ref[i, 0:8, :] = rows
        send_ref[i, 8:24, :] = im
        send_ref[i, 24:32, :] = norm


def gathered_total(a, b):
    return total(fold(a * b))


def second_image_kernel(g_ref, got3_ref, got2_ref, g0_ref, send_ref, alpha_ref, col_ref, im_ref):
    all_g0 = got2_ref[:, 16:24, :]
    gamma = gathered_total(all_g0, all_g0)
    g0 = g0_ref[...]
    back = fold(got3_ref[:, 0:8, :])
    norm = fold(got3_ref[:, 24:25, :])
    alpha = gamma / (norm + tikhonov * gamma)
    alpha_ref[0:1, :] = alpha
    alpha_ref[1:2, :] = gamma
    g1 = g0 - alpha * (back + tikhonov * g0)
    forward(g_ref, g1, col_ref, im_ref)
    im = im_ref[...]
    for i in range(8):
        send_ref[i, 0:16, :] = im
        send_ref[i, 16:24, :] = g1


def norm_kernel(got4_ref, got2_ref, alpha_ref, send_ref, scalar_ref):
    all_g0 = got2_ref[:, 16:24, :]
    all_g1 = got4_ref[:, 16:24, :]
    gamma0 = alpha_ref[1:2, :]
    gamma1 = gathered_total(all_g1, all_g1)
    cross = gathered_total(all_g1, all_g0)
    beta = gamma1 / gamma0
    im1 = fold(got4_ref[:, 0:16, :]) + beta * fold(got2_ref[:, 0:16, :])
    scalar_ref[0:1, :] = beta
    scalar_ref[1:2, :] = gamma1
    scalar_ref[2:3, :] = gamma1 + (2.0 * cross + beta * gamma0) * beta
    square = jnp.broadcast_to(total(im1 * im1), (8, 128))
    for i in range(8):
        send_ref[i, 0:16, :] = im1
        send_ref[i, 16:24, :] = square


def drive_kernel(got5_ref, got3_ref, got2_ref, got4_ref, alpha_ref, scalar_ref, send_ref):
    alpha0 = alpha_ref[0:1, :]
    beta = scalar_ref[0:1, :]
    norm = fold(got5_ref[:, 16:17, :])
    alpha1 = scalar_ref[1:2, :] / (norm + tikhonov * scalar_ref[2:3, :])
    from_first = alpha0 + alpha1 * beta
    for u in range(8):
        rows = from_first * got2_ref[u, 16:24, :] + alpha1 * got4_ref[u, 16:24, :]
        for i in range(8):
            send_ref[i, 8 * u : 8 * u + 8, :] = rows
    for half in range(2):
        member = half * 4 + lax.axis_index(("yhi", "zc"))
        change = alpha0 * got3_ref[member, 8:24, :] + alpha1 * got5_ref[member, 0:16, :]
        for i in range(8):
            send_ref[i, 64 + half : 65 + half, :] = change[i : i + 1, :]
            send_ref[i, 66 + half : 67 + half, :] = change[8 + i : 9 + i, :]


def field_kernel(got_ref, high_ref, low_ref, desired_ref, cells_ref, drives_ref, residual_ref, field_ref):
    for part in range(2):
        for half in range(2):
            lanes = slice(half * 128, half * 128 + 128)
            residual_ref[part, :, lanes] = desired_ref[part, :, lanes] - got_ref[:, 64 + part * 2 + half, :]
    drives = got_ref[:, 0:64, :].reshape(512, 128)
    for blk in range(2):
        lanes = slice(blk * 128, blk * 128 + 128)
        cells = cells_ref[pl.ds(lax.axis_index(SPK) * 2 + blk, 1), :]
        pick = (iota((128, 128), 0) == jnp.bitwise_and(cells, 127)).astype(f32)
        picked = jnp.dot(drives, pick, precision=lax.Precision.HIGHEST, preferred_element_type=f32)
        line = iota((64, 128), 0)
        place = jnp.right_shift(line, 3) * 4 + jnp.bitwise_and(line, 3)
        right = place == jnp.right_shift(cells, 7)
        real = jnp.bitwise_and(line, 4) == 0
        for part in range(2):
            mask = jnp.where(right & (real if part == 0 else ~real), 1.0, 0.0)
            for f in range(8):
                rows = picked[f * 64 : f * 64 + 64, :] * mask
                drives_ref[part, f : f + 1, lanes] = jnp.sum(rows, axis=0, keepdims=True)
    out = jnp.zeros((32, 256), f32)
    fine = jnp.zeros((16, 256), f32)
    dims = (((1,), (1,)), ((), ()))
    for u in range(8):
        for pair in range(2):
            parts = [
                jnp.concatenate(
                    [got_ref[:, u * 8 + part * 4 + pair * 2 + k, :] for k in range(2)], axis=1
                )
                for part in range(2)
            ]
            high, low = split_bf16(jnp.concatenate(parts, axis=0))
            both = jnp.concatenate([high, low], axis=0)
            at = (u * 2 + pair) * 256
            lanes = slice(at, at + 256)
            out = out + lax.dot_general(both, high_ref[:, lanes], dims, preferred_element_type=f32)
            fine = fine + lax.dot_general(high, low_ref[:, lanes], dims, preferred_element_type=f32)
    out = out[0:16, :] + out[16:32, :] + fine
    field_ref[0] = out[0:8, 0:128] - out[8:16, 128:256]
    field_ref[1] = out[0:8, 128:256] + out[8:16, 0:128]


def exchange(array, axes):
    return lax.all_to_all(array, axes, split_axis=0, concat_axis=0, tiled=True)


def local(desired, spk_cells, pt_cells, eval_cells, wavenumber):
    send0 = call(
        prepare_kernel,
        shape(8, 8, 128),
        [vmem((2, 8, 256), f32), vmem((3, 256), f32), pltpu.SemaphoreType.DMA((2,))],
        WHOLE, "aa", "prepare", 1024,
    )(desired, pt_cells)
    got0 = exchange(send0, FLD)
    high, low, token = call(
        eval_green_kernel,
        (shape(256, 4096, dtype=bf16), shape(256, 4096, dtype=bf16), shape(8, 128)),
        [], 8, "sv", "eval_green", 524288 * 40, 524288,
    )(wavenumber, eval_cells)
    g, send1 = call(
        first_kernel,
        (shape(8, 2, 512, 128), shape(8, 8, 128)),
        [vmem((8, 64, 128), f32), vmem((8, 8, 128), f32), vmem((2, 512, 128), f32)],
        8, "svv", "first", 524288 * 48, 524288,
    )(wavenumber, got0, token)
    got1 = exchange(send1, NEAR)
    send2, g0 = call(
        image_kernel,
        (shape(8, 24, 128), shape(8, 128)),
        [vmem((2, 512, 128), f32), vmem((16, 128), f32)], 8, "vv", "image", 524288 * 8,
    )(g, got1)
    got2 = exchange(send2, BANKS)
    send3 = call(
        adjoint_kernel, shape(8, 32, 128), [vmem((2, 512, 128), f32)], 8, "vv", "adjoint", 524288 * 8,
    )(g, got2)
    got3 = exchange(send3, NEAR)
    send4, alpha = call(
        second_image_kernel,
        (shape(8, 24, 128), shape(2, 128)),
        [vmem((2, 512, 128), f32), vmem((16, 128), f32)], 8, "vvvv", "second_image", 524288 * 8,
    )(g, got3, got2, g0)
    got4 = exchange(send4, BANKS)
    send5, scalars = call(
        norm_kernel, (shape(8, 24, 128), shape(3, 128)), [], 8, "vvv", "norm", 81920,
    )(got4, got2, alpha)
    got5 = exchange(send5, NEAR)
    send6 = call(
        drive_kernel, shape(8, 72, 128), [], 8, "vvvvvv", "drive", 81920,
    )(got5, got3, got2, got4, alpha, scalars)
    got6 = exchange(send6, FLD)
    return call(
        field_kernel,
        (shape(2, 8, 256), shape(2, 8, 256), shape(2, 8, 128)),
        [], 12, "vvvvv", "field", 524288 * 96,
    )(got6, high, low, desired, spk_cells.reshape(32, 128))


def solution(mesh):
    split = Mesh(
        mesh.devices.reshape(2, 4, 2, 2, 4, 2, 2), ("ylo", "x", "core", "yhi", "za", "zb", "zc")
    )
    in_specs = (P(None, None, PTS), P(), P(None, PTS), P(None, SPK + PTS), P())
    out_specs = (P(None, None, SPK), P(None, None, PTS), P(None, None, SPK + PTS))
    return jax.shard_map(local, mesh=split, in_specs=in_specs, out_specs=out_specs, check_vma=False)
```

time: 121 us -> 112 us (0.926)
  the two profiles are of different devices: /device:TPU:8 before, /device:TPU:1 now
where the time goes in v1:
time: 112 us; the launch traced here: 110 us
  blocking collectives  71.6 us (64%)
  starting transfers between devices  15.6 us (14%)
  Pallas kernels  13.2 us (12%)
  waiting for transfers between devices  6.06 us (5%)
  local copies, waits for them, and re-layouts  2.01 us (2%)
  between operations  1.35 us (1%)
    all_to_all x6, blocking collectives, exchange(): return lax.all_to_all(array, axes, split_axis=0, concat_axis=0, tiled=True)  71.6 us
    all_to_all x1, starting transfers between devices, exchange(): return lax.all_to_all(array, axes, split_axis=0, concat_axis=0, tiled=True)  15.6 us
    all_to_all x1, waiting for transfers between devices, exchange(): return lax.all_to_all(array, axes, split_axis=0, concat_axis=0, tiled=True)  6.06 us
    pallas_call x1, Pallas kernels, local(): call(first_kernel, (shape(8, 2, 512, 128), shape(8, 8, 128)), [vmem((8, 6...  3.29 us
    pallas_call x1, Pallas kernels, local(): call(eval_green_kernel, (shape(256, 4096, dtype=bf16), shape(256, 4096, d...  3.03 us
  transfers between devices with their start and end apart: 1, of which 1 were waited for; matrix products, arithmetic and copies ran while one was open for 0% of the time, Pallas kernels for 3%

profile of v1, /device:TPU:1, one launch (start us, length us, event | category | flops | bytes accessed | tf_op | source)
XLA Modules:
  0.0 109.8 jit_solution(15892766248598920936)
XLA Ops:
  0.6 1.3 %prepare.1 = f32[8,8,128]{2,1,0:T(8,128)} custom-call(f32[2,8,256]{2,1,0:T(8,128)} %desired_ref.1, f32[3,256]{1,0:T(4,128)} %points_hbm.1), custom_call_target="tpu_custom_call" | custom-call | flops 1024 | bytes 1048576 | tf_op jit(solution)/shard_map/prepare/pallas_call | solution.py:373
  2.0 15.6 %all-to-all-start = ((f32[8,8,128]{2,1,0:T(8,128)}), f32[8,8,128]{2,1,0:T(8,128)S(1)}, u32[]{:S(2)}, u32[]{:S(2)}) async-start(f32[8,8,128]{2,1,0:T(8,128)} %prepare.1), calls=%async_computation | async-start | bytes 65536 | tf_op jit(solution)/shard_map/all_to_all | solution.py:369
  18.3 0.0 copy-start.4
  18.3 0.7 copy-done.4
  19.0 3.0 %eval_green.1 = (bf16[256,4096]{1,0:T(8,128)(2,1)S(1)}, bf16[256,4096]{1,0:T(8,128)(2,1)S(1)}, f32[8,128]{1,0:T(8,128)S(1)}) custom-call(f32[1]{0:T(128)S(6)} %copy.8.wave_ref, f32[3,128]{1,0:T(4,128)S(1)} %copy-done.4), custom_call_target="tpu_custom_call" | custom-call | flops 20971520 | bytes 1048576 | tf_op jit(solution)/shard_map/eval_green/pallas_call | solution.py:380
  22.0 0.0 copy-start
  22.0 1.3 %copy-done = bf16[256,4096]{1,0:T(8,128)(2,1)} copy-done((bf16[256,4096]{1,0:T(8,128)(2,1)}, bf16[256,4096]{1,0:T(8,128)(2,1)S(1)}, u32[]{:S(2)}) %copy-start) | copy-done | bytes 2097176
  23.3 6.1 %all-to-all-done.got_ref = f32[8,8,128]{2,1,0:T(8,128)S(1)} async-done(((f32[8,8,128]{2,1,0:T(8,128)}), f32[8,8,128]{2,1,0:T(8,128)S(1)}, u32[]{:S(2)}, u32[]{:S(2)}) %all-to-all-start) | async-done | bytes 32800 | tf_op jit(solution)/shard_map/all_to_all | solution.py:369
  29.4 3.3 %first.1 = (f32[8,2,512,128]{3,2,1,0:T(8,128)S(1)}, f32[8,8,128]{2,1,0:T(8,128)S(1)}) custom-call(f32[1]{0:T(128)S(6)} %copy.8.wave_ref, f32[8,8,128]{2,1,0:T(8,128)S(1)} %all-to-all-done.got_ref, f32[8,128]{1,0:T(8,128)S(1)} %get-tuple-element.14.token_ref), custom_call_target="tpu_custom_call" | custom-call | flops 25165824 | bytes 1048576 | tf_op jit(solution)/shard_map/first/pallas_call | solution.py:385
  32.7 9.6 %all_to_all.35.got_ref = f32[8,8,128]{2,1,0:T(8,128)S(1)} all-to-all(f32[8,8,128]{2,1,0:T(8,128)S(1)} %get-tuple-element.16), channel_id=1, replica_groups=mesh['ylo'=2,'x'=4,'core'=2,'yhi'=2,'za'=4,'zb'=2,'zc'=2] {'ylo','yhi','..., dimensions={0} | all-to-all | bytes 65536 | tf_op jit(solution)/shard_map/all_to_all | solution.py:369
  42.3 1.0 image.1
  43.3 12.6 %all_to_all.36.got_ref.got2_ref = f32[8,24,128]{2,1,0:T(8,128)S(1)} all-to-all(f32[8,24,128]{2,1,0:T(8,128)S(1)} %get-tuple-element.17), channel_id=1, replica_groups=mesh['ylo'=2,'x'=4,'core'=2,'yhi'=2,'za'=4,'zb'=2,'zc'=2] {'x','core'}, dimensions={0} | all-to-all | bytes 196608 | tf_op jit(solution)/shard_map/all_to_all | solution.py:369
  55.9 0.9 adjoint.1
  56.8 8.0 %all_to_all.37.got3_ref = f32[8,32,128]{2,1,0:T(8,128)S(1)} all-to-all(f32[8,32,128]{2,1,0:T(8,128)S(1)} %adjoint.1), channel_id=1, replica_groups=mesh['ylo'=2,'x'=4,'core'=2,'yhi'=2,'za'=4,'zb'=2,'zc'=2] {'ylo','yhi','..., dimensions={0} | all-to-all | bytes 262144 | tf_op jit(solution)/shard_map/all_to_all | solution.py:369
  64.8 0.0 copy-start.1
  64.8 1.1 second_image.1
  65.9 9.3 %all_to_all.38.got4_ref = f32[8,24,128]{2,1,0:T(8,128)S(1)} all-to-all(f32[8,24,128]{2,1,0:T(8,128)S(1)} %get-tuple-element.19), channel_id=1, replica_groups=mesh['ylo'=2,'x'=4,'core'=2,'yhi'=2,'za'=4,'zb'=2,'zc'=2] {'x','core'}, dimensions={0} | all-to-all | bytes 196608 | tf_op jit(solution)/shard_map/all_to_all | solution.py:369
  75.2 0.2 norm.1
  75.5 7.9 %all_to_all.39.got5_ref = f32[8,24,128]{2,1,0:T(8,128)S(1)} all-to-all(f32[8,24,128]{2,1,0:T(8,128)S(1)} %get-tuple-element.21), channel_id=1, replica_groups=mesh['ylo'=2,'x'=4,'core'=2,'yhi'=2,'za'=4,'zb'=2,'zc'=2] {'ylo','yhi','..., dimensions={0} | all-to-all | bytes 196608 | tf_op jit(solution)/shard_map/all_to_all | solution.py:369
  83.4 24.2 %all_to_all.40.got_ref = f32[8,72,128]{2,1,0:T(8,128)S(1)} all-to-all(f32[8,72,128]{2,1,0:T(8,128)S(1)} %drive.1), channel_id=1, replica_groups=mesh['ylo'=2,'x'=4,'core'=2,'yhi'=2,'za'=4,'zb'=2,'zc'=2] {'za','zb'}, dimensions={0} | all-to-all | bytes 589824 | tf_op jit(solution)/shard_map/all_to_all | solution.py:369
  107.6 0.0 copy-done.1
  107.6 0.0 copy-done.2
  107.6 0.0 copy-done.3
  107.6 2.2 %field.1 = (f32[2,8,256]{2,1,0:T(8,128)}, f32[2,8,256]{2,1,0:T(8,128)}, f32[2,8,128]{2,1,0:T(8,128)}) custom-call(f32[8,72,128]{2,1,0:T(8,128)S(1)} %all_to_all.40.got_ref, bf16[256,4096]{1,0:T(8,128)(2,1)S(1)} %get-tuple-element.23.high_ref, bf16[256,4096]{1,0:T(8,128)(2,1)S(1)} %copy-done.1, f32[2,8,256]{2,1,0:T(8,128)S(1)} %copy-done.2, s32[32,128]{1,0:T(8,128)S(1)} %bitcast.1), custom_call_target="tpu_custom_call" | custom-call | flops 50331648 | bytes 1048576 | tf_op jit(solution)/shard_map/field/pallas_call | solution.py:416
  (3 shorter events, 0.0 us)
Async XLA Ops:
  2.0 27.4 %all-to-all-start = ((f32[8,8,128]{2,1,0:T(8,128)}), f32[8,8,128]{2,1,0:T(8,128)S(1)}, u32[]{:S(2)}, u32[]{:S(2)}) async-start(f32[8,8,128]{2,1,0:T(8,128)} %prepare.1), calls=%async_computation | async-start | bytes 65536 | tf_op jit(solution)/shard_map/all_to_all | solution.py:369
  18.3 0.7 copy-start.4
  22.0 1.3 %copy-start = (bf16[256,4096]{1,0:T(8,128)(2,1)}, bf16[256,4096]{1,0:T(8,128)(2,1)S(1)}, u32[]{:S(2)}) copy-start(bf16[256,4096]{1,0:T(8,128)(2,1)S(1)} %get-tuple-element.24.low_ref) | copy-start | bytes 6291460
  64.8 42.8 %copy-start.1 = (bf16[256,4096]{1,0:T(8,128)(2,1)S(1)}, bf16[256,4096]{1,0:T(8,128)(2,1)}, u32[]{:S(2)}) copy-start(bf16[256,4096]{1,0:T(8,128)(2,1)} %copy-done) | copy-start | bytes 6291460
  64.8 42.8 %copy-start.2 = (f32[2,8,256]{2,1,0:T(8,128)S(1)}, f32[2,8,256]{2,1,0:T(8,128)}, u32[]{:S(2)}) copy-start(f32[2,8,256]{2,1,0:T(8,128)} %desired_ref.1) | copy-start | bytes 49156
  64.8 42.8 %copy-start.3 = (s32[4096]{0:T(1024)S(1)}, s32[4096]{0:T(1024)}, u32[]{:S(2)}) copy-start(s32[4096]{0:T(1024)} %param.6) | copy-start | bytes 49156

commit v2 on v1

--- a/solution.py
+++ b/solution.py
@@ -40,15 +40,17 @@
 
 
 WHOLE = 64
-SPACES = {"s": pltpu.SMEM, "v": pltpu.VMEM, "a": pl.ANY}
-
-
-def call(kernel, out_shapes, scratch, limit_mib, spaces, name, flops, trans=0):
+SPACES = {"s": pltpu.SMEM, "v": pltpu.VMEM, "a": pl.ANY, "h": pltpu.HBM}
+
+
+def call(kernel, out_shapes, scratch, limit_mib, spaces, name, flops, trans=0, out_spaces=None):
     return pl.pallas_call(
         kernel,
         out_shape=out_shapes,
         in_specs=[spec(SPACES[c]) for c in spaces],
-        out_specs=jax.tree.map(lambda _: spec(), out_shapes),
+        out_specs=tuple(spec(SPACES[c]) for c in out_spaces)
+        if out_spaces
+        else jax.tree.map(lambda _: spec(), out_shapes),
         scratch_shapes=scratch,
         compiler_params=pltpu.CompilerParams(vmem_limit_bytes=min(limit_mib << 20, 67043328)),
         cost_estimate=pl.CostEstimate(flops=flops, bytes_accessed=1 << 20, transcendentals=trans),
@@ -100,27 +102,28 @@
     return lax.broadcasted_iota(jnp.int32, dims, dim)
 
 
-def prepare_kernel(desired_hbm, points_hbm, send_ref, desired_ref, points_ref, sems):
-    copies = [
-        pltpu.make_async_copy(desired_hbm, desired_ref, sems.at[0]),
-        pltpu.make_async_copy(points_hbm, points_ref, sems.at[1]),
-    ]
+def prepare_kernel(desired_hbm, points_hbm, send_hbm, sems):
+    lanes = pl.ds(pl.multiple_of(lax.axis_index("ylo") * 128, 128), 128)
+    copies = []
+    for part in range(2):
+        copies.append(
+            pltpu.make_async_copy(
+                desired_hbm.at[part, :, lanes], send_hbm.at[:, part, :], sems.at[part]
+            )
+        )
+    for f in range(8):
+        copies.append(
+            pltpu.make_async_copy(points_hbm.at[:, lanes], send_hbm.at[f, 2:5, :], sems.at[2 + f])
+        )
     for copy in copies:
         copy.start()
-    lanes = pl.ds(pl.multiple_of(lax.axis_index("ylo") * 128, 128), 128)
     for copy in copies:
         copy.wait()
-    points = points_ref[:, lanes]
-    for f in range(8):
-        send_ref[f, 0:1, :] = desired_ref[0, f : f + 1, lanes]
-        send_ref[f, 1:2, :] = desired_ref[1, f : f + 1, lanes]
-        send_ref[f, 2:5, :] = points
-
-
-def eval_green_kernel(wave_ref, eval_ref, high_ref, low_ref, token_ref):
+
+
+def eval_green_kernel(wave_ref, eval_ref, high_hbm, low_hbm, high_ref, low_ref, sems):
     kappa = wave_ref[0] * (0.5 / math.pi)
     strength = kappa * (1.0 / WALL)
-    token_ref[...] = jnp.zeros_like(token_ref)
     ex = column((front_gap + eval_ref[0:1, :] * depth_span) * kappa)
     ey = column((eval_ref[1:2, :] * side_span - 0.5 * side_span) * kappa)
     ez = column((eval_ref[2:3, :] * side_span - 0.5 * side_span) * kappa)
@@ -144,10 +147,20 @@
             low_ref[128 + start : 192 + start, lanes] = il
         return carry
 
-    lax.fori_loop(0, 32, step, 0)
-
-
-def first_kernel(wave_ref, got_ref, token_ref, g_ref, send_ref, dz2_ref, rest_ref, acc_ref):
+    copies = []
+    for quarter in range(4):
+        lax.fori_loop(quarter * 8, quarter * 8 + 8, step, 0)
+        lanes = slice(quarter * 1024, quarter * 1024 + 1024)
+        for k, (ref, hbm) in enumerate(((high_ref, high_hbm), (low_ref, low_hbm))):
+            copies.append(
+                pltpu.make_async_copy(ref.at[:, lanes], hbm.at[:, lanes], sems.at[k, quarter])
+            )
+            copies[-1].start()
+    for copy in copies:
+        copy.wait()
+
+
+def first_kernel(wave_ref, got_ref, g_ref, send_ref, dz2_ref, rest_ref, acc_ref):
     kappa = wave_ref[0] * (0.5 / math.pi)
     strength = kappa * (1.0 / WALL)
     wz = (iota((WALL, 128), 0).astype(f32) - centre) * (wall_pitch * kappa)
@@ -323,26 +336,39 @@
             send_ref[i, 66 + half : 67 + half, :] = change[8 + i : 9 + i, :]
 
 
+ROWS = 72
+
+
+def of_fields(got_ref, row):
+    return got_ref[pl.ds(row, 8, stride=ROWS), :]
+
+
 def field_kernel(got_ref, high_ref, low_ref, desired_ref, cells_ref, drives_ref, residual_ref, field_ref):
     for part in range(2):
         for half in range(2):
             lanes = slice(half * 128, half * 128 + 128)
-            residual_ref[part, :, lanes] = desired_ref[part, :, lanes] - got_ref[:, 64 + part * 2 + half, :]
-    drives = got_ref[:, 0:64, :].reshape(512, 128)
-    for blk in range(2):
-        lanes = slice(blk * 128, blk * 128 + 128)
-        cells = cells_ref[pl.ds(lax.axis_index(SPK) * 2 + blk, 1), :]
-        pick = (iota((128, 128), 0) == jnp.bitwise_and(cells, 127)).astype(f32)
-        picked = jnp.dot(drives, pick, precision=lax.Precision.HIGHEST, preferred_element_type=f32)
-        line = iota((64, 128), 0)
-        place = jnp.right_shift(line, 3) * 4 + jnp.bitwise_and(line, 3)
-        right = place == jnp.right_shift(cells, 7)
-        real = jnp.bitwise_and(line, 4) == 0
-        for part in range(2):
-            mask = jnp.where(right & (real if part == 0 else ~real), 1.0, 0.0)
-            for f in range(8):
-                rows = picked[f * 64 : f * 64 + 64, :] * mask
-                drives_ref[part, f : f + 1, lanes] = jnp.sum(rows, axis=0, keepdims=True)
+            residual_ref[part, :, lanes] = desired_ref[part, :, lanes] - of_fields(
+                got_ref, 64 + part * 2 + half
+            )
+    first_cell = lax.axis_index(SPK) * 2
+    cells = jnp.concatenate([cells_ref[pl.ds(first_cell + blk, 1), :] for blk in range(2)], axis=1)
+    pick = jnp.where(iota((128, 256), 0) == jnp.bitwise_and(cells, 127), 1.0, 0.0).astype(bf16)
+    line = iota((64, 256), 0)
+    place = jnp.right_shift(line, 3) * 4 + jnp.bitwise_and(line, 3)
+    right = place == jnp.right_shift(cells, 7)
+    is_real = jnp.bitwise_and(line, 4) == 0
+    real_mask = jnp.where(right & is_real, 1.0, 0.0)
+    imag_mask = jnp.where(right & ~is_real, 1.0, 0.0)
+    for f in range(8):
+        x = got_ref[f * ROWS : f * ROWS + 64, :]
+        high = x.astype(bf16)
+        left = x - high.astype(f32)
+        middle, low = split_bf16(left)
+        three = jnp.concatenate([high, middle, low], axis=0)
+        picked = jnp.dot(three, pick, preferred_element_type=f32)
+        picked = picked[0:64] + picked[64:128] + picked[128:192]
+        drives_ref[0, f : f + 1, :] = jnp.sum(picked * real_mask, axis=0, keepdims=True)
+        drives_ref[1, f : f + 1, :] = jnp.sum(picked * imag_mask, axis=0, keepdims=True)
     out = jnp.zeros((32, 256), f32)
     fine = jnp.zeros((16, 256), f32)
     dims = (((1,), (1,)), ((), ()))
@@ -350,7 +376,7 @@
         for pair in range(2):
             parts = [
                 jnp.concatenate(
-                    [got_ref[:, u * 8 + part * 4 + pair * 2 + k, :] for k in range(2)], axis=1
+                    [of_fields(got_ref, u * 8 + part * 4 + pair * 2 + k) for k in range(2)], axis=1
                 )
                 for part in range(2)
             ]
@@ -370,24 +396,24 @@
 
 
 def local(desired, spk_cells, pt_cells, eval_cells, wavenumber):
-    send0 = call(
-        prepare_kernel,
-        shape(8, 8, 128),
-        [vmem((2, 8, 256), f32), vmem((3, 256), f32), pltpu.SemaphoreType.DMA((2,))],
-        WHOLE, "aa", "prepare", 1024,
+    (send0,) = call(
+        prepare_kernel, (shape(8, 8, 128),), [pltpu.SemaphoreType.DMA((10,))],
+        WHOLE, "aa", "prepare", 1024, out_spaces="h",
     )(desired, pt_cells)
     got0 = exchange(send0, FLD)
-    high, low, token = call(
+    high, low = call(
         eval_green_kernel,
-        (shape(256, 4096, dtype=bf16), shape(256, 4096, dtype=bf16), shape(8, 128)),
-        [], 8, "sv", "eval_green", 524288 * 40, 524288,
+        (shape(256, 4096, dtype=bf16), shape(256, 4096, dtype=bf16)),
+        [vmem((256, 4096), bf16), vmem((256, 4096), bf16), pltpu.SemaphoreType.DMA((2, 4))],
+        63, "sv", "eval_green", 524288 * 40, 524288, out_spaces="hh",
     )(wavenumber, eval_cells)
+    got0, high, low = lax.optimization_barrier((got0, high, low))
     g, send1 = call(
         first_kernel,
         (shape(8, 2, 512, 128), shape(8, 8, 128)),
         [vmem((8, 64, 128), f32), vmem((8, 8, 128), f32), vmem((2, 512, 128), f32)],
-        8, "svv", "first", 524288 * 48, 524288,
-    )(wavenumber, got0, token)
+        8, "sv", "first", 524288 * 48, 524288,
+    )(wavenumber, got0)
     got1 = exchange(send1, NEAR)
     send2, g0 = call(
         image_kernel,
@@ -410,14 +436,14 @@
     )(got4, got2, alpha)
     got5 = exchange(send5, NEAR)
     send6 = call(
-        drive_kernel, shape(8, 72, 128), [], 8, "vvvvvv", "drive", 81920,
+        drive_kernel, shape(8, ROWS, 128), [], 8, "vvvvvv", "drive", 81920,
     )(got5, got3, got2, got4, alpha, scalars)
     got6 = exchange(send6, FLD)
     return call(
         field_kernel,
         (shape(2, 8, 256), shape(2, 8, 256), shape(2, 8, 128)),
         [], 12, "vvvvv", "field", 524288 * 96,
-    )(got6, high, low, desired, spk_cells.reshape(32, 128))
+    )(got6.reshape(8 * ROWS, 128), high, low, desired, spk_cells.reshape(32, 128))
 
 
 def solution(mesh):

time: 112 us -> 112 us (level)
  Pallas kernels: 13.2 us -> 15.2 us
  local copies, waits for them, and re-layouts: 2.01 us -> 0.01 us
    unnamed x10 -> x8, local copies, waits for them, and re-layouts: 2.01 us -> 0.01 us
    pallas_call x1, Pallas kernels: 3.03 us -> 4.79 us  [local(): call(eval_green_kernel, (shape(256, 4096, dtype=bf16), shape(256, 4096, d...]
  transfers between devices with their start and end apart: 1 -> 1, of which waited for: 1 -> 1; matrix products, arithmetic and copies ran while one was open for 0% -> 0% of each run, Pallas kernels for 3% -> 4%
where the time goes in v2:
time: 112 us; the launch traced here: 110 us
  blocking collectives  71.5 us (64%)
  starting transfers between devices  15.6 us (14%)
  Pallas kernels  15.2 us (14%)
  waiting for transfers between devices  6.32 us (6%)
  between operations  1.35 us (1%)
    all_to_all x6, blocking collectives, exchange(): return lax.all_to_all(array, axes, split_axis=0, concat_axis=0, tiled=True)  71.5 us
    all_to_all x1, starting transfers between devices, exchange(): return lax.all_to_all(array, axes, split_axis=0, concat_axis=0, tiled=True)  15.6 us
    all_to_all x1, waiting for transfers between devices, exchange(): return lax.all_to_all(array, axes, split_axis=0, concat_axis=0, tiled=True)  6.32 us
    pallas_call x1, Pallas kernels, local(): call(eval_green_kernel, (shape(256, 4096, dtype=bf16), shape(256, 4096, d...  4.79 us
    pallas_call x1, Pallas kernels, local(): call(first_kernel, (shape(8, 2, 512, 128), shape(8, 8, 128)), [vmem((8, 6...  3.29 us
  transfers between devices with their start and end apart: 1, of which 1 were waited for; matrix products, arithmetic and copies ran while one was open for 0% of the time, Pallas kernels for 4%

profile of v2, /device:TPU:1, one launch (start us, length us, event | category | flops | bytes accessed | tf_op | source)
XLA Modules:
  0.0 110.1 jit_solution(16755737209253712575)
XLA Ops:
  0.6 1.8 %prepare.1 = f32[8,8,128]{2,1,0:T(8,128)} custom-call(f32[2,8,256]{2,1,0:T(8,128)} %desired_ref.1, f32[3,256]{1,0:T(4,128)} %points_hbm.1), custom_call_target="tpu_custom_call" | custom-call | flops 1024 | bytes 1048576 | tf_op jit(solution)/shard_map/prepare/pallas_call | solution.py:399
  2.5 15.6 %all-to-all-start = ((f32[8,8,128]{2,1,0:T(8,128)}), f32[8,8,128]{2,1,0:T(8,128)S(1)}, u32[]{:S(2)}, u32[]{:S(2)}) async-start(f32[8,8,128]{2,1,0:T(8,128)} %prepare.1), calls=%async_computation | async-start | bytes 65536 | tf_op jit(solution)/shard_map/all_to_all | solution.py:395
  18.8 4.8 %eval_green.1 = (bf16[256,4096]{1,0:T(8,128)(2,1)}, bf16[256,4096]{1,0:T(8,128)(2,1)}) custom-call(f32[1]{0:T(128)S(6)} %copy.8.wave_ref, f32[3,128]{1,0:T(4,128)} %eval_ref.1), custom_call_target="tpu_custom_call" | custom-call | flops 20971520 | bytes 1048576 | tf_op jit(solution)/shard_map/eval_green/pallas_call | solution.py:404
  23.5 6.3 %all-to-all-done.got_ref = f32[8,8,128]{2,1,0:T(8,128)S(1)} async-done(((f32[8,8,128]{2,1,0:T(8,128)}), f32[8,8,128]{2,1,0:T(8,128)S(1)}, u32[]{:S(2)}, u32[]{:S(2)}) %all-to-all-start) | async-done | bytes 32800 | tf_op jit(solution)/shard_map/all_to_all | solution.py:395
  29.9 3.3 %first.1 = (f32[8,2,512,128]{3,2,1,0:T(8,128)S(1)}, f32[8,8,128]{2,1,0:T(8,128)S(1)}) custom-call(f32[1]{0:T(128)S(6)} %copy.8.wave_ref, f32[8,8,128]{2,1,0:T(8,128)S(1)} %all-to-all-done.got_ref), custom_call_target="tpu_custom_call" | custom-call | flops 25165824 | bytes 1048576 | tf_op jit(solution)/shard_map/first/pallas_call | solution.py:411
  33.2 9.6 %all_to_all.35.got_ref = f32[8,8,128]{2,1,0:T(8,128)S(1)} all-to-all(f32[8,8,128]{2,1,0:T(8,128)S(1)} %get-tuple-element.20), channel_id=1, replica_groups=mesh['ylo'=2,'x'=4,'core'=2,'yhi'=2,'za'=4,'zb'=2,'zc'=2] {'ylo','yhi','..., dimensions={0} | all-to-all | bytes 65536 | tf_op jit(solution)/shard_map/all_to_all | solution.py:395
  42.8 1.0 image.1
  43.7 12.6 %all_to_all.36.got_ref.got2_ref = f32[8,24,128]{2,1,0:T(8,128)S(1)} all-to-all(f32[8,24,128]{2,1,0:T(8,128)S(1)} %get-tuple-element.21), channel_id=1, replica_groups=mesh['ylo'=2,'x'=4,'core'=2,'yhi'=2,'za'=4,'zb'=2,'zc'=2] {'x','core'}, dimensions={0} | all-to-all | bytes 196608 | tf_op jit(solution)/shard_map/all_to_all | solution.py:395
  56.3 0.9 adjoint.1
  57.3 8.0 %all_to_all.37.got3_ref = f32[8,32,128]{2,1,0:T(8,128)S(1)} all-to-all(f32[8,32,128]{2,1,0:T(8,128)S(1)} %adjoint.1), channel_id=1, replica_groups=mesh['ylo'=2,'x'=4,'core'=2,'yhi'=2,'za'=4,'zb'=2,'zc'=2] {'ylo','yhi','..., dimensions={0} | all-to-all | bytes 262144 | tf_op jit(solution)/shard_map/all_to_all | solution.py:395
  65.3 0.0 copy-start
  65.3 0.0 copy-start.1
  65.3 0.0 copy-start.2
  65.3 0.0 copy-start.3
  65.3 1.1 second_image.1
  66.4 9.4 %all_to_all.38.got4_ref = f32[8,24,128]{2,1,0:T(8,128)S(1)} all-to-all(f32[8,24,128]{2,1,0:T(8,128)S(1)} %get-tuple-element.23), channel_id=1, replica_groups=mesh['ylo'=2,'x'=4,'core'=2,'yhi'=2,'za'=4,'zb'=2,'zc'=2] {'x','core'}, dimensions={0} | all-to-all | bytes 196608 | tf_op jit(solution)/shard_map/all_to_all | solution.py:395
  75.8 0.2 norm.1
  76.1 7.9 %all_to_all.39.got5_ref = f32[8,24,128]{2,1,0:T(8,128)S(1)} all-to-all(f32[8,24,128]{2,1,0:T(8,128)S(1)} %get-tuple-element.25), channel_id=1, replica_groups=mesh['ylo'=2,'x'=4,'core'=2,'yhi'=2,'za'=4,'zb'=2,'zc'=2] {'ylo','yhi','..., dimensions={0} | all-to-all | bytes 196608 | tf_op jit(solution)/shard_map/all_to_all | solution.py:395
  84.0 24.0 %all_to_all.40 = f32[8,72,128]{2,1,0:T(8,128)S(1)} all-to-all(f32[8,72,128]{2,1,0:T(8,128)S(1)} %drive.1), channel_id=1, replica_groups=mesh['ylo'=2,'x'=4,'core'=2,'yhi'=2,'za'=4,'zb'=2,'zc'=2] {'za','zb'}, dimensions={0} | all-to-all | bytes 589824 | tf_op jit(solution)/shard_map/all_to_all | solution.py:395
  108.0 0.0 copy-done
  108.0 0.0 copy-done.1
  108.0 0.0 copy-done.2
  108.0 0.0 copy-done.3
  108.0 2.1 %field.1 = (f32[2,8,256]{2,1,0:T(8,128)}, f32[2,8,256]{2,1,0:T(8,128)}, f32[2,8,128]{2,1,0:T(8,128)}) custom-call(f32[576,128]{1,0:T(8,128)S(1)} %bitcast.2, bf16[256,4096]{1,0:T(8,128)(2,1)S(1)} %copy-done, bf16[256,4096]{1,0:T(8,128)(2,1)S(1)} %copy-done.1, f32[2,8,256]{2,1,0:T(8,128)S(1)} %copy-done.2, s32[32,128]{1,0:T(8,128)S(1)} %bitcast.3), custom_call_target="tpu_custom_call" | custom-call | flops 50331648 | bytes 1048576 | tf_op jit(solution)/shard_map/field/pallas_call | solution.py:442
  (1 shorter events, 0.0 us)
Async XLA Ops:
  2.5 27.4 %all-to-all-start = ((f32[8,8,128]{2,1,0:T(8,128)}), f32[8,8,128]{2,1,0:T(8,128)S(1)}, u32[]{:S(2)}, u32[]{:S(2)}) async-start(f32[8,8,128]{2,1,0:T(8,128)} %prepare.1), calls=%async_computation | async-start | bytes 65536 | tf_op jit(solution)/shard_map/all_to_all | solution.py:395
  65.3 42.7 %copy-start = (bf16[256,4096]{1,0:T(8,128)(2,1)S(1)}, bf16[256,4096]{1,0:T(8,128)(2,1)}, u32[]{:S(2)}) copy-start(bf16[256,4096]{1,0:T(8,128)(2,1)} %get-tuple-element.27.high_ref) | copy-start | bytes 6291460
  65.3 42.7 %copy-start.1 = (bf16[256,4096]{1,0:T(8,128)(2,1)S(1)}, bf16[256,4096]{1,0:T(8,128)(2,1)}, u32[]{:S(2)}) copy-start(bf16[256,4096]{1,0:T(8,128)(2,1)} %get-tuple-element.28.low_ref) | copy-start | bytes 6291460
  65.3 42.7 %copy-start.2 = (f32[2,8,256]{2,1,0:T(8,128)S(1)}, f32[2,8,256]{2,1,0:T(8,128)}, u32[]{:S(2)}) copy-start(f32[2,8,256]{2,1,0:T(8,128)} %desired_ref.1) | copy-start | bytes 49156
  65.3 42.7 %copy-start.3 = (s32[4096]{0:T(1024)S(1)}, s32[4096]{0:T(1024)}, u32[]{:S(2)}) copy-start(s32[4096]{0:T(1024)} %param.6) | copy-start | bytes 49156

commit v3 on v2

--- a/solution.py
+++ b/solution.py
@@ -25,8 +25,10 @@
 SIN = (4.442879676818848, -7.307816505432129, 3.5977742671966553, -0.7911993861198425)
 COS = (-1.4142040014266968, 6.97763729095459, -5.715188026428223, 1.728213906288147)
 ROUNDER = 12582912.0
+LOW_SCALE = 4194304.0
 
 f32 = jnp.float32
+f8 = jnp.float8_e4m3fn
 bf16 = jnp.bfloat16
 vmem = pltpu.VMEM
 
@@ -52,7 +54,7 @@
         if out_spaces
         else jax.tree.map(lambda _: spec(), out_shapes),
         scratch_shapes=scratch,
-        compiler_params=pltpu.CompilerParams(vmem_limit_bytes=min(limit_mib << 20, 67043328)),
+        compiler_params=pltpu.CompilerParams(vmem_limit_bytes=min(int(limit_mib * (1 << 20)), 67043328)),
         cost_estimate=pl.CostEstimate(flops=flops, bytes_accessed=1 << 20, transcendentals=trans),
         name=name,
     )
@@ -102,26 +104,24 @@
     return lax.broadcasted_iota(jnp.int32, dims, dim)
 
 
-def prepare_kernel(desired_hbm, points_hbm, send_hbm, sems):
-    lanes = pl.ds(pl.multiple_of(lax.axis_index("ylo") * 128, 128), 128)
-    copies = []
-    for part in range(2):
-        copies.append(
-            pltpu.make_async_copy(
-                desired_hbm.at[part, :, lanes], send_hbm.at[:, part, :], sems.at[part]
-            )
-        )
-    for f in range(8):
-        copies.append(
-            pltpu.make_async_copy(points_hbm.at[:, lanes], send_hbm.at[f, 2:5, :], sems.at[2 + f])
-        )
+def prepare_kernel(desired_hbm, points_hbm, send_ref, desired_ref, points_ref, sems):
+    copies = [
+        pltpu.make_async_copy(desired_hbm, desired_ref, sems.at[0]),
+        pltpu.make_async_copy(points_hbm, points_ref, sems.at[1]),
+    ]
     for copy in copies:
         copy.start()
+    lanes = pl.ds(pl.multiple_of(lax.axis_index("ylo") * 128, 128), 128)
     for copy in copies:
         copy.wait()
-
-
-def eval_green_kernel(wave_ref, eval_ref, high_hbm, low_hbm, high_ref, low_ref, sems):
+    points = points_ref[:, lanes]
+    for f in range(8):
+        send_ref[f, 0:1, :] = desired_ref[0, f : f + 1, lanes]
+        send_ref[f, 1:2, :] = desired_ref[1, f : f + 1, lanes]
+        send_ref[f, 2:5, :] = points
+
+
+def eval_green_kernel(wave_ref, eval_ref, high_ref, low_ref):
     kappa = wave_ref[0] * (0.5 / math.pi)
     strength = kappa * (1.0 / WALL)
     ex = column((front_gap + eval_ref[0:1, :] * depth_span) * kappa)
@@ -139,25 +139,13 @@
             rows = slice(start, start + 64)
             dy = ey[rows] - wy
             real, imag = green(base[rows] + dy * dy, strength)
-            rh, rl = split_bf16(real)
-            ih, il = split_bf16(imag)
-            high_ref[start : start + 64, lanes] = rh
-            low_ref[start : start + 64, lanes] = rl
-            high_ref[128 + start : 192 + start, lanes] = ih
-            low_ref[128 + start : 192 + start, lanes] = il
+            for first, value in ((start, real), (128 + start, imag)):
+                high = value.astype(bf16)
+                high_ref[first : first + 64, lanes] = high
+                low_ref[first : first + 64, lanes] = ((value - high.astype(f32)) * LOW_SCALE).astype(f8)
         return carry
 
-    copies = []
-    for quarter in range(4):
-        lax.fori_loop(quarter * 8, quarter * 8 + 8, step, 0)
-        lanes = slice(quarter * 1024, quarter * 1024 + 1024)
-        for k, (ref, hbm) in enumerate(((high_ref, high_hbm), (low_ref, low_hbm))):
-            copies.append(
-                pltpu.make_async_copy(ref.at[:, lanes], hbm.at[:, lanes], sems.at[k, quarter])
-            )
-            copies[-1].start()
-    for copy in copies:
-        copy.wait()
+    lax.fori_loop(0, 32, step, 0)
 
 
 def first_kernel(wave_ref, got_ref, g_ref, send_ref, dz2_ref, rest_ref, acc_ref):
@@ -343,7 +331,9 @@
     return got_ref[pl.ds(row, 8, stride=ROWS), :]
 
 
-def field_kernel(got_ref, high_ref, low_ref, desired_ref, cells_ref, drives_ref, residual_ref, field_ref):
+def field_kernel(
+    got_ref, high_ref, low_ref, desired_ref, cells_ref, drives_ref, residual_ref, field_ref
+):
     for part in range(2):
         for half in range(2):
             lanes = slice(half * 128, half * 128 + 128)
@@ -385,8 +375,9 @@
             at = (u * 2 + pair) * 256
             lanes = slice(at, at + 256)
             out = out + lax.dot_general(both, high_ref[:, lanes], dims, preferred_element_type=f32)
-            fine = fine + lax.dot_general(high, low_ref[:, lanes], dims, preferred_element_type=f32)
-    out = out[0:16, :] + out[16:32, :] + fine
+            rest = low_ref[:, lanes].astype(bf16)
+            fine = fine + lax.dot_general(high, rest, dims, preferred_element_type=f32)
+    out = out[0:16, :] + out[16:32, :] + fine * (1.0 / LOW_SCALE)
     field_ref[0] = out[0:8, 0:128] - out[8:16, 128:256]
     field_ref[1] = out[0:8, 128:256] + out[8:16, 0:128]
 
@@ -396,18 +387,13 @@
 
 
 def local(desired, spk_cells, pt_cells, eval_cells, wavenumber):
-    (send0,) = call(
-        prepare_kernel, (shape(8, 8, 128),), [pltpu.SemaphoreType.DMA((10,))],
-        WHOLE, "aa", "prepare", 1024, out_spaces="h",
+    send0 = call(
+        prepare_kernel,
+        shape(8, 8, 128),
+        [vmem((2, 8, 256), f32), vmem((3, 256), f32), pltpu.SemaphoreType.DMA((2,))],
+        WHOLE, "aa", "prepare", 1024,
     )(desired, pt_cells)
     got0 = exchange(send0, FLD)
-    high, low = call(
-        eval_green_kernel,
-        (shape(256, 4096, dtype=bf16), shape(256, 4096, dtype=bf16)),
-        [vmem((256, 4096), bf16), vmem((256, 4096), bf16), pltpu.SemaphoreType.DMA((2, 4))],
-        63, "sv", "eval_green", 524288 * 40, 524288, out_spaces="hh",
-    )(wavenumber, eval_cells)
-    got0, high, low = lax.optimization_barrier((got0, high, low))
     g, send1 = call(
         first_kernel,
         (shape(8, 2, 512, 128), shape(8, 8, 128)),
@@ -439,6 +425,12 @@
         drive_kernel, shape(8, ROWS, 128), [], 8, "vvvvvv", "drive", 81920,
     )(got5, got3, got2, got4, alpha, scalars)
     got6 = exchange(send6, FLD)
+    eval_cells, got5 = lax.optimization_barrier((eval_cells, got5))
+    high, low = call(
+        eval_green_kernel,
+        (shape(256, 4096, dtype=bf16), shape(256, 4096, dtype=f8)),
+        [], 8, "sv", "eval_green", 524288 * 40, 524288,
+    )(wavenumber, eval_cells)
     return call(
         field_kernel,
         (shape(2, 8, 256), shape(2, 8, 256), shape(2, 8, 128)),

time: 112 us -> 111 us (level)
  blocking collectives: 71.5 us -> 47.5 us
  waiting for transfers between devices: 6.32 us -> 27.7 us
  starting transfers between devices: 15.6 us -> 19.1 us
  Pallas kernels: 15.2 us -> 13.7 us
    all_to_all x6 -> x5, blocking collectives: 71.5 us -> 47.5 us  [exchange(): return lax.all_to_all(array, axes, split_axis=0, concat_axis=0, tiled=True)]
    all_to_all x1 -> x2, waiting for transfers between devices: 6.32 us -> 27.7 us  [exchange(): return lax.all_to_all(array, axes, split_axis=0, concat_axis=0, tiled=True)]
    all_to_all x1 -> x2, starting transfers between devices: 15.6 us -> 19.1 us  [exchange(): return lax.all_to_all(array, axes, split_axis=0, concat_axis=0, tiled=True)]
    pallas_call x1, Pallas kernels: 4.79 us -> 3.04 us  [local(): call(eval_green_kernel, (shape(256, 4096, dtype=bf16), shape(256, 4096, d...]
  transfers between devices with their start and end apart: 1 -> 2, of which waited for: 1 -> 2; matrix products, arithmetic and copies ran while one was open for 0% -> 0% of each run, Pallas kernels for 4% -> 3%
where the time goes in v3:
time: 111 us; the launch traced here: 109 us
  blocking collectives  47.5 us (43%)
  waiting for transfers between devices  27.7 us (25%)
  starting transfers between devices  19.1 us (17%)
  Pallas kernels  13.7 us (12%)
  between operations  1.37 us (1%)
    all_to_all x5, blocking collectives, exchange(): return lax.all_to_all(array, axes, split_axis=0, concat_axis=0, tiled=True)  47.5 us
    all_to_all x2, waiting for transfers between devices, exchange(): return lax.all_to_all(array, axes, split_axis=0, concat_axis=0, tiled=True)  27.7 us
    all_to_all x2, starting transfers between devices, exchange(): return lax.all_to_all(array, axes, split_axis=0, concat_axis=0, tiled=True)  19.1 us
    pallas_call x1, Pallas kernels, local(): call(first_kernel, (shape(8, 2, 512, 128), shape(8, 8, 128)), [vmem((8, 6...  3.29 us
    pallas_call x1, Pallas kernels, local(): call(eval_green_kernel, (shape(256, 4096, dtype=bf16), shape(256, 4096, d...  3.04 us
  transfers between devices with their start and end apart: 2, of which 2 were waited for; matrix products, arithmetic and copies ran while one was open for 0% of the time, Pallas kernels for 3%

profile of v3, /device:TPU:1, one launch (start us, length us, event | category | flops | bytes accessed | tf_op | source)
XLA Modules:
  0.0 109.4 jit_solution(18161052084527715033)
XLA Ops:
  0.6 1.3 %prepare.1 = f32[8,8,128]{2,1,0:T(8,128)} custom-call(f32[2,8,256]{2,1,0:T(8,128)} %desired_ref.1, f32[3,256]{1,0:T(4,128)} %points_hbm.1), custom_call_target="tpu_custom_call" | custom-call | flops 1024 | bytes 1048576 | tf_op jit(solution)/shard_map/prepare/pallas_call | solution.py:390
  2.0 15.6 %all-to-all-start = ((f32[8,8,128]{2,1,0:T(8,128)}), f32[8,8,128]{2,1,0:T(8,128)S(1)}, u32[]{:S(2)}, u32[]{:S(2)}) async-start(f32[8,8,128]{2,1,0:T(8,128)} %prepare.1), calls=%async_computation | async-start | bytes 65536 | tf_op jit(solution)/shard_map/all_to_all | solution.py:386
  18.3 11.1 %all-to-all-done.got_ref = f32[8,8,128]{2,1,0:T(8,128)S(1)} async-done(((f32[8,8,128]{2,1,0:T(8,128)}), f32[8,8,128]{2,1,0:T(8,128)S(1)}, u32[]{:S(2)}, u32[]{:S(2)}) %all-to-all-start) | async-done | bytes 32800 | tf_op jit(solution)/shard_map/all_to_all | solution.py:386
  29.4 3.3 %first.1 = (f32[8,2,512,128]{3,2,1,0:T(8,128)S(1)}, f32[8,8,128]{2,1,0:T(8,128)S(1)}) custom-call(f32[1]{0:T(128)S(6)} %copy.8.wave_ref, f32[8,8,128]{2,1,0:T(8,128)S(1)} %all-to-all-done.got_ref), custom_call_target="tpu_custom_call" | custom-call | flops 25165824 | bytes 1048576 | tf_op jit(solution)/shard_map/first/pallas_call | solution.py:397
  32.7 9.6 %all_to_all.35.got_ref = f32[8,8,128]{2,1,0:T(8,128)S(1)} all-to-all(f32[8,8,128]{2,1,0:T(8,128)S(1)} %get-tuple-element.15), channel_id=1, replica_groups=mesh['ylo'=2,'x'=4,'core'=2,'yhi'=2,'za'=4,'zb'=2,'zc'=2] {'ylo','yhi','..., dimensions={0} | all-to-all | bytes 65536 | tf_op jit(solution)/shard_map/all_to_all | solution.py:386
  42.3 1.0 image.1
  43.3 12.6 %all_to_all.36.got_ref.got2_ref = f32[8,24,128]{2,1,0:T(8,128)S(1)} all-to-all(f32[8,24,128]{2,1,0:T(8,128)S(1)} %get-tuple-element.16), channel_id=1, replica_groups=mesh['ylo'=2,'x'=4,'core'=2,'yhi'=2,'za'=4,'zb'=2,'zc'=2] {'x','core'}, dimensions={0} | all-to-all | bytes 196608 | tf_op jit(solution)/shard_map/all_to_all | solution.py:386
  55.9 0.9 adjoint.1
  56.8 0.0 copy-start.2
  56.8 0.0 copy-start
  56.8 0.0 copy-start.1
  56.8 8.2 %all_to_all.37.got3_ref = f32[8,32,128]{2,1,0:T(8,128)S(1)} all-to-all(f32[8,32,128]{2,1,0:T(8,128)S(1)} %adjoint.1), channel_id=1, replica_groups=mesh['ylo'=2,'x'=4,'core'=2,'yhi'=2,'za'=4,'zb'=2,'zc'=2] {'ylo','yhi','..., dimensions={0} | all-to-all | bytes 262144 | tf_op jit(solution)/shard_map/all_to_all | solution.py:386
  65.0 1.1 %second_image.1 = (f32[8,24,128]{2,1,0:T(8,128)S(1)}, f32[2,128]{1,0:T(2,128)S(1)}) custom-call(f32[8,2,512,128]{3,2,1,0:T(8,128)S(1)} %get-tuple-element.14.g_ref, f32[8,32,128]{2,1,0:T(8,128)S(1)} %all_to_all.37.got3_ref, f32[8,24,128]{2,1,0:T(8,128)S(1)} %all_to_all.36.got_ref.got2_ref, f32[8,128]{1,0:T(8,128)S(1)} %get-tuple-element.17.g0_ref), custom_call_target="tpu_custom_call" | custom-call | flops 4194304 | bytes 1048576 | tf_op jit(solution)/shard_map/second_image/pallas_call | solution.py:414
  66.1 9.3 %all_to_all.38.got4_ref = f32[8,24,128]{2,1,0:T(8,128)S(1)} all-to-all(f32[8,24,128]{2,1,0:T(8,128)S(1)} %get-tuple-element.18), channel_id=1, replica_groups=mesh['ylo'=2,'x'=4,'core'=2,'yhi'=2,'za'=4,'zb'=2,'zc'=2] {'x','core'}, dimensions={0} | all-to-all | bytes 196608 | tf_op jit(solution)/shard_map/all_to_all | solution.py:386
  75.4 0.2 norm.1
  75.6 7.9 %all_to_all.39.got5_ref = f32[8,24,128]{2,1,0:T(8,128)S(1)} all-to-all(f32[8,24,128]{2,1,0:T(8,128)S(1)} %get-tuple-element.20), channel_id=1, replica_groups=mesh['ylo'=2,'x'=4,'core'=2,'yhi'=2,'za'=4,'zb'=2,'zc'=2] {'ylo','yhi','..., dimensions={0} | all-to-all | bytes 196608 | tf_op jit(solution)/shard_map/all_to_all | solution.py:386
  83.5 0.7 drive.1
  84.3 3.4 %all-to-all-start.6 = ((f32[8,72,128]{2,1,0:T(8,128)}), f32[8,72,128]{2,1,0:T(8,128)S(1)}, u32[]{:S(2)}, u32[]{:S(2)}) async-start(f32[8,72,128]{2,1,0:T(8,128)} %drive.1), calls=%async_computation.6 | async-start | bytes 589824 | tf_op jit(solution)/shard_map/all_to_all | solution.py:386
  87.7 0.0 copy-done.2
  87.7 3.0 %eval_green.1 = (bf16[256,4096]{1,0:T(8,128)(2,1)S(1)}, f8e4m3fn[256,4096]{1,0:T(32,128)(4,1)S(1)}) custom-call(f32[1]{0:T(128)S(6)} %copy.8.wave_ref, f32[3,128]{1,0:T(4,128)S(1)} %copy-done.2), custom_call_target="tpu_custom_call" | custom-call | flops 20971520 | bytes 1048576 | tf_op jit(solution)/shard_map/eval_green/pallas_call | solution.py:429
  90.7 16.6 %all-to-all-done.6 = f32[8,72,128]{2,1,0:T(8,128)S(1)} async-done(((f32[8,72,128]{2,1,0:T(8,128)}), f32[8,72,128]{2,1,0:T(8,128)S(1)}, u32[]{:S(2)}, u32[]{:S(2)}) %all-to-all-start.6) | async-done | bytes 294944 | tf_op jit(solution)/shard_map/all_to_all | solution.py:386
  107.4 0.0 copy-done
  107.4 0.0 copy-done.1
  107.4 2.0 %field.1 = (f32[2,8,256]{2,1,0:T(8,128)}, f32[2,8,256]{2,1,0:T(8,128)}, f32[2,8,128]{2,1,0:T(8,128)}) custom-call(f32[576,128]{1,0:T(8,128)S(1)} %bitcast.2, bf16[256,4096]{1,0:T(8,128)(2,1)S(1)} %get-tuple-element.23.high_ref, f8e4m3fn[256,4096]{1,0:T(32,128)(4,1)S(1)} %get-tuple-element.24.low_ref, f32[2,8,256]{2,1,0:T(8,128)S(1)} %copy-done, ...), custom_call_target="tpu_custom_call" | custom-call | flops 50331648 | bytes 1048576 | tf_op jit(solution)/shard_map/field/pallas_call | solution.py:434
Async XLA Ops:
  2.0 27.4 %all-to-all-start = ((f32[8,8,128]{2,1,0:T(8,128)}), f32[8,8,128]{2,1,0:T(8,128)S(1)}, u32[]{:S(2)}, u32[]{:S(2)}) async-start(f32[8,8,128]{2,1,0:T(8,128)} %prepare.1), calls=%async_computation | async-start | bytes 65536 | tf_op jit(solution)/shard_map/all_to_all | solution.py:386
  56.8 30.9 %copy-start.2 = (f32[3,128]{1,0:T(4,128)S(1)}, f32[3,128]{1,0:T(4,128)}, u32[]{:S(2)}) copy-start(f32[3,128]{1,0:T(4,128)} %eval_ref) | copy-start | bytes 4612
  56.8 50.6 %copy-start = (f32[2,8,256]{2,1,0:T(8,128)S(1)}, f32[2,8,256]{2,1,0:T(8,128)}, u32[]{:S(2)}) copy-start(f32[2,8,256]{2,1,0:T(8,128)} %desired_ref.1) | copy-start | bytes 49156
  56.8 50.5 %copy-start.1 = (s32[4096]{0:T(1024)S(1)}, s32[4096]{0:T(1024)}, u32[]{:S(2)}) copy-start(s32[4096]{0:T(1024)} %param.6) | copy-start | bytes 49156
  84.3 23.1 %all-to-all-start.6 = ((f32[8,72,128]{2,1,0:T(8,128)}), f32[8,72,128]{2,1,0:T(8,128)S(1)}, u32[]{:S(2)}, u32[]{:S(2)}) async-start(f32[8,72,128]{2,1,0:T(8,128)} %drive.1), calls=%async_computation.6 | async-start | bytes 589824 | tf_op jit(solution)/shard_map/all_to_all | solution.py:386

commit v4 on v3

--- a/solution.py
+++ b/solution.py
@@ -312,72 +312,89 @@
     norm = fold(got5_ref[:, 16:17, :])
     alpha1 = scalar_ref[1:2, :] / (norm + tikhonov * scalar_ref[2:3, :])
     from_first = alpha0 + alpha1 * beta
-    for u in range(8):
-        rows = from_first * got2_ref[u, 16:24, :] + alpha1 * got4_ref[u, 16:24, :]
+    core = lax.axis_index("core")
+    for k in range(4):
+        bank = core * 4 + k
+        rows = from_first * got2_ref[bank, 16:24, :] + alpha1 * got4_ref[bank, 16:24, :]
         for i in range(8):
-            send_ref[i, 8 * u : 8 * u + 8, :] = rows
+            send_ref[i, 8 * k : 8 * k + 8, :] = rows
     for half in range(2):
         member = half * 4 + lax.axis_index(("yhi", "zc"))
         change = alpha0 * got3_ref[member, 8:24, :] + alpha1 * got5_ref[member, 0:16, :]
         for i in range(8):
-            send_ref[i, 64 + half : 65 + half, :] = change[i : i + 1, :]
-            send_ref[i, 66 + half : 67 + half, :] = change[8 + i : 9 + i, :]
-
-
-ROWS = 72
+            send_ref[i, 32 + half : 33 + half, :] = change[i : i + 1, :]
+            send_ref[i, 34 + half : 35 + half, :] = change[8 + i : 9 + i, :]
+
+
+ROWS = 40
 
 
 def of_fields(got_ref, row):
     return got_ref[pl.ds(row, 8, stride=ROWS), :]
 
 
-def field_kernel(
-    got_ref, high_ref, low_ref, desired_ref, cells_ref, drives_ref, residual_ref, field_ref
+def field_part(got_ref, half, high_ref, low_ref, cells_ref):
+    first_cell = lax.axis_index(SPK) * 2
+    cells = jnp.concatenate([cells_ref[pl.ds(first_cell + blk, 1), :] for blk in range(2)], axis=1)
+    pick = jnp.where(iota((128, 256), 0) == jnp.bitwise_and(cells, 127), 1.0, 0.0).astype(bf16)
+    line = iota((32, 256), 0)
+    place = half * 16 + jnp.right_shift(line, 3) * 4 + jnp.bitwise_and(line, 3)
+    right = place == jnp.right_shift(cells, 7)
+    is_real = jnp.bitwise_and(line, 4) == 0
+    masks = [jnp.where(right & is_real, 1.0, 0.0), jnp.where(right & ~is_real, 1.0, 0.0)]
+    drives = [[], []]
+    for f in range(8):
+        x = got_ref[f * ROWS : f * ROWS + 32, :]
+        high = x.astype(bf16)
+        middle, low = split_bf16(x - high.astype(f32))
+        three = jnp.concatenate([high, middle, low], axis=0)
+        picked = jnp.dot(three, pick, preferred_element_type=f32)
+        picked = picked[0:32] + picked[32:64] + picked[64:96]
+        for part in range(2):
+            drives[part].append(jnp.sum(picked * masks[part], axis=0, keepdims=True))
+    out = jnp.zeros((32, 256), f32)
+    fine = jnp.zeros((16, 256), f32)
+    dims = (((1,), (1,)), ((), ()))
+    for k in range(4):
+        for pair in range(2):
+            parts = [
+                jnp.concatenate(
+                    [of_fields(got_ref, k * 8 + part * 4 + pair * 2 + i) for i in range(2)], axis=1
+                )
+                for part in range(2)
+            ]
+            high, low = split_bf16(jnp.concatenate(parts, axis=0))
+            both = jnp.concatenate([high, low], axis=0)
+            lanes = pl.ds(pl.multiple_of(half * 2048 + (k * 2 + pair) * 256, 256), 256)
+            out = out + lax.dot_general(both, high_ref[:, lanes], dims, preferred_element_type=f32)
+            rest = low_ref[:, lanes].astype(bf16)
+            fine = fine + lax.dot_general(high, rest, dims, preferred_element_type=f32)
+    out = out[0:16, :] + out[16:32, :] + fine * (1.0 / LOW_SCALE)
+    return [jnp.concatenate(rows, axis=0) for rows in drives], out
+
+
+def near_field_kernel(
+    got_ref, high_ref, low_ref, desired_ref, cells_ref, residual_ref, drives_ref, product_ref
 ):
     for part in range(2):
         for half in range(2):
             lanes = slice(half * 128, half * 128 + 128)
             residual_ref[part, :, lanes] = desired_ref[part, :, lanes] - of_fields(
-                got_ref, 64 + part * 2 + half
+                got_ref, 32 + part * 2 + half
             )
-    first_cell = lax.axis_index(SPK) * 2
-    cells = jnp.concatenate([cells_ref[pl.ds(first_cell + blk, 1), :] for blk in range(2)], axis=1)
-    pick = jnp.where(iota((128, 256), 0) == jnp.bitwise_and(cells, 127), 1.0, 0.0).astype(bf16)
-    line = iota((64, 256), 0)
-    place = jnp.right_shift(line, 3) * 4 + jnp.bitwise_and(line, 3)
-    right = place == jnp.right_shift(cells, 7)
-    is_real = jnp.bitwise_and(line, 4) == 0
-    real_mask = jnp.where(right & is_real, 1.0, 0.0)
-    imag_mask = jnp.where(right & ~is_real, 1.0, 0.0)
-    for f in range(8):
-        x = got_ref[f * ROWS : f * ROWS + 64, :]
-        high = x.astype(bf16)
-        left = x - high.astype(f32)
-        middle, low = split_bf16(left)
-        three = jnp.concatenate([high, middle, low], axis=0)
-        picked = jnp.dot(three, pick, preferred_element_type=f32)
-        picked = picked[0:64] + picked[64:128] + picked[128:192]
-        drives_ref[0, f : f + 1, :] = jnp.sum(picked * real_mask, axis=0, keepdims=True)
-        drives_ref[1, f : f + 1, :] = jnp.sum(picked * imag_mask, axis=0, keepdims=True)
-    out = jnp.zeros((32, 256), f32)
-    fine = jnp.zeros((16, 256), f32)
-    dims = (((1,), (1,)), ((), ()))
-    for u in range(8):
-        for pair in range(2):
-            parts = [
-                jnp.concatenate(
-                    [of_fields(got_ref, u * 8 + part * 4 + pair * 2 + k) for k in range(2)], axis=1
-                )
-                for part in range(2)
-            ]
-            high, low = split_bf16(jnp.concatenate(parts, axis=0))
-            both = jnp.concatenate([high, low], axis=0)
-            at = (u * 2 + pair) * 256
-            lanes = slice(at, at + 256)
-            out = out + lax.dot_general(both, high_ref[:, lanes], dims, preferred_element_type=f32)
-            rest = low_ref[:, lanes].astype(bf16)
-            fine = fine + lax.dot_general(high, rest, dims, preferred_element_type=f32)
-    out = out[0:16, :] + out[16:32, :] + fine * (1.0 / LOW_SCALE)
+    drives, out = field_part(got_ref, lax.axis_index("core"), high_ref, low_ref, cells_ref)
+    drives_ref[0] = drives[0]
+    drives_ref[1] = drives[1]
+    product_ref[...] = out
+
+
+def far_field_kernel(
+    got_ref, high_ref, low_ref, cells_ref, near_drives_ref, near_product_ref, drives_ref, field_ref
+):
+    drives, out = field_part(got_ref, 1 - lax.axis_index("core"), high_ref, low_ref, cells_ref)
+    drives_ref[0] = near_drives_ref[0] + drives[0]
+    drives_ref[1] = near_drives_ref[1] + drives[1]
+    out = near_product_ref[...] + out
     field_ref[0] = out[0:8, 0:128] - out[8:16, 128:256]
     field_ref[1] = out[0:8, 128:256] + out[8:16, 0:128]
 
@@ -431,11 +448,20 @@
         (shape(256, 4096, dtype=bf16), shape(256, 4096, dtype=f8)),
         [], 8, "sv", "eval_green", 524288 * 40, 524288,
     )(wavenumber, eval_cells)
-    return call(
-        field_kernel,
-        (shape(2, 8, 256), shape(2, 8, 256), shape(2, 8, 128)),
-        [], 12, "vvvvv", "field", 524288 * 96,
-    )(got6.reshape(8 * ROWS, 128), high, low, desired, spk_cells.reshape(32, 128))
+    got6, high, low = lax.optimization_barrier((got6.reshape(8 * ROWS, 128), high, low))
+    other = lax.ppermute(got6, "core", [(0, 1), (1, 0)])
+    cells = spk_cells.reshape(32, 128)
+    residual, near_drives, product = call(
+        near_field_kernel,
+        (shape(2, 8, 256), shape(2, 8, 256), shape(16, 256)),
+        [], 8, "vvvvv", "near_field", 524288 * 48,
+    )(got6, high, low, desired, cells)
+    drives, field = call(
+        far_field_kernel,
+        (shape(2, 8, 256), shape(2, 8, 128)),
+        [], 8, "vvvvvv", "far_field", 524288 * 48,
+    )(other, high, low, cells, near_drives, product)
+    return drives, residual, field
 
 
 def solution(mesh):

time: 111 us -> 110 us (level)
  waiting for transfers between devices: 27.7 us -> 21.3 us
  starting transfers between devices: 19.1 us -> 24.8 us
    all_to_all x2, waiting for transfers between devices: 27.7 us -> 21.3 us  [exchange(): return lax.all_to_all(array, axes, split_axis=0, concat_axis=0, tiled=True)]
    ppermute x0 -> x1, starting transfers between devices: none -> 5.81 us  [local(): other = lax.ppermute(got6, 'core', [(0, 1), (1, 0)])]
    pallas_call x1 -> x2, Pallas kernels: 2.02 us -> 2.7 us  [the longest x1 1.4 us: local(): call(far_field_kernel, (shape(2, 8, 256), shape(2, 8, 128)), [], 8, 'vvvv...]
  transfers between devices with their start and end apart: 2 -> 3, of which waited for: 2 -> 2; matrix products, arithmetic and copies ran while one was open for 0% -> 0% of each run, Pallas kernels for 3% -> 4%
where the time goes in v4:
time: 110 us; the launch traced here: 109 us
  blocking collectives  47.5 us (43%)
  starting transfers between devices  24.8 us (23%)
  waiting for transfers between devices  21.3 us (19%)
  Pallas kernels  14.3 us (13%)
  between operations  1.39 us (1%)
    all_to_all x5, blocking collectives, exchange(): return lax.all_to_all(array, axes, split_axis=0, concat_axis=0, tiled=True)  47.5 us
    all_to_all x2, waiting for transfers between devices, exchange(): return lax.all_to_all(array, axes, split_axis=0, concat_axis=0, tiled=True)  21.3 us
    all_to_all x2, starting transfers between devices, exchange(): return lax.all_to_all(array, axes, split_axis=0, concat_axis=0, tiled=True)  19 us
    ppermute x1, starting transfers between devices, local(): other = lax.ppermute(got6, 'core', [(0, 1), (1, 0)])  5.81 us
    pallas_call x1, Pallas kernels, local(): call(first_kernel, (shape(8, 2, 512, 128), shape(8, 8, 128)), [vmem((8, 6...  3.29 us
    pallas_call x1, Pallas kernels, local(): call(eval_green_kernel, (shape(256, 4096, dtype=bf16), shape(256, 4096, d...  3.04 us
  transfers between devices with their start and end apart: 3, of which 2 were waited for; matrix products, arithmetic and copies ran while one was open for 0% of the time, Pallas kernels for 4%

profile of v4, /device:TPU:1, one launch (start us, length us, event | category | flops | bytes accessed | tf_op | source)
XLA Modules:
  0.0 109.4 jit_solution(3197551998198895562)
XLA Ops:
  0.6 1.4 %prepare.1 = f32[8,8,128]{2,1,0:T(8,128)} custom-call(f32[2,8,256]{2,1,0:T(8,128)} %desired_ref.1, f32[3,256]{1,0:T(4,128)} %points_hbm.1), custom_call_target="tpu_custom_call" | custom-call | flops 1024 | bytes 1048576 | tf_op jit(solution)/shard_map/prepare/pallas_call | solution.py:407
  2.0 15.6 %all-to-all-start = ((f32[8,8,128]{2,1,0:T(8,128)}), f32[8,8,128]{2,1,0:T(8,128)S(1)}, u32[]{:S(2)}, u32[]{:S(2)}) async-start(f32[8,8,128]{2,1,0:T(8,128)} %prepare.1), calls=%async_computation | async-start | bytes 65536 | tf_op jit(solution)/shard_map/all_to_all | solution.py:403
  18.3 11.1 %all-to-all-done.got_ref = f32[8,8,128]{2,1,0:T(8,128)S(1)} async-done(((f32[8,8,128]{2,1,0:T(8,128)}), f32[8,8,128]{2,1,0:T(8,128)S(1)}, u32[]{:S(2)}, u32[]{:S(2)}) %all-to-all-start) | async-done | bytes 32800 | tf_op jit(solution)/shard_map/all_to_all | solution.py:403
  29.4 3.3 %first.1 = (f32[8,2,512,128]{3,2,1,0:T(8,128)S(1)}, f32[8,8,128]{2,1,0:T(8,128)S(1)}) custom-call(f32[1]{0:T(128)S(6)} %copy.8.wave_ref, f32[8,8,128]{2,1,0:T(8,128)S(1)} %all-to-all-done.got_ref), custom_call_target="tpu_custom_call" | custom-call | flops 25165824 | bytes 1048576 | tf_op jit(solution)/shard_map/first/pallas_call | solution.py:414
  32.7 9.6 %all_to_all.35.got_ref = f32[8,8,128]{2,1,0:T(8,128)S(1)} all-to-all(f32[8,8,128]{2,1,0:T(8,128)S(1)} %get-tuple-element.23), channel_id=1, replica_groups=mesh['ylo'=2,'x'=4,'core'=2,'yhi'=2,'za'=4,'zb'=2,'zc'=2] {'ylo','yhi','..., dimensions={0} | all-to-all | bytes 65536 | tf_op jit(solution)/shard_map/all_to_all | solution.py:403
  42.3 1.0 image.1
  43.3 12.6 %all_to_all.36.got_ref.got2_ref = f32[8,24,128]{2,1,0:T(8,128)S(1)} all-to-all(f32[8,24,128]{2,1,0:T(8,128)S(1)} %get-tuple-element.24), channel_id=1, replica_groups=mesh['ylo'=2,'x'=4,'core'=2,'yhi'=2,'za'=4,'zb'=2,'zc'=2] {'x','core'}, dimensions={0} | all-to-all | bytes 196608 | tf_op jit(solution)/shard_map/all_to_all | solution.py:403
  55.9 0.9 adjoint.1
  56.8 0.0 copy-start.2
  56.8 0.0 copy-start
  56.8 0.0 copy-start.1
  56.8 8.2 %all_to_all.37.got3_ref = f32[8,32,128]{2,1,0:T(8,128)S(1)} all-to-all(f32[8,32,128]{2,1,0:T(8,128)S(1)} %adjoint.1), channel_id=1, replica_groups=mesh['ylo'=2,'x'=4,'core'=2,'yhi'=2,'za'=4,'zb'=2,'zc'=2] {'ylo','yhi','..., dimensions={0} | all-to-all | bytes 262144 | tf_op jit(solution)/shard_map/all_to_all | solution.py:403
  65.0 1.1 %second_image.1 = (f32[8,24,128]{2,1,0:T(8,128)S(1)}, f32[2,128]{1,0:T(2,128)S(1)}) custom-call(f32[8,2,512,128]{3,2,1,0:T(8,128)S(1)} %get-tuple-element.22.g_ref, f32[8,32,128]{2,1,0:T(8,128)S(1)} %all_to_all.37.got3_ref, f32[8,24,128]{2,1,0:T(8,128)S(1)} %all_to_all.36.got_ref.got2_ref, f32[8,128]{1,0:T(8,128)S(1)} %get-tuple-element.25.g0_ref), custom_call_target="tpu_custom_call" | custom-call | flops 4194304 | bytes 1048576 | tf_op jit(solution)/shard_map/second_image/pallas_call | solution.py:431
  66.1 9.3 %all_to_all.38.got4_ref = f32[8,24,128]{2,1,0:T(8,128)S(1)} all-to-all(f32[8,24,128]{2,1,0:T(8,128)S(1)} %get-tuple-element.26), channel_id=1, replica_groups=mesh['ylo'=2,'x'=4,'core'=2,'yhi'=2,'za'=4,'zb'=2,'zc'=2] {'x','core'}, dimensions={0} | all-to-all | bytes 196608 | tf_op jit(solution)/shard_map/all_to_all | solution.py:403
  75.4 0.2 norm.1
  75.6 7.9 %all_to_all.39.got5_ref = f32[8,24,128]{2,1,0:T(8,128)S(1)} all-to-all(f32[8,24,128]{2,1,0:T(8,128)S(1)} %get-tuple-element.28), channel_id=1, replica_groups=mesh['ylo'=2,'x'=4,'core'=2,'yhi'=2,'za'=4,'zb'=2,'zc'=2] {'ylo','yhi','..., dimensions={0} | all-to-all | bytes 196608 | tf_op jit(solution)/shard_map/all_to_all | solution.py:403
  83.5 0.7 drive.1
  84.2 3.4 %all-to-all-start.6 = ((f32[8,40,128]{2,1,0:T(8,128)}), f32[8,40,128]{2,1,0:T(8,128)S(1)}, u32[]{:S(2)}, u32[]{:S(2)}) async-start(f32[8,40,128]{2,1,0:T(8,128)} %drive.1), calls=%async_computation.6 | async-start | bytes 327680 | tf_op jit(solution)/shard_map/all_to_all | solution.py:403
  87.6 3.0 %eval_green.1 = (bf16[256,4096]{1,0:T(8,128)(2,1)S(1)}, f8e4m3fn[256,4096]{1,0:T(32,128)(4,1)S(1)}) custom-call(f32[1]{0:T(128)S(6)} %copy.8.wave_ref, f32[3,128]{1,0:T(4,128)S(1)} %copy-done.2), custom_call_target="tpu_custom_call" | custom-call | flops 20971520 | bytes 1048576 | tf_op jit(solution)/shard_map/eval_green/pallas_call | solution.py:446
  90.7 10.2 %all-to-all-done.6 = f32[8,40,128]{2,1,0:T(8,128)S(1)} async-done(((f32[8,40,128]{2,1,0:T(8,128)}), f32[8,40,128]{2,1,0:T(8,128)S(1)}, u32[]{:S(2)}, u32[]{:S(2)}) %all-to-all-start.6) | async-done | bytes 163872 | tf_op jit(solution)/shard_map/all_to_all | solution.py:403
  100.9 5.8 %collective-permute-start = (f32[320,128]{1,0:T(8,128)S(1)}, f32[320,128]{1,0:T(8,128)S(1)}, u32[]{:S(2)}, u32[]{:S(2)}) collective-permute-start(f32[320,128]{1,0:T(8,128)S(1)} %bitcast.2), channel_id=1, source_target_pairs={{0,32},{32,0},{1,33},{33,1},{2,34},{34,2},{3,35},{35,3},{4,36},{36... | collective-permute-start | bytes 491528 | tf_op jit(solution)/shard_map/ppermute | solution.py:452
  106.7 1.3 %near_field.1 = (f32[2,8,256]{2,1,0:T(8,128)}, f32[2,8,256]{2,1,0:T(8,128)S(1)}, f32[16,256]{1,0:T(8,128)S(1)}) custom-call(f32[320,128]{1,0:T(8,128)S(1)} %bitcast.3, bf16[256,4096]{1,0:T(8,128)(2,1)S(1)} %get-tuple-element.34.high_ref, f8e4m3fn[256,4096]{1,0:T(32,128)(4,1)S(1)} %get-tuple-element.35.low_ref, f32[2,8,256]{2,1,0:T(8,128)S(1)} %copy-done.1, ...), custom_call_target="tpu_custom_call" | custom-call | flops 25165824 | bytes 1048576 | tf_op jit(solution)/shard_map/near_field/pallas_call | solution.py:454
  108.0 0.0 collective-permute-done.got_ref
  108.0 1.4 %far_field.1 = (f32[2,8,256]{2,1,0:T(8,128)}, f32[2,8,128]{2,1,0:T(8,128)}) custom-call(f32[320,128]{1,0:T(8,128)S(1)} %collective-permute-done.got_ref, bf16[256,4096]{1,0:T(8,128)(2,1)S(1)} %get-tuple-element.34.high_ref, f8e4m3fn[256,4096]{1,0:T(32,128)(4,1)S(1)} %get-tuple-element.35.low_ref, s32[32,128]{1,0:T(8,128)S(1)} %bitcast.5, ...), custom_call_target="tpu_custom_call" | custom-call | flops 25165824 | bytes 1048576 | tf_op jit(solution)/shard_map/far_field/pallas_call | solution.py:459
  (3 shorter events, 0.0 us)
Async XLA Ops:
  2.0 27.4 %all-to-all-start = ((f32[8,8,128]{2,1,0:T(8,128)}), f32[8,8,128]{2,1,0:T(8,128)S(1)}, u32[]{:S(2)}, u32[]{:S(2)}) async-start(f32[8,8,128]{2,1,0:T(8,128)} %prepare.1), calls=%async_computation | async-start | bytes 65536 | tf_op jit(solution)/shard_map/all_to_all | solution.py:403
  56.8 30.8 %copy-start.2 = (f32[3,128]{1,0:T(4,128)S(1)}, f32[3,128]{1,0:T(4,128)}, u32[]{:S(2)}) copy-start(f32[3,128]{1,0:T(4,128)} %eval_ref) | copy-start | bytes 4612
  56.8 49.9 %copy-start = (s32[4096]{0:T(1024)S(1)}, s32[4096]{0:T(1024)}, u32[]{:S(2)}) copy-start(s32[4096]{0:T(1024)} %param.6) | copy-start | bytes 49156
  56.8 49.9 %copy-start.1 = (f32[2,8,256]{2,1,0:T(8,128)S(1)}, f32[2,8,256]{2,1,0:T(8,128)}, u32[]{:S(2)}) copy-start(f32[2,8,256]{2,1,0:T(8,128)} %desired_ref.1) | copy-start | bytes 49156
  84.2 16.7 %all-to-all-start.6 = ((f32[8,40,128]{2,1,0:T(8,128)}), f32[8,40,128]{2,1,0:T(8,128)S(1)}, u32[]{:S(2)}, u32[]{:S(2)}) async-start(f32[8,40,128]{2,1,0:T(8,128)} %drive.1), calls=%async_computation.6 | async-start | bytes 327680 | tf_op jit(solution)/shard_map/all_to_all | solution.py:403
  100.9 7.1 %collective-permute-start = (f32[320,128]{1,0:T(8,128)S(1)}, f32[320,128]{1,0:T(8,128)S(1)}, u32[]{:S(2)}, u32[]{:S(2)}) collective-permute-start(f32[320,128]{1,0:T(8,128)S(1)} %bitcast.2), channel_id=1, source_target_pairs={{0,32},{32,0},{1,33},{33,1},{2,34},{34,2},{3,35},{35,3},{4,36},{36... | collective-permute-start | bytes 491528 | tf_op jit(solution)/shard_map/ppermute | solution.py:452

commit v5 on v4

--- a/solution.py
+++ b/solution.py
@@ -181,7 +181,7 @@
                 return real_sum, imag_sum
 
             zero = jnp.zeros((size, 128), f32)
-            real_sum, imag_sum = lax.fori_loop(0, 8, block, (zero, zero), unroll=2)
+            real_sum, imag_sum = lax.fori_loop(0, 8, block, (zero, zero), unroll=8)
             acc_ref[0, rows, :] = real_sum
             acc_ref[1, rows, :] = imag_sum
         return carry
@@ -227,7 +227,7 @@
 
 
 def adjoint(g_ref, im, acc_ref):
-    size = 64
+    size = 128
 
     def chunk(k, carry):
         rows = pl.ds(pl.multiple_of(k * size, size), size)
@@ -373,24 +373,23 @@
     return [jnp.concatenate(rows, axis=0) for rows in drives], out
 
 
-def near_field_kernel(
-    got_ref, high_ref, low_ref, desired_ref, cells_ref, residual_ref, drives_ref, product_ref
+def near_field_kernel(got_ref, high_ref, low_ref, cells_ref, drives_ref, product_ref):
+    drives, out = field_part(got_ref, lax.axis_index("core"), high_ref, low_ref, cells_ref)
+    drives_ref[0] = drives[0]
+    drives_ref[1] = drives[1]
+    product_ref[...] = out
+
+
+def far_field_kernel(
+    got_ref, high_ref, low_ref, cells_ref, near_drives_ref, near_product_ref, desired_ref, near_ref,
+    drives_ref, residual_ref, field_ref,
 ):
     for part in range(2):
         for half in range(2):
             lanes = slice(half * 128, half * 128 + 128)
             residual_ref[part, :, lanes] = desired_ref[part, :, lanes] - of_fields(
-                got_ref, 32 + part * 2 + half
+                near_ref, 32 + part * 2 + half
             )
-    drives, out = field_part(got_ref, lax.axis_index("core"), high_ref, low_ref, cells_ref)
-    drives_ref[0] = drives[0]
-    drives_ref[1] = drives[1]
-    product_ref[...] = out
-
-
-def far_field_kernel(
-    got_ref, high_ref, low_ref, cells_ref, near_drives_ref, near_product_ref, drives_ref, field_ref
-):
     drives, out = field_part(got_ref, 1 - lax.axis_index("core"), high_ref, low_ref, cells_ref)
     drives_ref[0] = near_drives_ref[0] + drives[0]
     drives_ref[1] = near_drives_ref[1] + drives[1]
@@ -451,17 +450,16 @@
     got6, high, low = lax.optimization_barrier((got6.reshape(8 * ROWS, 128), high, low))
     other = lax.ppermute(got6, "core", [(0, 1), (1, 0)])
     cells = spk_cells.reshape(32, 128)
-    residual, near_drives, product = call(
+    near_drives, product = call(
         near_field_kernel,
-        (shape(2, 8, 256), shape(2, 8, 256), shape(16, 256)),
-        [], 8, "vvvvv", "near_field", 524288 * 48,
-    )(got6, high, low, desired, cells)
-    drives, field = call(
+        (shape(2, 8, 256), shape(16, 256)),
+        [], 8, "vvvv", "near_field", 524288 * 48,
+    )(got6, high, low, cells)
+    return call(
         far_field_kernel,
-        (shape(2, 8, 256), shape(2, 8, 128)),
-        [], 8, "vvvvvv", "far_field", 524288 * 48,
-    )(other, high, low, cells, near_drives, product)
-    return drives, residual, field
+        (shape(2, 8, 256), shape(2, 8, 256), shape(2, 8, 128)),
+        [], 8, "vvvvvvvv", "far_field", 524288 * 48,
+    )(other, high, low, cells, near_drives, product, desired, got6)
 
 
 def solution(mesh):

time: 110 us -> 109 us (level)
  Pallas kernels: 14.3 us -> 13 us
  transfers between devices with their start and end apart: 3 -> 3, of which waited for: 2 -> 3; matrix products, arithmetic and copies ran while one was open for 0% -> 0% of each run, Pallas kernels for 4% -> 4%
where the time goes in v5:
time: 109 us; the launch traced here: 108 us
  blocking collectives  47.4 us (43%)
  starting transfers between devices  24.8 us (23%)
  waiting for transfers between devices  21.5 us (20%)
  Pallas kernels  13 us (12%)
  between operations  1.37 us (1%)
    all_to_all x5, blocking collectives, exchange(): return lax.all_to_all(array, axes, split_axis=0, concat_axis=0, tiled=True)  47.4 us
    all_to_all x2, waiting for transfers between devices, exchange(): return lax.all_to_all(array, axes, split_axis=0, concat_axis=0, tiled=True)  21.3 us
    all_to_all x2, starting transfers between devices, exchange(): return lax.all_to_all(array, axes, split_axis=0, concat_axis=0, tiled=True)  19 us
    ppermute x1, starting transfers between devices, local(): other = lax.ppermute(got6, 'core', [(0, 1), (1, 0)])  5.81 us
    pallas_call x1, Pallas kernels, local(): call(eval_green_kernel, (shape(256, 4096, dtype=bf16), shape(256, 4096, d...  3.04 us
    pallas_call x1, Pallas kernels, local(): call(first_kernel, (shape(8, 2, 512, 128), shape(8, 8, 128)), [vmem((8, 6...  2.57 us
  transfers between devices with their start and end apart: 3, of which 3 were waited for; matrix products, arithmetic and copies ran while one was open for 0% of the time, Pallas kernels for 4%

profile of v5, /device:TPU:1, one launch (start us, length us, event | category | flops | bytes accessed | tf_op | source)
XLA Modules:
  0.0 108.2 jit_solution(13152678468986867745)
XLA Ops:
  0.6 1.4 %prepare.1 = f32[8,8,128]{2,1,0:T(8,128)} custom-call(f32[2,8,256]{2,1,0:T(8,128)} %desired_ref.1, f32[3,256]{1,0:T(4,128)} %points_hbm.1), custom_call_target="tpu_custom_call" | custom-call | flops 1024 | bytes 1048576 | tf_op jit(solution)/shard_map/prepare/pallas_call | solution.py:406
  2.0 15.6 %all-to-all-start = ((f32[8,8,128]{2,1,0:T(8,128)}), f32[8,8,128]{2,1,0:T(8,128)S(1)}, u32[]{:S(2)}, u32[]{:S(2)}) async-start(f32[8,8,128]{2,1,0:T(8,128)} %prepare.1), calls=%async_computation | async-start | bytes 65536 | tf_op jit(solution)/shard_map/all_to_all | solution.py:402
  18.3 11.1 %all-to-all-done.got_ref = f32[8,8,128]{2,1,0:T(8,128)S(1)} async-done(((f32[8,8,128]{2,1,0:T(8,128)}), f32[8,8,128]{2,1,0:T(8,128)S(1)}, u32[]{:S(2)}, u32[]{:S(2)}) %all-to-all-start) | async-done | bytes 32800 | tf_op jit(solution)/shard_map/all_to_all | solution.py:402
  29.4 2.6 %first.1 = (f32[8,2,512,128]{3,2,1,0:T(8,128)S(1)}, f32[8,8,128]{2,1,0:T(8,128)S(1)}) custom-call(f32[1]{0:T(128)S(6)} %copy.8.wave_ref, f32[8,8,128]{2,1,0:T(8,128)S(1)} %all-to-all-done.got_ref), custom_call_target="tpu_custom_call" | custom-call | flops 25165824 | bytes 1048576 | tf_op jit(solution)/shard_map/first/pallas_call | solution.py:413
  32.0 9.6 %all_to_all.35.got_ref = f32[8,8,128]{2,1,0:T(8,128)S(1)} all-to-all(f32[8,8,128]{2,1,0:T(8,128)S(1)} %get-tuple-element.20), channel_id=1, replica_groups=mesh['ylo'=2,'x'=4,'core'=2,'yhi'=2,'za'=4,'zb'=2,'zc'=2] {'ylo','yhi','..., dimensions={0} | all-to-all | bytes 65536 | tf_op jit(solution)/shard_map/all_to_all | solution.py:402
  41.6 1.0 image.1
  42.5 12.6 %all_to_all.36.got_ref.got2_ref = f32[8,24,128]{2,1,0:T(8,128)S(1)} all-to-all(f32[8,24,128]{2,1,0:T(8,128)S(1)} %get-tuple-element.21), channel_id=1, replica_groups=mesh['ylo'=2,'x'=4,'core'=2,'yhi'=2,'za'=4,'zb'=2,'zc'=2] {'x','core'}, dimensions={0} | all-to-all | bytes 196608 | tf_op jit(solution)/shard_map/all_to_all | solution.py:402
  55.2 0.8 adjoint.1
  56.0 0.0 copy-start.2
  56.0 0.0 copy-start
  56.0 8.0 %all_to_all.37.got3_ref = f32[8,32,128]{2,1,0:T(8,128)S(1)} all-to-all(f32[8,32,128]{2,1,0:T(8,128)S(1)} %adjoint.1), channel_id=1, replica_groups=mesh['ylo'=2,'x'=4,'core'=2,'yhi'=2,'za'=4,'zb'=2,'zc'=2] {'ylo','yhi','..., dimensions={0} | all-to-all | bytes 262144 | tf_op jit(solution)/shard_map/all_to_all | solution.py:402
  64.0 1.1 %second_image.1 = (f32[8,24,128]{2,1,0:T(8,128)S(1)}, f32[2,128]{1,0:T(2,128)S(1)}) custom-call(f32[8,2,512,128]{3,2,1,0:T(8,128)S(1)} %get-tuple-element.19.g_ref, f32[8,32,128]{2,1,0:T(8,128)S(1)} %all_to_all.37.got3_ref, f32[8,24,128]{2,1,0:T(8,128)S(1)} %all_to_all.36.got_ref.got2_ref, f32[8,128]{1,0:T(8,128)S(1)} %get-tuple-element.22.g0_ref), custom_call_target="tpu_custom_call" | custom-call | flops 4194304 | bytes 1048576 | tf_op jit(solution)/shard_map/second_image/pallas_call | solution.py:430
  65.1 9.3 %all_to_all.38.got4_ref = f32[8,24,128]{2,1,0:T(8,128)S(1)} all-to-all(f32[8,24,128]{2,1,0:T(8,128)S(1)} %get-tuple-element.23), channel_id=1, replica_groups=mesh['ylo'=2,'x'=4,'core'=2,'yhi'=2,'za'=4,'zb'=2,'zc'=2] {'x','core'}, dimensions={0} | all-to-all | bytes 196608 | tf_op jit(solution)/shard_map/all_to_all | solution.py:402
  74.4 0.2 norm.1
  74.7 7.9 %all_to_all.39.got5_ref = f32[8,24,128]{2,1,0:T(8,128)S(1)} all-to-all(f32[8,24,128]{2,1,0:T(8,128)S(1)} %get-tuple-element.25), channel_id=1, replica_groups=mesh['ylo'=2,'x'=4,'core'=2,'yhi'=2,'za'=4,'zb'=2,'zc'=2] {'ylo','yhi','..., dimensions={0} | all-to-all | bytes 196608 | tf_op jit(solution)/shard_map/all_to_all | solution.py:402
  82.6 0.7 drive.1
  83.3 3.4 %all-to-all-start.6 = ((f32[8,40,128]{2,1,0:T(8,128)}), f32[8,40,128]{2,1,0:T(8,128)S(1)}, u32[]{:S(2)}, u32[]{:S(2)}) async-start(f32[8,40,128]{2,1,0:T(8,128)} %drive.1), calls=%async_computation.6 | async-start | bytes 327680 | tf_op jit(solution)/shard_map/all_to_all | solution.py:402
  86.6 0.0 copy-done.2
  86.7 3.0 %eval_green.1 = (bf16[256,4096]{1,0:T(8,128)(2,1)S(1)}, f8e4m3fn[256,4096]{1,0:T(32,128)(4,1)S(1)}) custom-call(f32[1]{0:T(128)S(6)} %copy.8.wave_ref, f32[3,128]{1,0:T(4,128)S(1)} %copy-done.2), custom_call_target="tpu_custom_call" | custom-call | flops 20971520 | bytes 1048576 | tf_op jit(solution)/shard_map/eval_green/pallas_call | solution.py:445
  89.7 10.2 %all-to-all-done.6 = f32[8,40,128]{2,1,0:T(8,128)S(1)} async-done(((f32[8,40,128]{2,1,0:T(8,128)}), f32[8,40,128]{2,1,0:T(8,128)S(1)}, u32[]{:S(2)}, u32[]{:S(2)}) %all-to-all-start.6) | async-done | bytes 163872 | tf_op jit(solution)/shard_map/all_to_all | solution.py:402
  99.9 5.8 %collective-permute-start = (f32[320,128]{1,0:T(8,128)S(1)}, f32[320,128]{1,0:T(8,128)S(1)}, u32[]{:S(2)}, u32[]{:S(2)}) collective-permute-start(f32[320,128]{1,0:T(8,128)S(1)} %bitcast.2), channel_id=1, source_target_pairs={{0,32},{32,0},{1,33},{33,1},{2,34},{34,2},{3,35},{35,3},{4,36},{36... | collective-permute-start | bytes 491528 | tf_op jit(solution)/shard_map/ppermute | solution.py:451
  105.8 0.8 near_field.1
  106.5 0.2 collective-permute-done.got_ref
  106.8 1.4 %far_field.1 = (f32[2,8,256]{2,1,0:T(8,128)}, f32[2,8,256]{2,1,0:T(8,128)}, f32[2,8,128]{2,1,0:T(8,128)}) custom-call(f32[320,128]{1,0:T(8,128)S(1)} %collective-permute-done.got_ref, bf16[256,4096]{1,0:T(8,128)(2,1)S(1)} %get-tuple-element.31.high_ref, f8e4m3fn[256,4096]{1,0:T(32,128)(4,1)S(1)} %get-tuple-element.32.low_ref, s32[32,128]{1,0:T(8,128)S(1)} %bitcast.6, ...), custom_call_target="tpu_custom_call" | custom-call | flops 25165824 | bytes 1048576 | tf_op jit(solution)/shard_map/far_field/pallas_call | solution.py:458
  (3 shorter events, 0.0 us)
Async XLA Ops:
  2.0 27.4 %all-to-all-start = ((f32[8,8,128]{2,1,0:T(8,128)}), f32[8,8,128]{2,1,0:T(8,128)S(1)}, u32[]{:S(2)}, u32[]{:S(2)}) async-start(f32[8,8,128]{2,1,0:T(8,128)} %prepare.1), calls=%async_computation | async-start | bytes 65536 | tf_op jit(solution)/shard_map/all_to_all | solution.py:402
  56.0 30.7 %copy-start.2 = (f32[3,128]{1,0:T(4,128)S(1)}, f32[3,128]{1,0:T(4,128)}, u32[]{:S(2)}) copy-start(f32[3,128]{1,0:T(4,128)} %eval_ref) | copy-start | bytes 4612
  56.0 49.8 %copy-start = (s32[4096]{0:T(1024)S(1)}, s32[4096]{0:T(1024)}, u32[]{:S(2)}) copy-start(s32[4096]{0:T(1024)} %param.6) | copy-start | bytes 49156
  64.0 42.7 %copy-start.1 = (f32[2,8,256]{2,1,0:T(8,128)S(1)}, f32[2,8,256]{2,1,0:T(8,128)}, u32[]{:S(2)}) copy-start(f32[2,8,256]{2,1,0:T(8,128)} %desired_ref.1) | copy-start | bytes 49156
  83.3 16.7 %all-to-all-start.6 = ((f32[8,40,128]{2,1,0:T(8,128)}), f32[8,40,128]{2,1,0:T(8,128)S(1)}, u32[]{:S(2)}, u32[]{:S(2)}) async-start(f32[8,40,128]{2,1,0:T(8,128)} %drive.1), calls=%async_computation.6 | async-start | bytes 327680 | tf_op jit(solution)/shard_map/all_to_all | solution.py:402
  99.9 6.8 %collective-permute-start = (f32[320,128]{1,0:T(8,128)S(1)}, f32[320,128]{1,0:T(8,128)S(1)}, u32[]{:S(2)}, u32[]{:S(2)}) collective-permute-start(f32[320,128]{1,0:T(8,128)S(1)} %bitcast.2), channel_id=1, source_target_pairs={{0,32},{32,0},{1,33},{33,1},{2,34},{34,2},{3,35},{35,3},{4,36},{36... | collective-permute-start | bytes 491528 | tf_op jit(solution)/shard_map/ppermute | solution.py:451

commit v6 on v5

--- a/solution.py
+++ b/solution.py
@@ -11,9 +11,10 @@
 WALL = 64
 SPK = ("ylo", "x", "core")
 PTS = ("yhi", "za", "zb", "zc")
-FLD = ("za", "zb")
-BANKS = ("x", "core")
-NEAR = ("ylo", "yhi", "zc")
+FLD = ("zb", "za")
+SPREAD = ("za", "zb")
+BANKS = ("core", "x")
+NEAR = ("zc", "yhi", "ylo")
 
 wall_pitch = 0.05
 front_gap = 0.5
@@ -115,10 +116,11 @@
     for copy in copies:
         copy.wait()
     points = points_ref[:, lanes]
-    for f in range(8):
-        send_ref[f, 0:1, :] = desired_ref[0, f : f + 1, lanes]
-        send_ref[f, 1:2, :] = desired_ref[1, f : f + 1, lanes]
-        send_ref[f, 2:5, :] = points
+    for i in range(8):
+        f = i % 2 * 4 + i // 2
+        send_ref[i, 0:1, :] = desired_ref[0, f : f + 1, lanes]
+        send_ref[i, 1:2, :] = desired_ref[1, f : f + 1, lanes]
+        send_ref[i, 2:5, :] = points
 
 
 def eval_green_kernel(wave_ref, eval_ref, high_ref, low_ref):
@@ -154,9 +156,10 @@
     wz = (iota((WALL, 128), 0).astype(f32) - centre) * (wall_pitch * kappa)
     wy = ((iota((8, 128), 0) + lax.axis_index(BANKS) * 8).astype(f32) - centre) * (wall_pitch * kappa)
     for j in range(8):
-        px = (front_gap + got_ref[j, 2:3, :] * depth_span) * kappa
-        py = (got_ref[j, 3:4, :] * side_span - 0.5 * side_span) * kappa
-        pz = (got_ref[j, 4:5, :] * side_span - 0.5 * side_span) * kappa
+        i = j % 4 * 2 + j // 4
+        px = (front_gap + got_ref[i, 2:3, :] * depth_span) * kappa
+        py = (got_ref[i, 3:4, :] * side_span - 0.5 * side_span) * kappa
+        pz = (got_ref[i, 4:5, :] * side_span - 0.5 * side_span) * kappa
         dz = pz - wz
         dz2_ref[j] = dz * dz
         dy = py - wy
@@ -169,8 +172,9 @@
 
             def block(j, sums):
                 real_sum, imag_sum = sums
-                vr = got_ref[j, 0:1, :]
-                vi = got_ref[j, 1:2, :]
+                i = jnp.bitwise_and(j, 3) * 2 + jnp.right_shift(j, 2)
+                vr = got_ref[i, 0:1, :]
+                vi = got_ref[i, 1:2, :]
                 real, imag = green(
                     dz2_ref[j, start : start + size, :] + rest_ref[j, pl.ds(r, 1), :], strength
                 )
@@ -319,7 +323,7 @@
         for i in range(8):
             send_ref[i, 8 * k : 8 * k + 8, :] = rows
     for half in range(2):
-        member = half * 4 + lax.axis_index(("yhi", "zc"))
+        member = lax.axis_index(("zc", "yhi")) * 2 + half
         change = alpha0 * got3_ref[member, 8:24, :] + alpha1 * got5_ref[member, 0:16, :]
         for i in range(8):
             send_ref[i, 32 + half : 33 + half, :] = change[i : i + 1, :]
@@ -409,7 +413,7 @@
         [vmem((2, 8, 256), f32), vmem((3, 256), f32), pltpu.SemaphoreType.DMA((2,))],
         WHOLE, "aa", "prepare", 1024,
     )(desired, pt_cells)
-    got0 = exchange(send0, FLD)
+    got0 = exchange(send0, SPREAD)
     g, send1 = call(
         first_kernel,
         (shape(8, 2, 512, 128), shape(8, 8, 128)),

time: 109 us -> 107 us (0.982)
  waiting for transfers between devices: 21.5 us -> 20.4 us
    all_to_all x2, waiting for transfers between devices: 21.3 us -> 20.2 us  [exchange(): return lax.all_to_all(array, axes, split_axis=0, concat_axis=0, tiled=True)]
where the time goes in v6:
time: 107 us; the launch traced here: 106 us
  blocking collectives  47 us (44%)
  starting transfers between devices  24.2 us (23%)
  waiting for transfers between devices  20.4 us (19%)
  Pallas kernels  13 us (12%)
  between operations  1.37 us (1%)
    all_to_all x5, blocking collectives, exchange(): return lax.all_to_all(array, axes, split_axis=0, concat_axis=0, tiled=True)  47 us
    all_to_all x2, waiting for transfers between devices, exchange(): return lax.all_to_all(array, axes, split_axis=0, concat_axis=0, tiled=True)  20.2 us
    all_to_all x2, starting transfers between devices, exchange(): return lax.all_to_all(array, axes, split_axis=0, concat_axis=0, tiled=True)  19 us
    ppermute x1, starting transfers between devices, local(): other = lax.ppermute(got6, 'core', [(0, 1), (1, 0)])  5.2 us
    pallas_call x1, Pallas kernels, local(): call(eval_green_kernel, (shape(256, 4096, dtype=bf16), shape(256, 4096, d...  3.04 us
    pallas_call x1, Pallas kernels, local(): call(first_kernel, (shape(8, 2, 512, 128), shape(8, 8, 128)), [vmem((8, 6...  2.57 us
  transfers between devices with their start and end apart: 3, of which 3 were waited for; matrix products, arithmetic and copies ran while one was open for 0% of the time, Pallas kernels for 4%

profile of v6, /device:TPU:1, one launch (start us, length us, event | category | flops | bytes accessed | tf_op | source)
XLA Modules:
  0.0 106.0 jit_solution(15150672658372288683)
XLA Ops:
  0.6 1.4 %prepare.1 = f32[8,8,128]{2,1,0:T(8,128)} custom-call(f32[2,8,256]{2,1,0:T(8,128)} %desired_ref.1, f32[3,256]{1,0:T(4,128)} %points_hbm.1), custom_call_target="tpu_custom_call" | custom-call | flops 1024 | bytes 1048576 | tf_op jit(solution)/shard_map/prepare/pallas_call | solution.py:410
  2.0 15.6 %all-to-all-start = ((f32[8,8,128]{2,1,0:T(8,128)}), f32[8,8,128]{2,1,0:T(8,128)S(1)}, u32[]{:S(2)}, u32[]{:S(2)}) async-start(f32[8,8,128]{2,1,0:T(8,128)} %prepare.1), calls=%async_computation | async-start | bytes 65536 | tf_op jit(solution)/shard_map/all_to_all | solution.py:406
  18.3 11.1 %all-to-all-done.got_ref = f32[8,8,128]{2,1,0:T(8,128)S(1)} async-done(((f32[8,8,128]{2,1,0:T(8,128)}), f32[8,8,128]{2,1,0:T(8,128)S(1)}, u32[]{:S(2)}, u32[]{:S(2)}) %all-to-all-start) | async-done | bytes 32800 | tf_op jit(solution)/shard_map/all_to_all | solution.py:406
  29.4 2.6 %first.1 = (f32[8,2,512,128]{3,2,1,0:T(8,128)S(1)}, f32[8,8,128]{2,1,0:T(8,128)S(1)}) custom-call(f32[1]{0:T(128)S(6)} %copy.8.wave_ref, f32[8,8,128]{2,1,0:T(8,128)S(1)} %all-to-all-done.got_ref), custom_call_target="tpu_custom_call" | custom-call | flops 25165824 | bytes 1048576 | tf_op jit(solution)/shard_map/first/pallas_call | solution.py:417
  32.0 9.6 %all_to_all.35.got_ref = f32[8,8,128]{2,1,0:T(8,128)S(1)} all-to-all(f32[8,8,128]{2,1,0:T(8,128)S(1)} %get-tuple-element.20), channel_id=1, replica_groups=mesh['ylo'=2,'x'=4,'core'=2,'yhi'=2,'za'=4,'zb'=2,'zc'=2] {'zc','yhi','y..., dimensions={0} | all-to-all | bytes 65536 | tf_op jit(solution)/shard_map/all_to_all | solution.py:406
  41.5 1.0 image.1
  42.5 12.6 %all_to_all.36.got_ref.got2_ref = f32[8,24,128]{2,1,0:T(8,128)S(1)} all-to-all(f32[8,24,128]{2,1,0:T(8,128)S(1)} %get-tuple-element.21), channel_id=1, replica_groups=mesh['ylo'=2,'x'=4,'core'=2,'yhi'=2,'za'=4,'zb'=2,'zc'=2] {'core','x'}, dimensions={0} | all-to-all | bytes 196608 | tf_op jit(solution)/shard_map/all_to_all | solution.py:406
  55.1 0.8 adjoint.1
  56.0 0.0 copy-start.2
  56.0 0.0 copy-start
  56.0 7.9 %all_to_all.37.got3_ref = f32[8,32,128]{2,1,0:T(8,128)S(1)} all-to-all(f32[8,32,128]{2,1,0:T(8,128)S(1)} %adjoint.1), channel_id=1, replica_groups=mesh['ylo'=2,'x'=4,'core'=2,'yhi'=2,'za'=4,'zb'=2,'zc'=2] {'zc','yhi','y..., dimensions={0} | all-to-all | bytes 262144 | tf_op jit(solution)/shard_map/all_to_all | solution.py:406
  63.9 1.1 %second_image.1 = (f32[8,24,128]{2,1,0:T(8,128)S(1)}, f32[2,128]{1,0:T(2,128)S(1)}) custom-call(f32[8,2,512,128]{3,2,1,0:T(8,128)S(1)} %get-tuple-element.19.g_ref, f32[8,32,128]{2,1,0:T(8,128)S(1)} %all_to_all.37.got3_ref, f32[8,24,128]{2,1,0:T(8,128)S(1)} %all_to_all.36.got_ref.got2_ref, f32[8,128]{1,0:T(8,128)S(1)} %get-tuple-element.22.g0_ref), custom_call_target="tpu_custom_call" | custom-call | flops 4194304 | bytes 1048576 | tf_op jit(solution)/shard_map/second_image/pallas_call | solution.py:434
  65.0 9.1 %all_to_all.38.got4_ref = f32[8,24,128]{2,1,0:T(8,128)S(1)} all-to-all(f32[8,24,128]{2,1,0:T(8,128)S(1)} %get-tuple-element.23), channel_id=1, replica_groups=mesh['ylo'=2,'x'=4,'core'=2,'yhi'=2,'za'=4,'zb'=2,'zc'=2] {'core','x'}, dimensions={0} | all-to-all | bytes 196608 | tf_op jit(solution)/shard_map/all_to_all | solution.py:406
  74.1 0.2 norm.1
  74.4 7.8 %all_to_all.39.got5_ref = f32[8,24,128]{2,1,0:T(8,128)S(1)} all-to-all(f32[8,24,128]{2,1,0:T(8,128)S(1)} %get-tuple-element.25), channel_id=1, replica_groups=mesh['ylo'=2,'x'=4,'core'=2,'yhi'=2,'za'=4,'zb'=2,'zc'=2] {'zc','yhi','y..., dimensions={0} | all-to-all | bytes 196608 | tf_op jit(solution)/shard_map/all_to_all | solution.py:406
  82.2 0.7 drive.1
  82.9 3.4 %all-to-all-start.6 = ((f32[8,40,128]{2,1,0:T(8,128)}), f32[8,40,128]{2,1,0:T(8,128)S(1)}, u32[]{:S(2)}, u32[]{:S(2)}) async-start(f32[8,40,128]{2,1,0:T(8,128)} %drive.1), calls=%async_computation.6 | async-start | bytes 327680 | tf_op jit(solution)/shard_map/all_to_all | solution.py:406
  86.2 0.0 copy-done.2
  86.3 3.0 %eval_green.1 = (bf16[256,4096]{1,0:T(8,128)(2,1)S(1)}, f8e4m3fn[256,4096]{1,0:T(32,128)(4,1)S(1)}) custom-call(f32[1]{0:T(128)S(6)} %copy.8.wave_ref, f32[3,128]{1,0:T(4,128)S(1)} %copy-done.2), custom_call_target="tpu_custom_call" | custom-call | flops 20971520 | bytes 1048576 | tf_op jit(solution)/shard_map/eval_green/pallas_call | solution.py:449
  89.3 9.0 %all-to-all-done.6 = f32[8,40,128]{2,1,0:T(8,128)S(1)} async-done(((f32[8,40,128]{2,1,0:T(8,128)}), f32[8,40,128]{2,1,0:T(8,128)S(1)}, u32[]{:S(2)}, u32[]{:S(2)}) %all-to-all-start.6) | async-done | bytes 163872 | tf_op jit(solution)/shard_map/all_to_all | solution.py:406
  98.3 5.2 %collective-permute-start = (f32[320,128]{1,0:T(8,128)S(1)}, f32[320,128]{1,0:T(8,128)S(1)}, u32[]{:S(2)}, u32[]{:S(2)}) collective-permute-start(f32[320,128]{1,0:T(8,128)S(1)} %bitcast.2), channel_id=1, source_target_pairs={{0,32},{32,0},{1,33},{33,1},{2,34},{34,2},{3,35},{35,3},{4,36},{36... | collective-permute-start | bytes 491528 | tf_op jit(solution)/shard_map/ppermute | solution.py:455
  103.6 0.8 near_field.1
  104.4 0.2 collective-permute-done.got_ref
  104.6 1.4 %far_field.1 = (f32[2,8,256]{2,1,0:T(8,128)}, f32[2,8,256]{2,1,0:T(8,128)}, f32[2,8,128]{2,1,0:T(8,128)}) custom-call(f32[320,128]{1,0:T(8,128)S(1)} %collective-permute-done.got_ref, bf16[256,4096]{1,0:T(8,128)(2,1)S(1)} %get-tuple-element.31.high_ref, f8e4m3fn[256,4096]{1,0:T(32,128)(4,1)S(1)} %get-tuple-element.32.low_ref, s32[32,128]{1,0:T(8,128)S(1)} %bitcast.6, ...), custom_call_target="tpu_custom_call" | custom-call | flops 25165824 | bytes 1048576 | tf_op jit(solution)/shard_map/far_field/pallas_call | solution.py:462
  (3 shorter events, 0.0 us)
Async XLA Ops:
  2.0 27.4 %all-to-all-start = ((f32[8,8,128]{2,1,0:T(8,128)}), f32[8,8,128]{2,1,0:T(8,128)S(1)}, u32[]{:S(2)}, u32[]{:S(2)}) async-start(f32[8,8,128]{2,1,0:T(8,128)} %prepare.1), calls=%async_computation | async-start | bytes 65536 | tf_op jit(solution)/shard_map/all_to_all | solution.py:406
  56.0 30.3 %copy-start.2 = (f32[3,128]{1,0:T(4,128)S(1)}, f32[3,128]{1,0:T(4,128)}, u32[]{:S(2)}) copy-start(f32[3,128]{1,0:T(4,128)} %eval_ref) | copy-start | bytes 4612
  56.0 47.6 %copy-start = (s32[4096]{0:T(1024)S(1)}, s32[4096]{0:T(1024)}, u32[]{:S(2)}) copy-start(s32[4096]{0:T(1024)} %param.6) | copy-start | bytes 49156
  63.9 40.7 %copy-start.1 = (f32[2,8,256]{2,1,0:T(8,128)S(1)}, f32[2,8,256]{2,1,0:T(8,128)}, u32[]{:S(2)}) copy-start(f32[2,8,256]{2,1,0:T(8,128)} %desired_ref.1) | copy-start | bytes 49156
  82.9 15.5 %all-to-all-start.6 = ((f32[8,40,128]{2,1,0:T(8,128)}), f32[8,40,128]{2,1,0:T(8,128)S(1)}, u32[]{:S(2)}, u32[]{:S(2)}) async-start(f32[8,40,128]{2,1,0:T(8,128)} %drive.1), calls=%async_computation.6 | async-start | bytes 327680 | tf_op jit(solution)/shard_map/all_to_all | solution.py:406
  98.3 6.2 %collective-permute-start = (f32[320,128]{1,0:T(8,128)S(1)}, f32[320,128]{1,0:T(8,128)S(1)}, u32[]{:S(2)}, u32[]{:S(2)}) collective-permute-start(f32[320,128]{1,0:T(8,128)S(1)} %bitcast.2), channel_id=1, source_target_pairs={{0,32},{32,0},{1,33},{33,1},{2,34},{34,2},{3,35},{35,3},{4,36},{36... | collective-permute-start | bytes 491528 | tf_op jit(solution)/shard_map/ppermute | solution.py:455

commit v7 on v6

--- a/solution.py
+++ b/solution.py
@@ -265,11 +265,9 @@
 def adjoint_kernel(g_ref, got_ref, send_ref, acc_ref):
     im = fold(got_ref[:, 0:16, :])
     rows = adjoint(g_ref, im, acc_ref)
-    norm = jnp.broadcast_to(total(im * im), (8, 128))
     for i in range(8):
         send_ref[i, 0:8, :] = rows
         send_ref[i, 8:24, :] = im
-        send_ref[i, 24:32, :] = norm
 
 
 def gathered_total(a, b):
@@ -281,7 +279,8 @@
     gamma = gathered_total(all_g0, all_g0)
     g0 = g0_ref[...]
     back = fold(got3_ref[:, 0:8, :])
-    norm = fold(got3_ref[:, 24:25, :])
+    all_im0 = got3_ref[:, 8:24, :]
+    norm = gathered_total(all_im0, all_im0)
     alpha = gamma / (norm + tikhonov * gamma)
     alpha_ref[0:1, :] = alpha
     alpha_ref[1:2, :] = gamma
@@ -304,16 +303,15 @@
     scalar_ref[0:1, :] = beta
     scalar_ref[1:2, :] = gamma1
     scalar_ref[2:3, :] = gamma1 + (2.0 * cross + beta * gamma0) * beta
-    square = jnp.broadcast_to(total(im1 * im1), (8, 128))
-    for i in range(8):
-        send_ref[i, 0:16, :] = im1
-        send_ref[i, 16:24, :] = square
+    for i in range(8):
+        send_ref[i] = im1
 
 
 def drive_kernel(got5_ref, got3_ref, got2_ref, got4_ref, alpha_ref, scalar_ref, send_ref):
     alpha0 = alpha_ref[0:1, :]
     beta = scalar_ref[0:1, :]
-    norm = fold(got5_ref[:, 16:17, :])
+    all_im1 = got5_ref[...]
+    norm = gathered_total(all_im1, all_im1)
     alpha1 = scalar_ref[1:2, :] / (norm + tikhonov * scalar_ref[2:3, :])
     from_first = alpha0 + alpha1 * beta
     core = lax.axis_index("core")
@@ -324,7 +322,7 @@
             send_ref[i, 8 * k : 8 * k + 8, :] = rows
     for half in range(2):
         member = lax.axis_index(("zc", "yhi")) * 2 + half
-        change = alpha0 * got3_ref[member, 8:24, :] + alpha1 * got5_ref[member, 0:16, :]
+        change = alpha0 * got3_ref[member, 8:24, :] + alpha1 * got5_ref[member]
         for i in range(8):
             send_ref[i, 32 + half : 33 + half, :] = change[i : i + 1, :]
             send_ref[i, 34 + half : 35 + half, :] = change[8 + i : 9 + i, :]
@@ -428,7 +426,7 @@
     )(g, got1)
     got2 = exchange(send2, BANKS)
     send3 = call(
-        adjoint_kernel, shape(8, 32, 128), [vmem((2, 512, 128), f32)], 8, "vv", "adjoint", 524288 * 8,
+        adjoint_kernel, shape(8, 24, 128), [vmem((2, 512, 128), f32)], 8, "vv", "adjoint", 524288 * 8,
     )(g, got2)
     got3 = exchange(send3, NEAR)
     send4, alpha = call(
@@ -438,7 +436,7 @@
     )(g, got3, got2, g0)
     got4 = exchange(send4, BANKS)
     send5, scalars = call(
-        norm_kernel, (shape(8, 24, 128), shape(3, 128)), [], 8, "vvv", "norm", 81920,
+        norm_kernel, (shape(8, 16, 128), shape(3, 128)), [], 8, "vvv", "norm", 81920,
     )(got4, got2, alpha)
     got5 = exchange(send5, NEAR)
     send6 = call(

time: 107 us -> 106 us (level)
  no operation moved by 1% of the time
where the time goes in v7:
time: 106 us
  blocking collectives  46.7 us (44%)
  starting transfers between devices  24.3 us (23%)
  waiting for transfers between devices  20.3 us (19%)
  Pallas kernels  13 us (12%)
  between operations  1.37 us (1%)
    all_to_all x5, blocking collectives, exchange(): return lax.all_to_all(array, axes, split_axis=0, concat_axis=0, tiled=True)  46.7 us
    all_to_all x2, waiting for transfers between devices, exchange(): return lax.all_to_all(array, axes, split_axis=0, concat_axis=0, tiled=True)  20.1 us
    all_to_all x2, starting transfers between devices, exchange(): return lax.all_to_all(array, axes, split_axis=0, concat_axis=0, tiled=True)  19 us
    ppermute x1, starting transfers between devices, local(): other = lax.ppermute(got6, 'core', [(0, 1), (1, 0)])  5.23 us
    pallas_call x1, Pallas kernels, local(): call(eval_green_kernel, (shape(256, 4096, dtype=bf16), shape(256, 4096, d...  3.04 us
    pallas_call x1, Pallas kernels, local(): call(first_kernel, (shape(8, 2, 512, 128), shape(8, 8, 128)), [vmem((8, 6...  2.57 us
  transfers between devices with their start and end apart: 3, of which 3 were waited for; matrix products, arithmetic and copies ran while one was open for 0% of the time, Pallas kernels for 4%

profile of v7, /device:TPU:1, one launch (start us, length us, event | category | flops | bytes accessed | tf_op | source)
XLA Modules:
  0.0 105.7 jit_solution(7276069549771453252)
XLA Ops:
  0.6 1.4 %prepare.1 = f32[8,8,128]{2,1,0:T(8,128)} custom-call(f32[2,8,256]{2,1,0:T(8,128)} %desired_ref.1, f32[3,256]{1,0:T(4,128)} %points_hbm.1), custom_call_target="tpu_custom_call" | custom-call | flops 1024 | bytes 1048576 | tf_op jit(solution)/shard_map/prepare/pallas_call | solution.py:408
  2.0 15.6 %all-to-all-start = ((f32[8,8,128]{2,1,0:T(8,128)}), f32[8,8,128]{2,1,0:T(8,128)S(1)}, u32[]{:S(2)}, u32[]{:S(2)}) async-start(f32[8,8,128]{2,1,0:T(8,128)} %prepare.1), calls=%async_computation | async-start | bytes 65536 | tf_op jit(solution)/shard_map/all_to_all | solution.py:404
  18.3 11.1 %all-to-all-done.got_ref = f32[8,8,128]{2,1,0:T(8,128)S(1)} async-done(((f32[8,8,128]{2,1,0:T(8,128)}), f32[8,8,128]{2,1,0:T(8,128)S(1)}, u32[]{:S(2)}, u32[]{:S(2)}) %all-to-all-start) | async-done | bytes 32800 | tf_op jit(solution)/shard_map/all_to_all | solution.py:404
  29.4 2.6 %first.1 = (f32[8,2,512,128]{3,2,1,0:T(8,128)S(1)}, f32[8,8,128]{2,1,0:T(8,128)S(1)}) custom-call(f32[1]{0:T(128)S(6)} %copy.8.wave_ref, f32[8,8,128]{2,1,0:T(8,128)S(1)} %all-to-all-done.got_ref), custom_call_target="tpu_custom_call" | custom-call | flops 25165824 | bytes 1048576 | tf_op jit(solution)/shard_map/first/pallas_call | solution.py:415
  32.0 9.6 %all_to_all.35.got_ref = f32[8,8,128]{2,1,0:T(8,128)S(1)} all-to-all(f32[8,8,128]{2,1,0:T(8,128)S(1)} %get-tuple-element.20), channel_id=1, replica_groups=mesh['ylo'=2,'x'=4,'core'=2,'yhi'=2,'za'=4,'zb'=2,'zc'=2] {'zc','yhi','y..., dimensions={0} | all-to-all | bytes 65536 | tf_op jit(solution)/shard_map/all_to_all | solution.py:404
  41.5 1.0 image.1
  42.5 12.6 %all_to_all.36.got_ref.got2_ref = f32[8,24,128]{2,1,0:T(8,128)S(1)} all-to-all(f32[8,24,128]{2,1,0:T(8,128)S(1)} %get-tuple-element.21), channel_id=1, replica_groups=mesh['ylo'=2,'x'=4,'core'=2,'yhi'=2,'za'=4,'zb'=2,'zc'=2] {'core','x'}, dimensions={0} | all-to-all | bytes 196608 | tf_op jit(solution)/shard_map/all_to_all | solution.py:404
  55.1 0.8 adjoint.1
  55.9 0.0 copy-start
  55.9 7.8 %all_to_all.37.got3_ref = f32[8,24,128]{2,1,0:T(8,128)S(1)} all-to-all(f32[8,24,128]{2,1,0:T(8,128)S(1)} %adjoint.1), channel_id=1, replica_groups=mesh['ylo'=2,'x'=4,'core'=2,'yhi'=2,'za'=4,'zb'=2,'zc'=2] {'zc','yhi','y..., dimensions={0} | all-to-all | bytes 196608 | tf_op jit(solution)/shard_map/all_to_all | solution.py:404
  63.7 1.1 %second_image.1 = (f32[8,24,128]{2,1,0:T(8,128)S(1)}, f32[2,128]{1,0:T(2,128)S(1)}) custom-call(f32[8,2,512,128]{3,2,1,0:T(8,128)S(1)} %get-tuple-element.19.g_ref, f32[8,24,128]{2,1,0:T(8,128)S(1)} %all_to_all.37.got3_ref, f32[8,24,128]{2,1,0:T(8,128)S(1)} %all_to_all.36.got_ref.got2_ref, f32[8,128]{1,0:T(8,128)S(1)} %get-tuple-element.22.g0_ref), custom_call_target="tpu_custom_call" | custom-call | flops 4194304 | bytes 1048576 | tf_op jit(solution)/shard_map/second_image/pallas_call | solution.py:432
  64.8 9.1 %all_to_all.38.got4_ref = f32[8,24,128]{2,1,0:T(8,128)S(1)} all-to-all(f32[8,24,128]{2,1,0:T(8,128)S(1)} %get-tuple-element.23), channel_id=1, replica_groups=mesh['ylo'=2,'x'=4,'core'=2,'yhi'=2,'za'=4,'zb'=2,'zc'=2] {'core','x'}, dimensions={0} | all-to-all | bytes 196608 | tf_op jit(solution)/shard_map/all_to_all | solution.py:404
  73.9 0.1 norm.1
  74.0 7.7 %all_to_all.39.got5_ref = f32[8,16,128]{2,1,0:T(8,128)S(1)} all-to-all(f32[8,16,128]{2,1,0:T(8,128)S(1)} %get-tuple-element.25), channel_id=1, replica_groups=mesh['ylo'=2,'x'=4,'core'=2,'yhi'=2,'za'=4,'zb'=2,'zc'=2] {'zc','yhi','y..., dimensions={0} | all-to-all | bytes 131072 | tf_op jit(solution)/shard_map/all_to_all | solution.py:404
  81.7 0.8 drive.1
  82.5 3.4 %all-to-all-start.6 = ((f32[8,40,128]{2,1,0:T(8,128)}), f32[8,40,128]{2,1,0:T(8,128)S(1)}, u32[]{:S(2)}, u32[]{:S(2)}) async-start(f32[8,40,128]{2,1,0:T(8,128)} %drive.1), calls=%async_computation.6 | async-start | bytes 327680 | tf_op jit(solution)/shard_map/all_to_all | solution.py:404
  85.9 0.0 copy-done.2
  85.9 3.0 %eval_green.1 = (bf16[256,4096]{1,0:T(8,128)(2,1)S(1)}, f8e4m3fn[256,4096]{1,0:T(32,128)(4,1)S(1)}) custom-call(f32[1]{0:T(128)S(6)} %copy.8.wave_ref, f32[3,128]{1,0:T(4,128)S(1)} %copy-done.2), custom_call_target="tpu_custom_call" | custom-call | flops 20971520 | bytes 1048576 | tf_op jit(solution)/shard_map/eval_green/pallas_call | solution.py:447
  89.0 9.0 %all-to-all-done.6 = f32[8,40,128]{2,1,0:T(8,128)S(1)} async-done(((f32[8,40,128]{2,1,0:T(8,128)}), f32[8,40,128]{2,1,0:T(8,128)S(1)}, u32[]{:S(2)}, u32[]{:S(2)}) %all-to-all-start.6) | async-done | bytes 163872 | tf_op jit(solution)/shard_map/all_to_all | solution.py:404
  98.0 5.2 %collective-permute-start = (f32[320,128]{1,0:T(8,128)S(1)}, f32[320,128]{1,0:T(8,128)S(1)}, u32[]{:S(2)}, u32[]{:S(2)}) collective-permute-start(f32[320,128]{1,0:T(8,128)S(1)} %bitcast.2), channel_id=1, source_target_pairs={{0,32},{32,0},{1,33},{33,1},{2,34},{34,2},{3,35},{35,3},{4,36},{36... | collective-permute-start | bytes 491528 | tf_op jit(solution)/shard_map/ppermute | solution.py:453
  103.2 0.0 copy-done
  103.3 0.8 near_field.1
  104.0 0.2 collective-permute-done.got_ref
  104.3 1.4 %far_field.1 = (f32[2,8,256]{2,1,0:T(8,128)}, f32[2,8,256]{2,1,0:T(8,128)}, f32[2,8,128]{2,1,0:T(8,128)}) custom-call(f32[320,128]{1,0:T(8,128)S(1)} %collective-permute-done.got_ref, bf16[256,4096]{1,0:T(8,128)(2,1)S(1)} %get-tuple-element.31.high_ref, f8e4m3fn[256,4096]{1,0:T(32,128)(4,1)S(1)} %get-tuple-element.32.low_ref, s32[32,128]{1,0:T(8,128)S(1)} %bitcast.6, ...), custom_call_target="tpu_custom_call" | custom-call | flops 25165824 | bytes 1048576 | tf_op jit(solution)/shard_map/far_field/pallas_call | solution.py:460
  (3 shorter events, 0.0 us)
Async XLA Ops:
  2.0 27.4 %all-to-all-start = ((f32[8,8,128]{2,1,0:T(8,128)}), f32[8,8,128]{2,1,0:T(8,128)S(1)}, u32[]{:S(2)}, u32[]{:S(2)}) async-start(f32[8,8,128]{2,1,0:T(8,128)} %prepare.1), calls=%async_computation | async-start | bytes 65536 | tf_op jit(solution)/shard_map/all_to_all | solution.py:404
  55.1 30.8 %copy-start.2 = (f32[3,128]{1,0:T(4,128)S(1)}, f32[3,128]{1,0:T(4,128)}, u32[]{:S(2)}) copy-start(f32[3,128]{1,0:T(4,128)} %eval_ref) | copy-start | bytes 4612
  55.9 47.3 %copy-start = (s32[4096]{0:T(1024)S(1)}, s32[4096]{0:T(1024)}, u32[]{:S(2)}) copy-start(s32[4096]{0:T(1024)} %param.6) | copy-start | bytes 49156
  63.7 40.5 %copy-start.1 = (f32[2,8,256]{2,1,0:T(8,128)S(1)}, f32[2,8,256]{2,1,0:T(8,128)}, u32[]{:S(2)}) copy-start(f32[2,8,256]{2,1,0:T(8,128)} %desired_ref.1) | copy-start | bytes 49156
  82.5 15.5 %all-to-all-start.6 = ((f32[8,40,128]{2,1,0:T(8,128)}), f32[8,40,128]{2,1,0:T(8,128)S(1)}, u32[]{:S(2)}, u32[]{:S(2)}) async-start(f32[8,40,128]{2,1,0:T(8,128)} %drive.1), calls=%async_computation.6 | async-start | bytes 327680 | tf_op jit(solution)/shard_map/all_to_all | solution.py:404
  98.0 6.2 %collective-permute-start = (f32[320,128]{1,0:T(8,128)S(1)}, f32[320,128]{1,0:T(8,128)S(1)}, u32[]{:S(2)}, u32[]{:S(2)}) collective-permute-start(f32[320,128]{1,0:T(8,128)S(1)} %bitcast.2), channel_id=1, source_target_pairs={{0,32},{32,0},{1,33},{33,1},{2,34},{34,2},{3,35},{35,3},{4,36},{36... | collective-permute-start | bytes 491528 | tf_op jit(solution)/shard_map/ppermute | solution.py:453

commit v8 on v7

--- a/solution.py
+++ b/solution.py
@@ -12,7 +12,6 @@
 SPK = ("ylo", "x", "core")
 PTS = ("yhi", "za", "zb", "zc")
 FLD = ("zb", "za")
-SPREAD = ("za", "zb")
 BANKS = ("core", "x")
 NEAR = ("zc", "yhi", "ylo")
 
@@ -116,11 +115,10 @@
     for copy in copies:
         copy.wait()
     points = points_ref[:, lanes]
-    for i in range(8):
-        f = i % 2 * 4 + i // 2
-        send_ref[i, 0:1, :] = desired_ref[0, f : f + 1, lanes]
-        send_ref[i, 1:2, :] = desired_ref[1, f : f + 1, lanes]
-        send_ref[i, 2:5, :] = points
+    for f in range(8):
+        send_ref[f, 0:1, :] = desired_ref[0, f : f + 1, lanes]
+        send_ref[f, 1:2, :] = desired_ref[1, f : f + 1, lanes]
+        send_ref[f, 2:5, :] = points
 
 
 def eval_green_kernel(wave_ref, eval_ref, high_ref, low_ref):
@@ -156,15 +154,14 @@
     wz = (iota((WALL, 128), 0).astype(f32) - centre) * (wall_pitch * kappa)
     wy = ((iota((8, 128), 0) + lax.axis_index(BANKS) * 8).astype(f32) - centre) * (wall_pitch * kappa)
     for j in range(8):
-        i = j % 4 * 2 + j // 4
-        px = (front_gap + got_ref[i, 2:3, :] * depth_span) * kappa
-        py = (got_ref[i, 3:4, :] * side_span - 0.5 * side_span) * kappa
-        pz = (got_ref[i, 4:5, :] * side_span - 0.5 * side_span) * kappa
+        px = (front_gap + got_ref[j, 2:3, :] * depth_span) * kappa
+        py = (got_ref[j, 3:4, :] * side_span - 0.5 * side_span) * kappa
+        pz = (got_ref[j, 4:5, :] * side_span - 0.5 * side_span) * kappa
         dz = pz - wz
         dz2_ref[j] = dz * dz
         dy = py - wy
         rest_ref[j] = px * px + dy * dy
-    size = 32
+    size = 64
 
     def wall_row(r, carry):
         for start in range(0, WALL, size):
@@ -172,9 +169,8 @@
 
             def block(j, sums):
                 real_sum, imag_sum = sums
-                i = jnp.bitwise_and(j, 3) * 2 + jnp.right_shift(j, 2)
-                vr = got_ref[i, 0:1, :]
-                vi = got_ref[i, 1:2, :]
+                vr = got_ref[j, 0:1, :]
+                vi = got_ref[j, 1:2, :]
                 real, imag = green(
                     dz2_ref[j, start : start + size, :] + rest_ref[j, pl.ds(r, 1), :], strength
                 )
@@ -411,7 +407,7 @@
         [vmem((2, 8, 256), f32), vmem((3, 256), f32), pltpu.SemaphoreType.DMA((2,))],
         WHOLE, "aa", "prepare", 1024,
     )(desired, pt_cells)
-    got0 = exchange(send0, SPREAD)
+    got0 = exchange(send0, FLD)
     g, send1 = call(
         first_kernel,
         (shape(8, 2, 512, 128), shape(8, 8, 128)),

time: 106 us -> 106 us (level)
  no operation moved by 1% of the time
where the time goes in v8:
time: 106 us
  blocking collectives  47.1 us (44%)
  starting transfers between devices  24.3 us (23%)
  waiting for transfers between devices  20 us (19%)
  Pallas kernels  12.9 us (12%)
  between operations  1.37 us (1%)
    all_to_all x5, blocking collectives, exchange(): return lax.all_to_all(array, axes, split_axis=0, concat_axis=0, tiled=True)  47.1 us
    all_to_all x2, waiting for transfers between devices, exchange(): return lax.all_to_all(array, axes, split_axis=0, concat_axis=0, tiled=True)  19.8 us
    all_to_all x2, starting transfers between devices, exchange(): return lax.all_to_all(array, axes, split_axis=0, concat_axis=0, tiled=True)  19 us
    ppermute x1, starting transfers between devices, local(): other = lax.ppermute(got6, 'core', [(0, 1), (1, 0)])  5.23 us
    pallas_call x1, Pallas kernels, local(): call(eval_green_kernel, (shape(256, 4096, dtype=bf16), shape(256, 4096, d...  3.04 us
    pallas_call x1, Pallas kernels, local(): call(first_kernel, (shape(8, 2, 512, 128), shape(8, 8, 128)), [vmem((8, 6...  2.57 us
  transfers between devices with their start and end apart: 3, of which 3 were waited for; matrix products, arithmetic and copies ran while one was open for 0% of the time, Pallas kernels for 4%

profile of v8, /device:TPU:1, one launch (start us, length us, event | category | flops | bytes accessed | tf_op | source)
XLA Modules:
  0.0 105.6 jit_solution(14289853065798519712)
XLA Ops:
  0.6 1.4 %prepare.1 = f32[8,8,128]{2,1,0:T(8,128)} custom-call(f32[2,8,256]{2,1,0:T(8,128)} %desired_ref.1, f32[3,256]{1,0:T(4,128)} %points_hbm.1), custom_call_target="tpu_custom_call" | custom-call | flops 1024 | bytes 1048576 | tf_op jit(solution)/shard_map/prepare/pallas_call | solution.py:404
  2.0 15.6 %all-to-all-start = ((f32[8,8,128]{2,1,0:T(8,128)}), f32[8,8,128]{2,1,0:T(8,128)S(1)}, u32[]{:S(2)}, u32[]{:S(2)}) async-start(f32[8,8,128]{2,1,0:T(8,128)} %prepare.1), calls=%async_computation | async-start | bytes 65536 | tf_op jit(solution)/shard_map/all_to_all | solution.py:400
  18.3 10.7 %all-to-all-done.got_ref = f32[8,8,128]{2,1,0:T(8,128)S(1)} async-done(((f32[8,8,128]{2,1,0:T(8,128)}), f32[8,8,128]{2,1,0:T(8,128)S(1)}, u32[]{:S(2)}, u32[]{:S(2)}) %all-to-all-start) | async-done | bytes 32800 | tf_op jit(solution)/shard_map/all_to_all | solution.py:400
  29.0 2.6 %first.1 = (f32[8,2,512,128]{3,2,1,0:T(8,128)S(1)}, f32[8,8,128]{2,1,0:T(8,128)S(1)}) custom-call(f32[1]{0:T(128)S(6)} %copy.8.wave_ref, f32[8,8,128]{2,1,0:T(8,128)S(1)} %all-to-all-done.got_ref), custom_call_target="tpu_custom_call" | custom-call | flops 25165824 | bytes 1048576 | tf_op jit(solution)/shard_map/first/pallas_call | solution.py:411
  31.6 9.9 %all_to_all.35.got_ref = f32[8,8,128]{2,1,0:T(8,128)S(1)} all-to-all(f32[8,8,128]{2,1,0:T(8,128)S(1)} %get-tuple-element.20), channel_id=1, replica_groups=mesh['ylo'=2,'x'=4,'core'=2,'yhi'=2,'za'=4,'zb'=2,'zc'=2] {'zc','yhi','y..., dimensions={0} | all-to-all | bytes 65536 | tf_op jit(solution)/shard_map/all_to_all | solution.py:400
  41.5 1.0 image.1
  42.5 12.6 %all_to_all.36.got_ref.got2_ref = f32[8,24,128]{2,1,0:T(8,128)S(1)} all-to-all(f32[8,24,128]{2,1,0:T(8,128)S(1)} %get-tuple-element.21), channel_id=1, replica_groups=mesh['ylo'=2,'x'=4,'core'=2,'yhi'=2,'za'=4,'zb'=2,'zc'=2] {'core','x'}, dimensions={0} | all-to-all | bytes 196608 | tf_op jit(solution)/shard_map/all_to_all | solution.py:400
  55.1 0.8 adjoint.1
  55.9 0.0 copy-start
  55.9 7.8 %all_to_all.37.got3_ref = f32[8,24,128]{2,1,0:T(8,128)S(1)} all-to-all(f32[8,24,128]{2,1,0:T(8,128)S(1)} %adjoint.1), channel_id=1, replica_groups=mesh['ylo'=2,'x'=4,'core'=2,'yhi'=2,'za'=4,'zb'=2,'zc'=2] {'zc','yhi','y..., dimensions={0} | all-to-all | bytes 196608 | tf_op jit(solution)/shard_map/all_to_all | solution.py:400
  63.7 1.1 %second_image.1 = (f32[8,24,128]{2,1,0:T(8,128)S(1)}, f32[2,128]{1,0:T(2,128)S(1)}) custom-call(f32[8,2,512,128]{3,2,1,0:T(8,128)S(1)} %get-tuple-element.19.g_ref, f32[8,24,128]{2,1,0:T(8,128)S(1)} %all_to_all.37.got3_ref, f32[8,24,128]{2,1,0:T(8,128)S(1)} %all_to_all.36.got_ref.got2_ref, f32[8,128]{1,0:T(8,128)S(1)} %get-tuple-element.22.g0_ref), custom_call_target="tpu_custom_call" | custom-call | flops 4194304 | bytes 1048576 | tf_op jit(solution)/shard_map/second_image/pallas_call | solution.py:428
  64.8 9.1 %all_to_all.38.got4_ref = f32[8,24,128]{2,1,0:T(8,128)S(1)} all-to-all(f32[8,24,128]{2,1,0:T(8,128)S(1)} %get-tuple-element.23), channel_id=1, replica_groups=mesh['ylo'=2,'x'=4,'core'=2,'yhi'=2,'za'=4,'zb'=2,'zc'=2] {'core','x'}, dimensions={0} | all-to-all | bytes 196608 | tf_op jit(solution)/shard_map/all_to_all | solution.py:400
  73.9 0.1 norm.1
  74.0 7.7 %all_to_all.39.got5_ref = f32[8,16,128]{2,1,0:T(8,128)S(1)} all-to-all(f32[8,16,128]{2,1,0:T(8,128)S(1)} %get-tuple-element.25), channel_id=1, replica_groups=mesh['ylo'=2,'x'=4,'core'=2,'yhi'=2,'za'=4,'zb'=2,'zc'=2] {'zc','yhi','y..., dimensions={0} | all-to-all | bytes 131072 | tf_op jit(solution)/shard_map/all_to_all | solution.py:400
  81.7 0.8 drive.1
  82.5 3.4 %all-to-all-start.6 = ((f32[8,40,128]{2,1,0:T(8,128)}), f32[8,40,128]{2,1,0:T(8,128)S(1)}, u32[]{:S(2)}, u32[]{:S(2)}) async-start(f32[8,40,128]{2,1,0:T(8,128)} %drive.1), calls=%async_computation.6 | async-start | bytes 327680 | tf_op jit(solution)/shard_map/all_to_all | solution.py:400
  85.9 0.0 copy-done.2
  85.9 3.0 %eval_green.1 = (bf16[256,4096]{1,0:T(8,128)(2,1)S(1)}, f8e4m3fn[256,4096]{1,0:T(32,128)(4,1)S(1)}) custom-call(f32[1]{0:T(128)S(6)} %copy.8.wave_ref, f32[3,128]{1,0:T(4,128)S(1)} %copy-done.2), custom_call_target="tpu_custom_call" | custom-call | flops 20971520 | bytes 1048576 | tf_op jit(solution)/shard_map/eval_green/pallas_call | solution.py:443
  88.9 9.0 %all-to-all-done.6 = f32[8,40,128]{2,1,0:T(8,128)S(1)} async-done(((f32[8,40,128]{2,1,0:T(8,128)}), f32[8,40,128]{2,1,0:T(8,128)S(1)}, u32[]{:S(2)}, u32[]{:S(2)}) %all-to-all-start.6) | async-done | bytes 163872 | tf_op jit(solution)/shard_map/all_to_all | solution.py:400
  98.0 5.2 %collective-permute-start = (f32[320,128]{1,0:T(8,128)S(1)}, f32[320,128]{1,0:T(8,128)S(1)}, u32[]{:S(2)}, u32[]{:S(2)}) collective-permute-start(f32[320,128]{1,0:T(8,128)S(1)} %bitcast.2), channel_id=1, source_target_pairs={{0,32},{32,0},{1,33},{33,1},{2,34},{34,2},{3,35},{35,3},{4,36},{36... | collective-permute-start | bytes 491528 | tf_op jit(solution)/shard_map/ppermute | solution.py:449
  103.2 0.0 copy-done
  103.2 0.8 near_field.1
  104.0 0.2 collective-permute-done.got_ref
  104.2 1.4 %far_field.1 = (f32[2,8,256]{2,1,0:T(8,128)}, f32[2,8,256]{2,1,0:T(8,128)}, f32[2,8,128]{2,1,0:T(8,128)}) custom-call(f32[320,128]{1,0:T(8,128)S(1)} %collective-permute-done.got_ref, bf16[256,4096]{1,0:T(8,128)(2,1)S(1)} %get-tuple-element.31.high_ref, f8e4m3fn[256,4096]{1,0:T(32,128)(4,1)S(1)} %get-tuple-element.32.low_ref, s32[32,128]{1,0:T(8,128)S(1)} %bitcast.6, ...), custom_call_target="tpu_custom_call" | custom-call | flops 25165824 | bytes 1048576 | tf_op jit(solution)/shard_map/far_field/pallas_call | solution.py:456
  (3 shorter events, 0.0 us)
Async XLA Ops:
  2.0 27.0 %all-to-all-start = ((f32[8,8,128]{2,1,0:T(8,128)}), f32[8,8,128]{2,1,0:T(8,128)S(1)}, u32[]{:S(2)}, u32[]{:S(2)}) async-start(f32[8,8,128]{2,1,0:T(8,128)} %prepare.1), calls=%async_computation | async-start | bytes 65536 | tf_op jit(solution)/shard_map/all_to_all | solution.py:400
  55.1 30.8 %copy-start.2 = (f32[3,128]{1,0:T(4,128)S(1)}, f32[3,128]{1,0:T(4,128)}, u32[]{:S(2)}) copy-start(f32[3,128]{1,0:T(4,128)} %eval_ref) | copy-start | bytes 4612
  55.9 47.3 %copy-start = (s32[4096]{0:T(1024)S(1)}, s32[4096]{0:T(1024)}, u32[]{:S(2)}) copy-start(s32[4096]{0:T(1024)} %param.6) | copy-start | bytes 49156
  63.7 40.5 %copy-start.1 = (f32[2,8,256]{2,1,0:T(8,128)S(1)}, f32[2,8,256]{2,1,0:T(8,128)}, u32[]{:S(2)}) copy-start(f32[2,8,256]{2,1,0:T(8,128)} %desired_ref.1) | copy-start | bytes 49156
  82.5 15.5 %all-to-all-start.6 = ((f32[8,40,128]{2,1,0:T(8,128)}), f32[8,40,128]{2,1,0:T(8,128)S(1)}, u32[]{:S(2)}, u32[]{:S(2)}) async-start(f32[8,40,128]{2,1,0:T(8,128)} %drive.1), calls=%async_computation.6 | async-start | bytes 327680 | tf_op jit(solution)/shard_map/all_to_all | solution.py:400
  98.0 6.2 %collective-permute-start = (f32[320,128]{1,0:T(8,128)S(1)}, f32[320,128]{1,0:T(8,128)S(1)}, u32[]{:S(2)}, u32[]{:S(2)}) collective-permute-start(f32[320,128]{1,0:T(8,128)S(1)} %bitcast.2), channel_id=1, source_target_pairs={{0,32},{32,0},{1,33},{33,1},{2,34},{34,2},{3,35},{35,3},{4,36},{36... | collective-permute-start | bytes 491528 | tf_op jit(solution)/shard_map/ppermute | solution.py:449

commit v9 on v8

--- a/solution.py
+++ b/solution.py
@@ -9,10 +9,10 @@
 from jax.sharding import PartitionSpec as P
 
 WALL = 64
-SPK = ("ylo", "x", "core")
-PTS = ("yhi", "za", "zb", "zc")
-FLD = ("zb", "za")
-BANKS = ("core", "x")
+SPK = ("ylo", "xhi", "xlo", "core")
+PTS = ("yhi", "zhi", "zlo", "zb", "zc")
+FLD = ("zb", "zlo", "zhi")
+BANKS = ("core", "xlo", "xhi")
 NEAR = ("zc", "yhi", "ylo")
 
 wall_pitch = 0.05
@@ -461,9 +461,7 @@
 
 
 def solution(mesh):
-    split = Mesh(
-        mesh.devices.reshape(2, 4, 2, 2, 4, 2, 2), ("ylo", "x", "core", "yhi", "za", "zb", "zc")
-    )
+    split = Mesh(mesh.devices.reshape((2,) * 9), SPK + PTS)
     in_specs = (P(None, None, PTS), P(), P(None, PTS), P(None, SPK + PTS), P())
     out_specs = (P(None, None, SPK), P(None, None, PTS), P(None, None, SPK + PTS))
     return jax.shard_map(local, mesh=split, in_specs=in_specs, out_specs=out_specs, check_vma=False)

time: 106 us -> 105 us (level)
  no operation moved by 1% of the time
where the time goes in v9:
time: 105 us
  blocking collectives  46.7 us (44%)
  starting transfers between devices  23.9 us (23%)
  waiting for transfers between devices  19.6 us (19%)
  Pallas kernels  13 us (12%)
  between operations  1.37 us (1%)
    all_to_all x5, blocking collectives, exchange(): return lax.all_to_all(array, axes, split_axis=0, concat_axis=0, tiled=True)  46.7 us
    all_to_all x2, waiting for transfers between devices, exchange(): return lax.all_to_all(array, axes, split_axis=0, concat_axis=0, tiled=True)  19.4 us
    all_to_all x2, starting transfers between devices, exchange(): return lax.all_to_all(array, axes, split_axis=0, concat_axis=0, tiled=True)  19 us
    ppermute x1, starting transfers between devices, local(): other = lax.ppermute(got6, 'core', [(0, 1), (1, 0)])  4.88 us
    pallas_call x1, Pallas kernels, local(): call(eval_green_kernel, (shape(256, 4096, dtype=bf16), shape(256, 4096, d...  3.04 us
    pallas_call x1, Pallas kernels, local(): call(first_kernel, (shape(8, 2, 512, 128), shape(8, 8, 128)), [vmem((8, 6...  2.57 us
  transfers between devices with their start and end apart: 3, of which 3 were waited for; matrix products, arithmetic and copies ran while one was open for 0% of the time, Pallas kernels for 4%

profile of v9, /device:TPU:1, one launch (start us, length us, event | category | flops | bytes accessed | tf_op | source)
XLA Modules:
  0.0 104.5 jit_solution(1498909016055088559)
XLA Ops:
  0.6 1.4 %prepare.1 = f32[8,8,128]{2,1,0:T(8,128)} custom-call(f32[2,8,256]{2,1,0:T(8,128)} %desired_ref.1, f32[3,256]{1,0:T(4,128)} %points_hbm.1), custom_call_target="tpu_custom_call" | custom-call | flops 1024 | bytes 1048576 | tf_op jit(solution)/shard_map/prepare/pallas_call | solution.py:404
  2.0 15.6 %all-to-all-start = ((f32[8,8,128]{2,1,0:T(8,128)}), f32[8,8,128]{2,1,0:T(8,128)S(1)}, u32[]{:S(2)}, u32[]{:S(2)}) async-start(f32[8,8,128]{2,1,0:T(8,128)} %prepare.1), calls=%async_computation | async-start | bytes 65536 | tf_op jit(solution)/shard_map/all_to_all | solution.py:400
  18.3 10.7 %all-to-all-done.got_ref = f32[8,8,128]{2,1,0:T(8,128)S(1)} async-done(((f32[8,8,128]{2,1,0:T(8,128)}), f32[8,8,128]{2,1,0:T(8,128)S(1)}, u32[]{:S(2)}, u32[]{:S(2)}) %all-to-all-start) | async-done | bytes 32800 | tf_op jit(solution)/shard_map/all_to_all | solution.py:400
  29.0 2.6 %first.1 = (f32[8,2,512,128]{3,2,1,0:T(8,128)S(1)}, f32[8,8,128]{2,1,0:T(8,128)S(1)}) custom-call(f32[1]{0:T(128)S(6)} %copy.8.wave_ref, f32[8,8,128]{2,1,0:T(8,128)S(1)} %all-to-all-done.got_ref), custom_call_target="tpu_custom_call" | custom-call | flops 25165824 | bytes 1048576 | tf_op jit(solution)/shard_map/first/pallas_call | solution.py:411
  31.6 9.6 %all_to_all.35.got_ref = f32[8,8,128]{2,1,0:T(8,128)S(1)} all-to-all(f32[8,8,128]{2,1,0:T(8,128)S(1)} %get-tuple-element.20), channel_id=1, replica_groups=mesh['ylo'=2,'xhi'=2,'xlo'=2,'core'=2,'yhi'=2,'zhi'=2,'zlo'=2,'zb'=2,'zc..., dimensions={0} | all-to-all | bytes 65536 | tf_op jit(solution)/shard_map/all_to_all | solution.py:400
  41.2 1.0 image.1
  42.1 12.6 %all_to_all.36.got_ref.got2_ref = f32[8,24,128]{2,1,0:T(8,128)S(1)} all-to-all(f32[8,24,128]{2,1,0:T(8,128)S(1)} %get-tuple-element.21), channel_id=1, replica_groups=mesh['ylo'=2,'xhi'=2,'xlo'=2,'core'=2,'yhi'=2,'zhi'=2,'zlo'=2,'zb'=2,'zc..., dimensions={0} | all-to-all | bytes 196608 | tf_op jit(solution)/shard_map/all_to_all | solution.py:400
  54.8 0.8 adjoint.1
  55.5 0.0 copy-start
  55.6 7.8 %all_to_all.37.got3_ref = f32[8,24,128]{2,1,0:T(8,128)S(1)} all-to-all(f32[8,24,128]{2,1,0:T(8,128)S(1)} %adjoint.1), channel_id=1, replica_groups=mesh['ylo'=2,'xhi'=2,'xlo'=2,'core'=2,'yhi'=2,'zhi'=2,'zlo'=2,'zb'=2,'zc..., dimensions={0} | all-to-all | bytes 196608 | tf_op jit(solution)/shard_map/all_to_all | solution.py:400
  63.3 1.1 %second_image.1 = (f32[8,24,128]{2,1,0:T(8,128)S(1)}, f32[2,128]{1,0:T(2,128)S(1)}) custom-call(f32[8,2,512,128]{3,2,1,0:T(8,128)S(1)} %get-tuple-element.19.g_ref, f32[8,24,128]{2,1,0:T(8,128)S(1)} %all_to_all.37.got3_ref, f32[8,24,128]{2,1,0:T(8,128)S(1)} %all_to_all.36.got_ref.got2_ref, f32[8,128]{1,0:T(8,128)S(1)} %get-tuple-element.22.g0_ref), custom_call_target="tpu_custom_call" | custom-call | flops 4194304 | bytes 1048576 | tf_op jit(solution)/shard_map/second_image/pallas_call | solution.py:428
  64.4 9.1 %all_to_all.38.got4_ref = f32[8,24,128]{2,1,0:T(8,128)S(1)} all-to-all(f32[8,24,128]{2,1,0:T(8,128)S(1)} %get-tuple-element.23), channel_id=1, replica_groups=mesh['ylo'=2,'xhi'=2,'xlo'=2,'core'=2,'yhi'=2,'zhi'=2,'zlo'=2,'zb'=2,'zc..., dimensions={0} | all-to-all | bytes 196608 | tf_op jit(solution)/shard_map/all_to_all | solution.py:400
  73.5 0.1 norm.1
  73.7 7.7 %all_to_all.39.got5_ref = f32[8,16,128]{2,1,0:T(8,128)S(1)} all-to-all(f32[8,16,128]{2,1,0:T(8,128)S(1)} %get-tuple-element.25), channel_id=1, replica_groups=mesh['ylo'=2,'xhi'=2,'xlo'=2,'core'=2,'yhi'=2,'zhi'=2,'zlo'=2,'zb'=2,'zc..., dimensions={0} | all-to-all | bytes 131072 | tf_op jit(solution)/shard_map/all_to_all | solution.py:400
  81.3 0.8 drive.1
  82.2 3.4 %all-to-all-start.6 = ((f32[8,40,128]{2,1,0:T(8,128)}), f32[8,40,128]{2,1,0:T(8,128)S(1)}, u32[]{:S(2)}, u32[]{:S(2)}) async-start(f32[8,40,128]{2,1,0:T(8,128)} %drive.1), calls=%async_computation.6 | async-start | bytes 327680 | tf_op jit(solution)/shard_map/all_to_all | solution.py:400
  85.5 0.0 copy-done.2
  85.6 3.0 %eval_green.1 = (bf16[256,4096]{1,0:T(8,128)(2,1)S(1)}, f8e4m3fn[256,4096]{1,0:T(32,128)(4,1)S(1)}) custom-call(f32[1]{0:T(128)S(6)} %copy.8.wave_ref, f32[3,128]{1,0:T(4,128)S(1)} %copy-done.2), custom_call_target="tpu_custom_call" | custom-call | flops 20971520 | bytes 1048576 | tf_op jit(solution)/shard_map/eval_green/pallas_call | solution.py:443
  88.6 8.6 %all-to-all-done.6 = f32[8,40,128]{2,1,0:T(8,128)S(1)} async-done(((f32[8,40,128]{2,1,0:T(8,128)}), f32[8,40,128]{2,1,0:T(8,128)S(1)}, u32[]{:S(2)}, u32[]{:S(2)}) %all-to-all-start.6) | async-done | bytes 163872 | tf_op jit(solution)/shard_map/all_to_all | solution.py:400
  97.2 4.9 %collective-permute-start = (f32[320,128]{1,0:T(8,128)S(1)}, f32[320,128]{1,0:T(8,128)S(1)}, u32[]{:S(2)}, u32[]{:S(2)}) collective-permute-start(f32[320,128]{1,0:T(8,128)S(1)} %bitcast.2), channel_id=1, source_target_pairs={{0,32},{32,0},{1,33},{33,1},{2,34},{34,2},{3,35},{35,3},{4,36},{36... | collective-permute-start | bytes 491528 | tf_op jit(solution)/shard_map/ppermute | solution.py:449
  102.1 0.0 copy-done
  102.1 0.8 near_field.1
  102.9 0.2 collective-permute-done.got_ref
  103.1 1.4 %far_field.1 = (f32[2,8,256]{2,1,0:T(8,128)}, f32[2,8,256]{2,1,0:T(8,128)}, f32[2,8,128]{2,1,0:T(8,128)}) custom-call(f32[320,128]{1,0:T(8,128)S(1)} %collective-permute-done.got_ref, bf16[256,4096]{1,0:T(8,128)(2,1)S(1)} %get-tuple-element.31.high_ref, f8e4m3fn[256,4096]{1,0:T(32,128)(4,1)S(1)} %get-tuple-element.32.low_ref, s32[32,128]{1,0:T(8,128)S(1)} %bitcast.6, ...), custom_call_target="tpu_custom_call" | custom-call | flops 25165824 | bytes 1048576 | tf_op jit(solution)/shard_map/far_field/pallas_call | solution.py:456
  (3 shorter events, 0.0 us)
Async XLA Ops:
  2.0 27.0 %all-to-all-start = ((f32[8,8,128]{2,1,0:T(8,128)}), f32[8,8,128]{2,1,0:T(8,128)S(1)}, u32[]{:S(2)}, u32[]{:S(2)}) async-start(f32[8,8,128]{2,1,0:T(8,128)} %prepare.1), calls=%async_computation | async-start | bytes 65536 | tf_op jit(solution)/shard_map/all_to_all | solution.py:400
  54.8 30.8 %copy-start.2 = (f32[3,128]{1,0:T(4,128)S(1)}, f32[3,128]{1,0:T(4,128)}, u32[]{:S(2)}) copy-start(f32[3,128]{1,0:T(4,128)} %eval_ref) | copy-start | bytes 4612
  55.5 46.6 %copy-start = (s32[4096]{0:T(1024)S(1)}, s32[4096]{0:T(1024)}, u32[]{:S(2)}) copy-start(s32[4096]{0:T(1024)} %param.6) | copy-start | bytes 49156
  63.3 39.8 %copy-start.1 = (f32[2,8,256]{2,1,0:T(8,128)S(1)}, f32[2,8,256]{2,1,0:T(8,128)}, u32[]{:S(2)}) copy-start(f32[2,8,256]{2,1,0:T(8,128)} %desired_ref.1) | copy-start | bytes 49156
  82.2 15.1 %all-to-all-start.6 = ((f32[8,40,128]{2,1,0:T(8,128)}), f32[8,40,128]{2,1,0:T(8,128)S(1)}, u32[]{:S(2)}, u32[]{:S(2)}) async-start(f32[8,40,128]{2,1,0:T(8,128)} %drive.1), calls=%async_computation.6 | async-start | bytes 327680 | tf_op jit(solution)/shard_map/all_to_all | solution.py:400
  97.2 5.9 %collective-permute-start = (f32[320,128]{1,0:T(8,128)S(1)}, f32[320,128]{1,0:T(8,128)S(1)}, u32[]{:S(2)}, u32[]{:S(2)}) collective-permute-start(f32[320,128]{1,0:T(8,128)S(1)} %bitcast.2), channel_id=1, source_target_pairs={{0,32},{32,0},{1,33},{33,1},{2,34},{34,2},{3,35},{35,3},{4,36},{36... | collective-permute-start | bytes 491528 | tf_op jit(solution)/shard_map/ppermute | solution.py:449

commit v10 on v9

--- a/solution.py
+++ b/solution.py
@@ -13,7 +13,7 @@
 PTS = ("yhi", "zhi", "zlo", "zb", "zc")
 FLD = ("zb", "zlo", "zhi")
 BANKS = ("core", "xlo", "xhi")
-NEAR = ("zc", "yhi", "ylo")
+NEAR = ("ylo", "zc", "yhi")
 
 wall_pitch = 0.05
 front_gap = 0.5
@@ -317,7 +317,7 @@
         for i in range(8):
             send_ref[i, 8 * k : 8 * k + 8, :] = rows
     for half in range(2):
-        member = lax.axis_index(("zc", "yhi")) * 2 + half
+        member = half * 4 + lax.axis_index(("zc", "yhi"))
         change = alpha0 * got3_ref[member, 8:24, :] + alpha1 * got5_ref[member]
         for i in range(8):
             send_ref[i, 32 + half : 33 + half, :] = change[i : i + 1, :]

time: 105 us -> 105 us (level)
  no operation moved by 1% of the time
where the time goes in v10:
time: 105 us
  blocking collectives  47 us (45%)
  starting transfers between devices  23.9 us (23%)
  waiting for transfers between devices  19.6 us (19%)
  Pallas kernels  13 us (12%)
  between operations  1.37 us (1%)
    all_to_all x5, blocking collectives, exchange(): return lax.all_to_all(array, axes, split_axis=0, concat_axis=0, tiled=True)  47 us
    all_to_all x2, waiting for transfers between devices, exchange(): return lax.all_to_all(array, axes, split_axis=0, concat_axis=0, tiled=True)  19.4 us
    all_to_all x2, starting transfers between devices, exchange(): return lax.all_to_all(array, axes, split_axis=0, concat_axis=0, tiled=True)  19 us
    ppermute x1, starting transfers between devices, local(): other = lax.ppermute(got6, 'core', [(0, 1), (1, 0)])  4.86 us
    pallas_call x1, Pallas kernels, local(): call(eval_green_kernel, (shape(256, 4096, dtype=bf16), shape(256, 4096, d...  3.04 us
    pallas_call x1, Pallas kernels, local(): call(first_kernel, (shape(8, 2, 512, 128), shape(8, 8, 128)), [vmem((8, 6...  2.57 us
  transfers between devices with their start and end apart: 3, of which 3 were waited for; matrix products, arithmetic and copies ran while one was open for 0% of the time, Pallas kernels for 4%

profile of v10, /device:TPU:1, one launch (start us, length us, event | category | flops | bytes accessed | tf_op | source)
XLA Modules:
  0.0 104.8 jit_solution(11051087200622798164)
XLA Ops:
  0.6 1.4 %prepare.1 = f32[8,8,128]{2,1,0:T(8,128)} custom-call(f32[2,8,256]{2,1,0:T(8,128)} %desired_ref.1, f32[3,256]{1,0:T(4,128)} %points_hbm.1), custom_call_target="tpu_custom_call" | custom-call | flops 1024 | bytes 1048576 | tf_op jit(solution)/shard_map/prepare/pallas_call | solution.py:404
  2.0 15.6 %all-to-all-start = ((f32[8,8,128]{2,1,0:T(8,128)}), f32[8,8,128]{2,1,0:T(8,128)S(1)}, u32[]{:S(2)}, u32[]{:S(2)}) async-start(f32[8,8,128]{2,1,0:T(8,128)} %prepare.1), calls=%async_computation | async-start | bytes 65536 | tf_op jit(solution)/shard_map/all_to_all | solution.py:400
  18.3 10.7 %all-to-all-done.got_ref = f32[8,8,128]{2,1,0:T(8,128)S(1)} async-done(((f32[8,8,128]{2,1,0:T(8,128)}), f32[8,8,128]{2,1,0:T(8,128)S(1)}, u32[]{:S(2)}, u32[]{:S(2)}) %all-to-all-start) | async-done | bytes 32800 | tf_op jit(solution)/shard_map/all_to_all | solution.py:400
  29.0 2.6 %first.1 = (f32[8,2,512,128]{3,2,1,0:T(8,128)S(1)}, f32[8,8,128]{2,1,0:T(8,128)S(1)}) custom-call(f32[1]{0:T(128)S(6)} %copy.8.wave_ref, f32[8,8,128]{2,1,0:T(8,128)S(1)} %all-to-all-done.got_ref), custom_call_target="tpu_custom_call" | custom-call | flops 25165824 | bytes 1048576 | tf_op jit(solution)/shard_map/first/pallas_call | solution.py:411
  31.6 9.6 %all_to_all.35.got_ref = f32[8,8,128]{2,1,0:T(8,128)S(1)} all-to-all(f32[8,8,128]{2,1,0:T(8,128)S(1)} %get-tuple-element.20), channel_id=1, replica_groups=mesh['ylo'=2,'xhi'=2,'xlo'=2,'core'=2,'yhi'=2,'zhi'=2,'zlo'=2,'zb'=2,'zc..., dimensions={0} | all-to-all | bytes 65536 | tf_op jit(solution)/shard_map/all_to_all | solution.py:400
  41.2 1.0 image.1
  42.2 12.6 %all_to_all.36.got_ref.got2_ref = f32[8,24,128]{2,1,0:T(8,128)S(1)} all-to-all(f32[8,24,128]{2,1,0:T(8,128)S(1)} %get-tuple-element.21), channel_id=1, replica_groups=mesh['ylo'=2,'xhi'=2,'xlo'=2,'core'=2,'yhi'=2,'zhi'=2,'zlo'=2,'zb'=2,'zc..., dimensions={0} | all-to-all | bytes 196608 | tf_op jit(solution)/shard_map/all_to_all | solution.py:400
  54.8 0.8 adjoint.1
  55.6 0.0 copy-start
  55.6 7.9 %all_to_all.37.got3_ref = f32[8,24,128]{2,1,0:T(8,128)S(1)} all-to-all(f32[8,24,128]{2,1,0:T(8,128)S(1)} %adjoint.1), channel_id=1, replica_groups=mesh['ylo'=2,'xhi'=2,'xlo'=2,'core'=2,'yhi'=2,'zhi'=2,'zlo'=2,'zb'=2,'zc..., dimensions={0} | all-to-all | bytes 196608 | tf_op jit(solution)/shard_map/all_to_all | solution.py:400
  63.5 1.1 %second_image.1 = (f32[8,24,128]{2,1,0:T(8,128)S(1)}, f32[2,128]{1,0:T(2,128)S(1)}) custom-call(f32[8,2,512,128]{3,2,1,0:T(8,128)S(1)} %get-tuple-element.19.g_ref, f32[8,24,128]{2,1,0:T(8,128)S(1)} %all_to_all.37.got3_ref, f32[8,24,128]{2,1,0:T(8,128)S(1)} %all_to_all.36.got_ref.got2_ref, f32[8,128]{1,0:T(8,128)S(1)} %get-tuple-element.22.g0_ref), custom_call_target="tpu_custom_call" | custom-call | flops 4194304 | bytes 1048576 | tf_op jit(solution)/shard_map/second_image/pallas_call | solution.py:428
  64.6 9.1 %all_to_all.38.got4_ref = f32[8,24,128]{2,1,0:T(8,128)S(1)} all-to-all(f32[8,24,128]{2,1,0:T(8,128)S(1)} %get-tuple-element.23), channel_id=1, replica_groups=mesh['ylo'=2,'xhi'=2,'xlo'=2,'core'=2,'yhi'=2,'zhi'=2,'zlo'=2,'zb'=2,'zc..., dimensions={0} | all-to-all | bytes 196608 | tf_op jit(solution)/shard_map/all_to_all | solution.py:400
  73.7 0.1 norm.1
  73.8 7.7 %all_to_all.39.got5_ref = f32[8,16,128]{2,1,0:T(8,128)S(1)} all-to-all(f32[8,16,128]{2,1,0:T(8,128)S(1)} %get-tuple-element.25), channel_id=1, replica_groups=mesh['ylo'=2,'xhi'=2,'xlo'=2,'core'=2,'yhi'=2,'zhi'=2,'zlo'=2,'zb'=2,'zc..., dimensions={0} | all-to-all | bytes 131072 | tf_op jit(solution)/shard_map/all_to_all | solution.py:400
  81.5 0.8 drive.1
  82.4 3.4 %all-to-all-start.6 = ((f32[8,40,128]{2,1,0:T(8,128)}), f32[8,40,128]{2,1,0:T(8,128)S(1)}, u32[]{:S(2)}, u32[]{:S(2)}) async-start(f32[8,40,128]{2,1,0:T(8,128)} %drive.1), calls=%async_computation.6 | async-start | bytes 327680 | tf_op jit(solution)/shard_map/all_to_all | solution.py:400
  85.8 0.0 copy-done.2
  85.8 3.0 %eval_green.1 = (bf16[256,4096]{1,0:T(8,128)(2,1)S(1)}, f8e4m3fn[256,4096]{1,0:T(32,128)(4,1)S(1)}) custom-call(f32[1]{0:T(128)S(6)} %copy.8.wave_ref, f32[3,128]{1,0:T(4,128)S(1)} %copy-done.2), custom_call_target="tpu_custom_call" | custom-call | flops 20971520 | bytes 1048576 | tf_op jit(solution)/shard_map/eval_green/pallas_call | solution.py:443
  88.8 8.7 %all-to-all-done.6 = f32[8,40,128]{2,1,0:T(8,128)S(1)} async-done(((f32[8,40,128]{2,1,0:T(8,128)}), f32[8,40,128]{2,1,0:T(8,128)S(1)}, u32[]{:S(2)}, u32[]{:S(2)}) %all-to-all-start.6) | async-done | bytes 163872 | tf_op jit(solution)/shard_map/all_to_all | solution.py:400
  97.5 4.9 %collective-permute-start = (f32[320,128]{1,0:T(8,128)S(1)}, f32[320,128]{1,0:T(8,128)S(1)}, u32[]{:S(2)}, u32[]{:S(2)}) collective-permute-start(f32[320,128]{1,0:T(8,128)S(1)} %bitcast.2), channel_id=1, source_target_pairs={{0,32},{32,0},{1,33},{33,1},{2,34},{34,2},{3,35},{35,3},{4,36},{36... | collective-permute-start | bytes 491528 | tf_op jit(solution)/shard_map/ppermute | solution.py:449
  102.4 0.0 copy-done
  102.4 0.8 near_field.1
  103.2 0.2 collective-permute-done.got_ref
  103.4 1.4 %far_field.1 = (f32[2,8,256]{2,1,0:T(8,128)}, f32[2,8,256]{2,1,0:T(8,128)}, f32[2,8,128]{2,1,0:T(8,128)}) custom-call(f32[320,128]{1,0:T(8,128)S(1)} %collective-permute-done.got_ref, bf16[256,4096]{1,0:T(8,128)(2,1)S(1)} %get-tuple-element.31.high_ref, f8e4m3fn[256,4096]{1,0:T(32,128)(4,1)S(1)} %get-tuple-element.32.low_ref, s32[32,128]{1,0:T(8,128)S(1)} %bitcast.6, ...), custom_call_target="tpu_custom_call" | custom-call | flops 25165824 | bytes 1048576 | tf_op jit(solution)/shard_map/far_field/pallas_call | solution.py:456
  (3 shorter events, 0.0 us)
Async XLA Ops:
  2.0 27.0 %all-to-all-start = ((f32[8,8,128]{2,1,0:T(8,128)}), f32[8,8,128]{2,1,0:T(8,128)S(1)}, u32[]{:S(2)}, u32[]{:S(2)}) async-start(f32[8,8,128]{2,1,0:T(8,128)} %prepare.1), calls=%async_computation | async-start | bytes 65536 | tf_op jit(solution)/shard_map/all_to_all | solution.py:400
  54.8 31.0 %copy-start.2 = (f32[3,128]{1,0:T(4,128)S(1)}, f32[3,128]{1,0:T(4,128)}, u32[]{:S(2)}) copy-start(f32[3,128]{1,0:T(4,128)} %eval_ref) | copy-start | bytes 4612
  55.6 46.8 %copy-start = (s32[4096]{0:T(1024)S(1)}, s32[4096]{0:T(1024)}, u32[]{:S(2)}) copy-start(s32[4096]{0:T(1024)} %param.6) | copy-start | bytes 49156
  63.5 39.9 %copy-start.1 = (f32[2,8,256]{2,1,0:T(8,128)S(1)}, f32[2,8,256]{2,1,0:T(8,128)}, u32[]{:S(2)}) copy-start(f32[2,8,256]{2,1,0:T(8,128)} %desired_ref.1) | copy-start | bytes 49156
  82.4 15.2 %all-to-all-start.6 = ((f32[8,40,128]{2,1,0:T(8,128)}), f32[8,40,128]{2,1,0:T(8,128)S(1)}, u32[]{:S(2)}, u32[]{:S(2)}) async-start(f32[8,40,128]{2,1,0:T(8,128)} %drive.1), calls=%async_computation.6 | async-start | bytes 327680 | tf_op jit(solution)/shard_map/all_to_all | solution.py:400
  97.5 5.9 %collective-permute-start = (f32[320,128]{1,0:T(8,128)S(1)}, f32[320,128]{1,0:T(8,128)S(1)}, u32[]{:S(2)}, u32[]{:S(2)}) collective-permute-start(f32[320,128]{1,0:T(8,128)S(1)} %bitcast.2), channel_id=1, source_target_pairs={{0,32},{32,0},{1,33},{33,1},{2,34},{34,2},{3,35},{35,3},{4,36},{36... | collective-permute-start | bytes 491528 | tf_op jit(solution)/shard_map/ppermute | solution.py:449
